TPU v7x, 32 devices: a whole 2x2x4 slice. The times are simulated.
32 devices in a mesh: groups: 2 (over y), seq: 4 (over z), section: 2 (over x), mp: 2 (over core).
Axes of the slice: x: 2, y: 2, z: 4, core: 2. Of those that a mesh axis runs over, the one named last changes fastest.
Arguments:
- section_inputs: bfloat16 [2, 1024, 768], P('section', ('groups', 'seq')), parts along dimension 1, may hold values from -6 to 6
- cotangent: bfloat16 [1024, 768], P(('groups', 'seq')), parts along dimension 0, may hold values from -6 to 6
- w_in: bfloat16 [2, 768, 1536], P('section', None, 'mp'), may hold values from -0.21875 to 0.21875
- w_bc: bfloat16 [2, 768, 32], P('section'), may hold values from -0.21875 to 0.21875
- w_out: bfloat16 [2, 1536, 768], P('section', 'mp'), may hold values from -0.15625 to 0.15625
- decay_rates: float32 [2, 24], P('section', 'mp'), may hold values from 0.0001953125 to 0.05
- resets: int32 [1024], P(('groups', 'seq')), parts along dimension 0, may hold values 0 or 1
Outputs:
- grad_inputs: bfloat16 [2, 1024, 768], P('section', ('groups', 'seq')), parts along dimension 1
- grad_w_bc: float32 [2, 1536, 32], P('section', 'groups'), parts along dimension 1
- grad_rates: float32 [2, 48], P('section', ('groups', 'mp')), parts along dimension 1
There are 2 independent parts, one for each index of `groups`. A program takes and returns all parts, laid end to end along the dimension named above; an argument that names none is the same for every part. Nothing has to cross between parts.
All inputs are finite; a program needn't handle non-finite values. No bound on the sum of `resets` on one device may be relied on, other than what follows from the above.
Results may differ from a plain program's by a relative error of at most 0.018.
Values may be sent and summed in bfloat16 or wider, within the bound.
No kernel may reach another device: no remote copies, remote signals or barrier semaphores. Data moves between devices by JAX's collectives and lax.ppermute only.
A program may use at most 64 MiB of HBM per device.

v0:
```python
import jax
import jax.numpy as jnp
from jax import lax
from jax.sharding import PartitionSpec as P

highest = lax.Precision.HIGHEST
retain_inside_segment = 0.6


def shifted(shard, axis, by):
    devices = lax.axis_size(axis)
    pairs = [(i, i + by) for i in range(devices) if 0 <= i + by < devices]
    return lax.ppermute(shard, axis, pairs)


def forward_over_span(inner_f, coef_f, speed_real_number, restart_real_mask, state_in):
    tokens_here = inner_f.shape[0]
    channels = inner_f.shape[1]
    head_count = speed_real_number.shape[0]
    head_width = channels // head_count
    states = coef_f.shape[1] // 2
    logarithmic_fade_increment = (
        restart_real_mask[:, None] * jnp.log(retain_inside_segment) - speed_real_number[None, :]
    )
    cumulative_log_decay = jnp.cumsum(logarithmic_fade_increment, axis=0)
    in_scale = jnp.sqrt(-jnp.expm1(-2.0 * speed_real_number))
    b_part = coef_f[:, :states]
    c_part = coef_f[:, states:]
    scores = jnp.dot(c_part, b_part.T, precision=highest)
    sequence_place = jnp.arange(tokens_here)
    causal = sequence_place[:, None] >= sequence_place[None, :]
    cum_heads = cumulative_log_decay.T
    log_gaps = jnp.where(causal[None], cum_heads[:, :, None] - cum_heads[:, None, :], -10000.0)
    weights = jnp.exp(log_gaps) * scores[None]
    scaled = inner_f.reshape(tokens_here, head_count, head_width) * in_scale[None, :, None]
    intra = jnp.einsum("hts,shp->thp", weights, scaled, precision=highest).reshape(
        tokens_here, channels
    )
    growth = jnp.repeat(jnp.exp(cumulative_log_decay), head_width, axis=1)
    mixed_out = intra + growth * jnp.dot(c_part, state_in, precision=highest)
    tail_weight = jnp.repeat(
        jnp.exp(cumulative_log_decay[-1][None, :] - cumulative_log_decay), head_width, axis=1
    )
    state_out = growth[-1][None, :] * state_in + jnp.dot(
        b_part.T, tail_weight * scaled.reshape(tokens_here, channels), precision=highest
    )
    return (mixed_out, state_out)


def blocked_forward(inner_f, coef_f, speed_real_number, restart_real_mask, state_in):
    tokens_here = inner_f.shape[0]
    block_len = 128
    block_count = tokens_here // block_len

    def advance_block(state_now, pieces):
        mixed_out, state_next = forward_over_span(
            pieces[0], pieces[1], speed_real_number, pieces[2], state_now
        )
        return (state_next, mixed_out)

    pieces = (
        inner_f.reshape(block_count, block_len, inner_f.shape[1]),
        coef_f.reshape(block_count, block_len, coef_f.shape[1]),
        restart_real_mask.reshape(block_count, block_len),
    )
    state_out, mixed_all = lax.scan(advance_block, state_in, pieces)
    return (mixed_all.reshape(tokens_here, inner_f.shape[1]), state_out)


def combine_gathered(all_logs, all_states, seq_index, head_width, from_later):
    device_order = jnp.arange(all_logs.shape[0])
    inclusive = jnp.cumsum(all_logs, axis=0)
    if from_later:
        chosen = device_order > seq_index
        own_total = jnp.sum(jnp.where((device_order <= seq_index)[:, None], all_logs, 0.0), axis=0)
        log_gaps = inclusive - all_logs - own_total[None, :]
    else:
        chosen = device_order < seq_index
        total_before = jnp.sum(jnp.where(chosen[:, None], all_logs, 0.0), axis=0)
        log_gaps = total_before[None, :] - inclusive
    log_gaps = jnp.where(chosen[:, None], log_gaps, -10000.0)
    weights = jnp.repeat(jnp.exp(log_gaps), head_width, axis=1)
    return jnp.sum(weights[:, None, :] * all_states, axis=0)


def shards(section_inputs, cotangent, w_in, w_bc, w_out, decay_rates, resets):
    layer_activation_values = section_inputs[0]
    inner_act = jnp.dot(
        layer_activation_values, w_in[0], preferred_element_type=jnp.float32
    ).astype(jnp.bfloat16)
    coef_bc = jnp.dot(layer_activation_values, w_bc[0], preferred_element_type=jnp.float32)
    shard_speed_entries = decay_rates[0]
    restart_real_mask = resets.astype(jnp.float32)
    head_count = shard_speed_entries.shape[0]
    channels = inner_act.shape[1]
    head_width = channels // head_count
    states = coef_bc.shape[1] // 2
    inner_f = inner_act.astype(jnp.float32)
    cumulative_log_decay = jnp.cumsum(
        restart_real_mask[:, None] * jnp.log(retain_inside_segment) - shard_speed_entries[None, :],
        axis=0,
    )
    span_log = cumulative_log_decay[-1]
    in_scale = jnp.sqrt(-jnp.expm1(-2.0 * shard_speed_entries))
    scaled = inner_f * jnp.repeat(in_scale, head_width)[None, :]
    tail_weight = jnp.repeat(jnp.exp(span_log[None, :] - cumulative_log_decay), head_width, axis=1)
    shard_hidden_vector = jnp.dot(coef_bc[:, :states].T, tail_weight * scaled, precision=highest)
    seq_index = lax.axis_index("seq")
    all_logs, all_states = (
        lax.all_gather(span_log[None], "seq", axis=0, tiled=True),
        lax.all_gather(shard_hidden_vector[None], "seq", axis=0, tiled=True),
    )
    state_in = combine_gathered(all_logs, all_states, seq_index, head_width, False)
    _, pullback = jax.vjp(
        lambda inner_v, coef_v, rate_v, state_v: blocked_forward(
            inner_v, coef_v, rate_v, restart_real_mask, state_v
        ),
        inner_f,
        coef_bc,
        shard_speed_entries,
        state_in,
    )
    growth = jnp.repeat(jnp.exp(cumulative_log_decay), head_width, axis=1)
    c_part = coef_bc[:, states:]
    section_index = lax.axis_index("section")
    section_count = lax.axis_size("section")

    def advance(moment, carried):
        received, kept_grad, kept_coef, kept_rate = carried
        current = jnp.where(section_index == section_count - 1, cotangent, received)
        active = moment == section_count - 1 - section_index
        grad_mixed = lax.dot_general(
            current, w_out[0], (((1,), (1,)), ((), ())), preferred_element_type=jnp.float32
        )
        local_adjoint = jnp.dot(c_part.T, growth * grad_mixed, precision=highest)
        all_adjoint = lax.all_gather(local_adjoint[None], "seq", axis=0, tiled=True)
        adjoint = combine_gathered(all_logs, all_adjoint, seq_index, head_width, True)
        grad_inner, coefficient_adjoint_term, grad_rate, _ = pullback((grad_mixed, adjoint))
        partial_back = lax.dot_general(
            grad_inner.astype(jnp.bfloat16),
            w_in[0],
            (((1,), (1,)), ((), ())),
            preferred_element_type=jnp.float32,
        )
        summed_back, summed_coef = lax.psum((partial_back, coefficient_adjoint_term), "mp")
        coef_term = lax.dot_general(
            summed_coef.astype(jnp.bfloat16),
            w_bc[0],
            (((1,), (1,)), ((), ())),
            preferred_element_type=jnp.float32,
        )
        result = (current.astype(jnp.float32) + summed_back + coef_term).astype(jnp.bfloat16)
        kept_grad = jnp.where(active, result, kept_grad)
        kept_coef = jnp.where(active, summed_coef, kept_coef)
        kept_rate = jnp.where(active, grad_rate, kept_rate)
        passed = shifted(result, "section", -1)
        return (passed, kept_grad, kept_coef, kept_rate)

    start = (
        jnp.zeros_like(cotangent),
        jnp.zeros_like(cotangent),
        jnp.zeros_like(coef_bc),
        jnp.zeros_like(shard_speed_entries),
    )
    _, kept_grad, kept_coef, kept_rate = lax.fori_loop(0, section_count, advance, start)
    coef_grad = jnp.dot(layer_activation_values.astype(jnp.float32).T, kept_coef, precision=highest)
    rate_total, coef_total = lax.psum((kept_rate, coef_grad), "seq")
    return (kept_grad[None], coef_total[None], rate_total[None])


def solution(mesh):
    return jax.shard_map(
        shards,
        mesh=mesh,
        in_specs=(
            P("section", ("groups", "seq"), None),
            P(("groups", "seq"), None),
            P("section", None, "mp"),
            P("section", None, None),
            P("section", "mp", None),
            P("section", "mp"),
            P(("groups", "seq")),
        ),
        out_specs=(
            P("section", ("groups", "seq"), None),
            P("section", "groups", None),
            P("section", ("groups", "mp")),
        ),
        check_vma=False,
    )
```

profile of v0, /device:TPU:0, one launch (start us, length us, event | category | flops | bytes accessed | tf_op | source)
XLA Modules:
  0.0 200.9 jit_solution(225096522491550213)
XLA Ops:
  15.6 1.6 fusion.51
  18.8 12.5 %all-gather.2 = f32[4,1,12]{2,1,0:T(1,128)S(1)} all-gather(f32[1,1,12]{2,1,0:T(1,128)S(1)} %get-tuple-element.1549), channel_id=1, replica_groups=mesh['groups'=2,'seq'=4,'section'=2,'mp'=2] {'seq'}, dimensions={0}, use_global_device_ids=true | all-gather | bytes 240 | tf_op jit(solution)/shard_map/all_gather | solution.py:110
  35.2 13.6 %all-gather.1 = f32[64,768]{1,0:T(8,128)S(1)} all-gather(f32[16,768]{1,0:T(8,128)S(1)} %fusion.59), channel_id=3, replica_groups=mesh['groups'=2,'seq'=4,'section'=2,'mp'=2] {'seq'}, dimensions={0}, use_global_device_ids=true | all-gather | bytes 245760 | tf_op jit(solution)/shard_map/all_gather | solution.py:111
  50.1 104.0 %while.26 = (s32[]{:T(128)}, bf16[128,768]{1,0:T(8,128)(2,1)S(1)}, bf16[128,768]{1,0:T(8,128)(2,1)}, f32[128,32]{0,1:T(8,128)}, f32[12]{0:T(128)}, /*index=5*/pr...) while((s32[]{:T(128)}, bf16[128,768]{1,0:T(8,128)(2,1)S(1)}, ...), condition=%wide.region_19.20_spmd.clone.clone.clone, body=%wide.region_4.19_spmd.clone.clone.clone.sunk | while | flops 696906240 | bytes 35304876 | solution.py:165
  52.2 1.8 fusion.116
  55.3 13.6 %all-gather.7 = f32[64,768]{1,0:T(8,128)S(1)} all-gather(f32[16,768]{1,0:T(8,128)S(1)} %convolution_bitcast_fusion.8), channel_id=2, replica_groups=mesh['groups'=2,'seq'=4,'section'=2,'mp'=2] {'seq'}, dimensions={0}, use_global_device_ids=true | all-gather | bytes 245760 | tf_op jit(solution)/shard_map/while/body/eval_jaxpr/all_gather | solution.py:136
  69.8 2.7 %fusion.119 = (f32[12]{0:T(128)}, bf16[128,12,64]{0,2,1:T(8,128)(2,1)S(1)}) fusion(f32[1,128,12,64]{1,3,2,0:T(8,128)} %copy-done.14, f32[12]{0:T(128)S(1)} %bitcast.279, f32[128,12,64]{0,2,1:T(8,128)S(1)} %bitcast.259, f32[12,64,128]{2,1,0:T(8,128)S(1)} %bitcast.260, f32[128,128]{1,0:T(8,128)S(1)} %copy-done.27, f32[12,128]{1,0:T(8,128)S(1)} %copy-done.34, ...), kind=kOutput, calls=%fused_computation.33.clone.1 | convolution fusion | flops 152076272 | bytes 1464416 | tf_op jit(solution)/shard_map/while/body/eval_jaxpr/transpose(jvp())/while/body/eval_jaxpr/hts,shp->thp/dot_general | solution.py:36
  76.2 1.9 fusion.118
  78.4 2.9 %fusion.117 = (f32[12,128]{1,0:T(8,128)S(1)}, f32[12,128]{1,0:T(8,128)S(1)}, f32[128,128]{1,0:T(8,128)S(1)}) fusion(f32[12,128]{1,0:T(8,128)} %get-tuple-element.1888, f32[128,128]{1,0:T(8,128)} %get-tuple-element.1890, pred[128,128]{1,0:T(8,128)(4,1)} %get-tuple-element.1889, f32[12,64,128]{2,1,0:T(8,128)S(1)} %bitcast.261, ...), kind=kOutput, calls=%fused_computation.27.clone.1 | convolution fusion | flops 152744960 | bytes 952320 | tf_op jit(solution)/shard_map/while/body/eval_jaxpr/transpose(jvp())/while/body/eval_jaxpr/hts,shp->thp/dot_general | solution.py:36
  83.2 3.4 %psum.50 = f32[128,32]{0,1:T(8,128)S(1)} all-reduce(f32[128,32]{0,1:T(8,128)S(1)} %pad_add_fusion.2), channel_id=1, replica_groups=mesh['groups'=2,'seq'=4,'section'=2,'mp'=2] {'mp'}, use_global_device_ids=true, to_apply=%region_9.9 | all-reduce | flops 4096 | bytes 32768 | tf_op jit(solution)/shard_map/while/body/eval_jaxpr/psum | solution.py:145
  86.6 4.0 %all-reduce.9.cloned.1.call-done = f32[128,768]{1,0:T(8,128)} async-done(((f32[128,768]{1,0:T(8,128)}), f32[128,768]{1,0:T(8,128)}) %all-reduce.9.cloned.1.call-update) | async-done | bytes 393232 | tf_op jit(solution)/shard_map/while/body/eval_jaxpr/psum | solution.py:145
  93.3 7.6 %collective-permute-done = bf16[128,768]{1,0:T(8,128)(2,1)S(1)} collective-permute-done((bf16[128,768]{1,0:T(8,128)(2,1)S(1)}, bf16[128,768]{1,0:T(8,128)(2,1)S(1)}, u32[]{:S(2)}, u32[]{:S(2)}) %collective-permute-start) | collective-permute-done | bytes 196640 | tf_op jit(solution)/shard_map/while/body/eval_jaxpr/ppermute | solution.py:13
  102.9 1.8 fusion.116
  106.1 14.0 %all-gather.7 = f32[64,768]{1,0:T(8,128)S(1)} all-gather(f32[16,768]{1,0:T(8,128)S(1)} %convolution_bitcast_fusion.8), channel_id=2, replica_groups=mesh['groups'=2,'seq'=4,'section'=2,'mp'=2] {'seq'}, dimensions={0}, use_global_device_ids=true | all-gather | bytes 245760 | tf_op jit(solution)/shard_map/while/body/eval_jaxpr/all_gather | solution.py:136
  121.0 2.7 %fusion.119 = (f32[12]{0:T(128)}, bf16[128,12,64]{0,2,1:T(8,128)(2,1)S(1)}) fusion(f32[1,128,12,64]{1,3,2,0:T(8,128)} %copy-done.14, f32[12]{0:T(128)S(1)} %bitcast.279, f32[128,12,64]{0,2,1:T(8,128)S(1)} %bitcast.259, f32[12,64,128]{2,1,0:T(8,128)S(1)} %bitcast.260, f32[128,128]{1,0:T(8,128)S(1)} %copy-done.27, f32[12,128]{1,0:T(8,128)S(1)} %copy-done.34, ...), kind=kOutput, calls=%fused_computation.33.clone.1 | convolution fusion | flops 152076272 | bytes 1464416 | tf_op jit(solution)/shard_map/while/body/eval_jaxpr/transpose(jvp())/while/body/eval_jaxpr/hts,shp->thp/dot_general | solution.py:36
  127.4 1.9 fusion.118
  129.7 2.9 %fusion.117 = (f32[12,128]{1,0:T(8,128)S(1)}, f32[12,128]{1,0:T(8,128)S(1)}, f32[128,128]{1,0:T(8,128)S(1)}) fusion(f32[12,128]{1,0:T(8,128)} %get-tuple-element.1888, f32[128,128]{1,0:T(8,128)} %get-tuple-element.1890, pred[128,128]{1,0:T(8,128)(4,1)} %get-tuple-element.1889, f32[12,64,128]{2,1,0:T(8,128)S(1)} %bitcast.261, ...), kind=kOutput, calls=%fused_computation.27.clone.1 | convolution fusion | flops 152744960 | bytes 952320 | tf_op jit(solution)/shard_map/while/body/eval_jaxpr/transpose(jvp())/while/body/eval_jaxpr/hts,shp->thp/dot_general | solution.py:36
  134.4 3.4 %psum.50 = f32[128,32]{0,1:T(8,128)S(1)} all-reduce(f32[128,32]{0,1:T(8,128)S(1)} %pad_add_fusion.2), channel_id=1, replica_groups=mesh['groups'=2,'seq'=4,'section'=2,'mp'=2] {'mp'}, use_global_device_ids=true, to_apply=%region_9.9 | all-reduce | flops 4096 | bytes 32768 | tf_op jit(solution)/shard_map/while/body/eval_jaxpr/psum | solution.py:145
  137.8 6.0 %all-reduce.9.cloned.1.call-done = f32[128,768]{1,0:T(8,128)} async-done(((f32[128,768]{1,0:T(8,128)}), f32[128,768]{1,0:T(8,128)}) %all-reduce.9.cloned.1.call-update) | async-done | bytes 393232 | tf_op jit(solution)/shard_map/while/body/eval_jaxpr/psum | solution.py:145
  146.5 7.5 %collective-permute-done = bf16[128,768]{1,0:T(8,128)(2,1)S(1)} collective-permute-done((bf16[128,768]{1,0:T(8,128)(2,1)S(1)}, bf16[128,768]{1,0:T(8,128)(2,1)S(1)}, u32[]{:S(2)}, u32[]{:S(2)}) %collective-permute-start) | collective-permute-done | bytes 196640 | tf_op jit(solution)/shard_map/while/body/eval_jaxpr/ppermute | solution.py:13
  154.2 1.6 convolution_bitcast_fusion.5
  155.8 12.5 %psum.41 = f32[1,12]{1,0:T(1,128)} all-reduce(f32[1,12]{1,0:T(1,128)} %bitcast.277), channel_id=1, replica_groups=mesh['groups'=2,'seq'=4,'section'=2,'mp'=2] {'seq'}, use_global_device_ids=true, to_apply=%region_21.22 | all-reduce | flops 12 | bytes 96 | tf_op jit(solution)/shard_map/psum | solution.py:167
  168.3 23.6 %all-reduce.7.cloned.1.call-done = f32[1,768,32]{1,2,0:T(8,128)} async-done(((f32[1,768,32]{1,2,0:T(8,128)}), f32[1,768,32]{1,2,0:T(8,128)}) %all-reduce.7.cloned.1.call-update) | async-done | bytes 98320 | tf_op jit(solution)/shard_map/psum | solution.py:167
  191.9 1.5 copy.71
  (246 shorter events, 39.1 us)
Async XLA Ops:
  34.2 15.9 %copy-start.1 = (bf16[1,768,768]{2,1,0:T(8,128)(2,1)S(1)}, bf16[1,768,768]{2,1,0:T(8,128)(2,1)}, u32[]{:S(2)}) copy-start(bf16[1,768,768]{2,1,0:T(8,128)(2,1)} %param.11) | copy-start | bytes 3538948
  34.2 15.9 %copy-start.2 = (bf16[128,768]{1,0:T(8,128)(2,1)S(1)}, bf16[128,768]{1,0:T(8,128)(2,1)}, u32[]{:S(2)}) copy-start(bf16[128,768]{1,0:T(8,128)(2,1)} %param.10) | copy-start | bytes 589828
  50.2 18.7 %copy-start.4 = (f32[1,128,768]{1,2,0:T(8,128)}, f32[1,128,768]{1,2,0:T(8,128)S(1)}, u32[]{:S(2)}) copy-start(f32[1,128,768]{1,2,0:T(8,128)S(1)} %get-tuple-element.1881) | copy-start | bytes 1179652 | tf_op jit(solution)/shard_map/while
  50.2 23.5 %copy-start.9 = (f32[1,16,768]{2,1,0:T(8,128)}, f32[1,16,768]{2,1,0:T(8,128)S(1)}, u32[]{:S(2)}) copy-start(f32[1,16,768]{2,1,0:T(8,128)S(1)} %get-tuple-element.1872) | copy-start | bytes 147460 | tf_op jit(solution)/shard_map/while
  50.2 40.5 %all-reduce.9.cloned.1.call-start = ((), (), s32[]{:S(2)}) async-start(), calls=%async_computation.1 | async-start | bytes 786432 | tf_op jit(solution)/shard_map/while/body/eval_jaxpr/psum | solution.py:145
  81.4 19.5 %copy-start.5 = (f32[1,128,768]{1,2,0:T(8,128)S(1)}, f32[1,128,768]{1,2,0:T(8,128)}, u32[]{:S(2)}) copy-start(f32[1,128,768]{1,2,0:T(8,128)} %copy-done.4) | copy-start | bytes 1179652 | tf_op jit(solution)/shard_map/while
  81.4 19.5 %copy-start.10 = (f32[1,16,768]{2,1,0:T(8,128)S(1)}, f32[1,16,768]{2,1,0:T(8,128)}, u32[]{:S(2)}) copy-start(f32[1,16,768]{2,1,0:T(8,128)} %copy-done.9) | copy-start | bytes 147460 | tf_op jit(solution)/shard_map/while
  81.4 19.5 %copy-start.15 = (f32[1,128,12,64]{1,3,2,0:T(8,128)S(1)}, f32[1,128,12,64]{1,3,2,0:T(8,128)}, u32[]{:S(2)}) copy-start(f32[1,128,12,64]{1,3,2,0:T(8,128)} %copy-done.14) | copy-start | bytes 1179652 | tf_op jit(solution)/shard_map/while
  81.5 19.5 %copy-start.26 = (f32[4,12]{1,0:T(4,128)S(1)}, f32[4,12]{1,0:T(4,128)}, u32[]{:S(2)}) copy-start(f32[4,12]{1,0:T(4,128)} %copy-done.25) | copy-start | bytes 580 | tf_op jit(solution)/shard_map/while
  91.9 8.9 %collective-permute-start = (bf16[128,768]{1,0:T(8,128)(2,1)S(1)}, bf16[128,768]{1,0:T(8,128)(2,1)S(1)}, u32[]{:S(2)}, u32[]{:S(2)}) collective-permute-start(bf16[128,768]{1,0:T(8,128)(2,1)S(1)} %get-tuple-element.1777), channel_id=1, source_target_pairs={{2,0},{3,1},{6,4},{7,5},{10,8},{11,9},{14,12},{15,13},{18,16},{19,... | collective-permute-start | bytes 589832 | tf_op jit(solution)/shard_map/while/body/eval_jaxpr/ppermute | solution.py:13
  100.9 19.2 %copy-start.4 = (f32[1,128,768]{1,2,0:T(8,128)}, f32[1,128,768]{1,2,0:T(8,128)S(1)}, u32[]{:S(2)}) copy-start(f32[1,128,768]{1,2,0:T(8,128)S(1)} %get-tuple-element.1881) | copy-start | bytes 1179652 | tf_op jit(solution)/shard_map/while
  101.0 24.0 %copy-start.9 = (f32[1,16,768]{2,1,0:T(8,128)}, f32[1,16,768]{2,1,0:T(8,128)S(1)}, u32[]{:S(2)}) copy-start(f32[1,16,768]{2,1,0:T(8,128)S(1)} %get-tuple-element.1872) | copy-start | bytes 147460 | tf_op jit(solution)/shard_map/while
  101.0 42.9 %all-reduce.9.cloned.1.call-start = ((), (), s32[]{:S(2)}) async-start(), calls=%async_computation.1 | async-start | bytes 786432 | tf_op jit(solution)/shard_map/while/body/eval_jaxpr/psum | solution.py:145
  104.8 15.3 %copy-start.21 = (f32[128,12]{0,1:T(8,128)S(1)}, f32[128,12]{0,1:T(8,128)}, u32[]{:S(2)}) copy-start(f32[128,12]{0,1:T(8,128)} %get-tuple-element.1886) | copy-start | bytes 18436 | tf_op jit(solution)/shard_map/while
  105.7 15.2 %copy-start.30 = (pred[128,128]{1,0:T(8,128)(4,1)S(1)}, pred[128,128]{1,0:T(8,128)(4,1)}, u32[]{:S(2)}) copy-start(pred[128,128]{1,0:T(8,128)(4,1)} %get-tuple-element.1889) | copy-start | bytes 49156 | tf_op jit(solution)/shard_map/while
  105.7 15.2 %copy-start.34 = (f32[12,128]{1,0:T(8,128)S(1)}, f32[12,128]{1,0:T(8,128)}, u32[]{:S(2)}) copy-start(f32[12,128]{1,0:T(8,128)} %get-tuple-element.1888) | copy-start | bytes 18436 | tf_op jit(solution)/shard_map/while
  105.7 15.2 %copy-start.35 = (f32[1,12,1]{1,2,0:T(1,128)S(1)}, f32[1,12,1]{1,2,0:T(1,128)}, u32[]{:S(2)}) copy-start(f32[1,12,1]{1,2,0:T(1,128)} %get-tuple-element.1870) | copy-start | bytes 148 | tf_op jit(solution)/shard_map/while
  132.6 21.4 %copy-start.5 = (f32[1,128,768]{1,2,0:T(8,128)S(1)}, f32[1,128,768]{1,2,0:T(8,128)}, u32[]{:S(2)}) copy-start(f32[1,128,768]{1,2,0:T(8,128)} %copy-done.4) | copy-start | bytes 1179652 | tf_op jit(solution)/shard_map/while
  132.6 21.4 %copy-start.10 = (f32[1,16,768]{2,1,0:T(8,128)S(1)}, f32[1,16,768]{2,1,0:T(8,128)}, u32[]{:S(2)}) copy-start(f32[1,16,768]{2,1,0:T(8,128)} %copy-done.9) | copy-start | bytes 147460 | tf_op jit(solution)/shard_map/while
  132.6 21.4 %copy-start.15 = (f32[1,128,12,64]{1,3,2,0:T(8,128)S(1)}, f32[1,128,12,64]{1,3,2,0:T(8,128)}, u32[]{:S(2)}) copy-start(f32[1,128,12,64]{1,3,2,0:T(8,128)} %copy-done.14) | copy-start | bytes 1179652 | tf_op jit(solution)/shard_map/while
  132.7 21.4 %copy-start.26 = (f32[4,12]{1,0:T(4,128)S(1)}, f32[4,12]{1,0:T(4,128)}, u32[]{:S(2)}) copy-start(f32[4,12]{1,0:T(4,128)} %copy-done.25) | copy-start | bytes 580 | tf_op jit(solution)/shard_map/while
  137.8 16.2 %copy-start.19 = (f32[128,32]{0,1:T(8,128)}, f32[128,32]{0,1:T(8,128)S(1)}, u32[]{:S(2)}) copy-start(f32[128,32]{0,1:T(8,128)S(1)} %select_select_fusion.5) | copy-start | bytes 49156 | tf_op jit(solution)/shard_map/while
  145.1 8.9 %collective-permute-start = (bf16[128,768]{1,0:T(8,128)(2,1)S(1)}, bf16[128,768]{1,0:T(8,128)(2,1)S(1)}, u32[]{:S(2)}, u32[]{:S(2)}) collective-permute-start(bf16[128,768]{1,0:T(8,128)(2,1)S(1)} %get-tuple-element.1777), channel_id=1, source_target_pairs={{2,0},{3,1},{6,4},{7,5},{10,8},{11,9},{14,12},{15,13},{18,16},{19,... | collective-permute-start | bytes 589832 | tf_op jit(solution)/shard_map/while/body/eval_jaxpr/ppermute | solution.py:13
  154.1 37.8 %all-reduce.7.cloned.1.call-start = ((), (), s32[]{:S(2)}) async-start(), calls=%async_computation | async-start | bytes 196608 | tf_op jit(solution)/shard_map/psum | solution.py:167
  (49 other events, 415.1 us)
Sparse Core Ops, SparseCore 0:
  73.9 16.7 all-reduce.8
  125.1 18.7 all-reduce.8
Sparse Core Ops, SparseCore 1:
  157.5 34.4 all-reduce.6
where the time goes:
time: 202 us; the launch traced here: 201 us
  blocking collectives  73 us (36%)
  waiting for transfers between devices  48.9 us (24%)
  matrix products  35.2 us (17%)
  between operations  15.6 us (8%)
  other arithmetic  13.9 us (7%)
  local copies, waits for them, and re-layouts  10.5 us (5%)
  starting transfers between devices  2.71 us (1%)
    all_gather x2, blocking collectives, advance(): all_adjoint = lax.all_gather(local_adjoint[None], 'seq', axis=0, tiled=True)  27.6 us
    psum x1, waiting for transfers between devices, shards(): rate_total, coef_total = lax.psum((kept_rate, coef_grad), 'seq')  23.6 us
    ppermute x2, waiting for transfers between devices, shifted(): return lax.ppermute(shard, axis, pairs)  15.1 us
    all_gather x1, blocking collectives, shards(): lax.all_gather(shard_hidden_vector[None], 'seq', axis=0, tiled=True)  13.6 us
    psum x1, blocking collectives, shards(): rate_total, coef_total = lax.psum((kept_rate, coef_grad), 'seq')  12.5 us
    all_gather x1, blocking collectives, shards(): lax.all_gather(span_log[None], 'seq', axis=0, tiled=True)  12.5 us
    dot_general x4, matrix products, forward_over_span(): jnp.einsum('hts,shp->thp', weights, scaled, precision=highest)  11.2 us
    psum x2, waiting for transfers between devices, advance(): lax.psum((partial_back, coefficient_adjoint_term), 'mp')  10.1 us
  transfers between devices with their start and end apart: 5, of which 5 were waited for; matrix products, arithmetic and copies ran while one was open for 9% of the time, Pallas kernels for 0%

commit v1 on v0

v1 whole, which is shorter than its diff:
```python
import functools
import math

import jax
import jax.numpy as jnp
from jax import lax
from jax.experimental import pallas as pl
from jax.experimental.pallas import tpu as pltpu
from jax.sharding import PartitionSpec as P

LOG_KEEP = math.log(0.6)
F32 = jnp.float32
BF16 = jnp.bfloat16

NN = (((1,), (0,)), ((), ()))
NT = (((1,), (1,)), ((), ()))
TN = (((0,), (0,)), ((), ()))

RATE, EMID, ATOT, INV, COUNT = 0, 1, 2, 3, 4
TABLE_ROWS = 8


def mm(a, b, dims):
    return lax.dot_general(a, b, dims, preferred_element_type=F32)


def rotate(value, axis, by):
    n = lax.axis_size(axis)
    return lax.ppermute(value, axis, [(i, (i + by) % n) for i in range(n)])


def swap(value, axis):
    return rotate(value, axis, 1)


def expm1_small(y):
    return y * (1 + y / 2 * (1 + y / 3 * (1 + y / 4 * (1 + y / 5 * (1 + y / 6)))))


def column(tokens):
    return lax.broadcasted_iota(F32, (tokens, 1), 0) if False else lax.broadcasted_iota(
        jnp.int32, (tokens, 1), 0
    ).astype(F32)


def tril_mask(tokens):
    t = lax.broadcasted_iota(jnp.int32, (tokens, tokens), 0)
    s = lax.broadcasted_iota(jnp.int32, (tokens, tokens), 1)
    return t, s


def call(kernel, outs, args, *, smem=(), flops=0, bytes_accessed=0, name=None):
    return pl.pallas_call(
        kernel,
        out_shape=[jax.ShapeDtypeStruct(s, d) for s, d in outs],
        in_specs=[
            pl.BlockSpec(memory_space=pltpu.SMEM if i in smem else pltpu.VMEM)
            for i in range(len(args))
        ],
        out_specs=[pl.BlockSpec(memory_space=pltpu.VMEM) for _ in outs],
        compiler_params=pltpu.CompilerParams(vmem_limit_bytes=24 << 20),
        cost_estimate=pl.CostEstimate(
            flops=flops, bytes_accessed=bytes_accessed, transcendentals=0
        ),
        name=name,
    )(*args)


def start_kernel(
    seq_size,
    x_ref,
    g_ref,
    w_in_ref,
    w_bc_ref,
    w_out_ref,
    rates_ref,
    resets_ref,
    up_ref,
    gmp_ref,
    coef_ref,
    a_ref,
    sa_ref,
    table_ref,
    *pay_refs,
):
    tokens = x_ref.shape[1]
    channels = w_in_ref.shape[2]
    heads = rates_ref.shape[1]
    width = channels // heads
    states = w_bc_ref.shape[2] // 2
    x = x_ref[0]
    gm = mm(g_ref[...], w_out_ref[0], NT)
    coef = mm(x, w_bc_ref[0], NN)
    inner = mm(x, w_in_ref[0], NN).astype(BF16).astype(F32)

    lane_head = lax.broadcasted_iota(jnp.int32, (1, channels), 1) // width
    rate = jnp.zeros((1, channels), F32)
    for k in range(heads):
        rate = jnp.where(lane_head == k, rates_ref[0, k], rate)
    t, s = tril_mask(tokens)
    resets = resets_ref[...].astype(F32)
    count = jnp.sum(jnp.where(s <= t, resets, 0.0), axis=1, keepdims=True)
    log = count * LOG_KEEP - (column(tokens) + 1.0) * rate
    mid = log[tokens // 2 - 1 : tokens // 2, :]
    a = jnp.exp(log - mid)
    growth = expm1_small(2.0 * rate)
    scale = jnp.sqrt(growth / (1.0 + growth))
    emid = jnp.exp(mid)
    atot = a[tokens - 1 : tokens, :]
    up = (inner * (scale / a)).astype(BF16)
    gmp = (gm * a).astype(BF16)
    coef_b = coef.astype(BF16)
    up_ref[...] = up
    gmp_ref[...] = gmp
    coef_ref[...] = coef_b
    a_ref[...] = a
    sa_ref[...] = scale / a
    total = jnp.broadcast_to(count[tokens - 1 : tokens, :], (1, channels))
    table_ref[...] = jnp.concatenate(
        [rate, emid, atot, 1.0 / growth, total, jnp.zeros((TABLE_ROWS - 5, channels), F32)], axis=0
    )
    both = mm(coef_b, up, TN)
    state = atot * both[:states, :]
    both = mm(coef_b, gmp, TN)
    adjoint = emid * both[states:, :]
    me = lax.axis_index("seq")
    tail = jnp.broadcast_to(total, (8, channels))
    for k in range(1, seq_size):
        forward = me + k < seq_size
        data = jnp.where(forward, state, adjoint)
        pay_refs[k - 1][...] = jnp.concatenate([data, tail], axis=0).astype(BF16)


def local_kernel(up_ref, gmp_ref, coef_ref, gu_ref, gcoef_ref, lag_ref):
    tokens = up_ref.shape[0]
    states = coef_ref.shape[1] // 2
    up, gmp = up_ref[...], gmp_ref[...]
    coef = coef_ref[...]
    b_part, c_part = coef[:, :states], coef[:, states:]
    t, s = tril_mask(tokens)
    causal = s <= t
    scores = jnp.where(causal, mm(c_part, b_part, NT), 0.0)
    gu_ref[...] = mm(scores.astype(BF16), gmp, TN)
    lagged = (scores * (t - s).astype(F32)).astype(BF16)
    lag_ref[...] = jnp.sum(gmp.astype(F32) * mm(lagged, up, NN), axis=0, keepdims=True)
    gs = jnp.where(causal, mm(gmp, up, NT), 0.0).astype(BF16)
    gcoef_ref[...] = jnp.concatenate([mm(gs, c_part, TN), mm(gs, b_part, NN)], axis=1)


def unpack(seq_size, recv_refs, table_ref, states, tokens):
    channels = table_ref.shape[1]
    rate = table_ref[RATE : RATE + 1, :]
    me = lax.axis_index("seq")
    source = [lax.rem(me - k + seq_size, seq_size) for k in range(1, seq_size)]
    data = [r[...].astype(F32) for r in recv_refs]
    gap = [d[states : states + 1, :] * LOG_KEEP - tokens * rate for d in data]
    h_in = jnp.zeros((states, channels), F32)
    adj = jnp.zeros((states, channels), F32)
    weights = []
    for i, src in enumerate(source):
        forward = src < me
        low, high = jnp.minimum(src, me), jnp.maximum(src, me)
        log = jnp.zeros((1, channels), F32)
        for j, other in enumerate(source):
            if j != i:
                between = jnp.logical_and(other > low, other < high)
                log = log + jnp.where(between, gap[j], 0.0)
        weight = jnp.exp(log)
        term = weight * data[i][:states, :]
        h_in = h_in + jnp.where(forward, term, 0.0)
        adj = adj + jnp.where(forward, 0.0, term)
        weights.append(jnp.where(forward, 0.0, weight))
    return h_in, adj, weights


def finish(
    adj, hpp, gu, gcoef, lag, up_ref, gmp_ref, coef_ref, sa_ref, table_ref, x_ref, w_in_ref, w_bc_ref
):
    tokens, channels = up_ref.shape
    states = coef_ref.shape[1] // 2
    up, gmp, coef = up_ref[...], gmp_ref[...], coef_ref[...]
    atot = table_ref[ATOT : ATOT + 1, :]
    adjp = atot * adj
    zero = jnp.zeros((states, channels), BF16)
    adj_rows = jnp.concatenate([adjp.astype(BF16), zero], axis=0)
    h_rows = jnp.concatenate([zero, hpp.astype(BF16)], axis=0)
    v = mm(coef, adj_rows, NN)
    ch = mm(coef, h_rows, NN)
    gu = gu + v
    grad_inner = (sa_ref[...] * gu).astype(BF16)
    gcoef = (gcoef + mm(up, adj_rows, NT) + mm(gmp, h_rows, NT)).astype(BF16)
    back = mm(grad_inner, w_in_ref[0], NT) + mm(gcoef, w_bc_ref[0], NT)
    place = column(tokens)
    up_f, gmp_f = up.astype(F32), gmp.astype(F32)
    lag = (
        lag
        + jnp.sum(gmp_f * ((place + 1.0) * ch), axis=0, keepdims=True)
        + jnp.sum(up_f * ((tokens - 1.0 - place) * v), axis=0, keepdims=True)
        + tokens * jnp.sum(hpp * adjp, axis=0, keepdims=True)
    )
    total = jnp.sum(up_f * gu, axis=0, keepdims=True)
    rate_row = total * table_ref[INV : INV + 1, :] - lag
    dw = mm(gcoef, x_ref[0], TN)
    reduced = jnp.concatenate([dw, jnp.broadcast_to(rate_row, (8, channels))], axis=0)
    return back, reduced


def first_finish_kernel(
    seq_size,
    up_ref,
    gmp_ref,
    coef_ref,
    sa_ref,
    table_ref,
    x_ref,
    w_in_ref,
    w_bc_ref,
    gu_ref,
    gcoef_ref,
    lag_ref,
    g_ref,
    *refs,
):
    recv_refs, (send_ref, keep_ref, red_ref, hpp_ref, weight_ref) = (
        refs[: seq_size - 1],
        refs[seq_size - 1 :],
    )
    tokens = up_ref.shape[0]
    states = coef_ref.shape[1] // 2
    h_in, adj, weights = unpack(seq_size, recv_refs, table_ref, states, tokens)
    hpp = table_ref[EMID : EMID + 1, :] * h_in
    hpp_ref[...] = hpp
    for k, weight in enumerate(weights):
        weight_ref[k : k + 1, :] = weight
    back, red_ref[...] = finish(
        adj,
        hpp,
        gu_ref[...],
        gcoef_ref[...],
        lag_ref[...],
        up_ref,
        gmp_ref,
        coef_ref,
        sa_ref,
        table_ref,
        x_ref,
        w_in_ref,
        w_bc_ref,
    )
    split(back, g_ref[...], send_ref, keep_ref)


def split(back, g, send_ref, keep_ref):
    half = back.shape[1] // 2
    low = lax.axis_index("mp") == 0
    send_ref[...] = jnp.where(low, back[:, half:], back[:, :half]).astype(BF16)
    own = jnp.where(low, back[:, :half], back[:, half:])
    keep_ref[...] = own + jnp.where(low, g[:, :half], g[:, half:]).astype(F32)


def joined(mine, other):
    low = lax.axis_index("mp") == 0
    return jnp.concatenate([jnp.where(low, mine, other), jnp.where(low, other, mine)], axis=1)


def gather_adjoint(recv_refs, weight_ref):
    adj = None
    for k, r in enumerate(recv_refs):
        term = weight_ref[k : k + 1, :] * r[...].astype(F32)
        adj = term if adj is None else adj + term
    return adj


def hop_kernel(
    mine_ref, other_ref, w_out_ref, coef_ref, a_ref, table_ref, gmp_ref, adjoint_ref
):
    states = coef_ref.shape[1] // 2
    g = joined(mine_ref[...], other_ref[...])
    gmp = (a_ref[...] * mm(g, w_out_ref[0], NT)).astype(BF16)
    gmp_ref[...] = gmp
    both = mm(coef_ref[...], gmp, TN)
    adjoint_ref[...] = (table_ref[EMID : EMID + 1, :] * both[states:, :]).astype(BF16)


def middle_finish_kernel(
    seq_size,
    up_ref,
    gmp_ref,
    coef_ref,
    sa_ref,
    table_ref,
    x_ref,
    w_in_ref,
    w_bc_ref,
    gu_ref,
    gcoef_ref,
    lag_ref,
    mine_ref,
    other_ref,
    hpp_ref,
    weight_ref,
    *refs,
):
    recv_refs, (send_ref, keep_ref, red_ref) = refs[: seq_size - 1], refs[seq_size - 1 :]
    back, red_ref[...] = finish(
        gather_adjoint(recv_refs, weight_ref),
        hpp_ref[...],
        gu_ref[...],
        gcoef_ref[...],
        lag_ref[...],
        up_ref,
        gmp_ref,
        coef_ref,
        sa_ref,
        table_ref,
        x_ref,
        w_in_ref,
        w_bc_ref,
    )
    split(back, joined(mine_ref[...], other_ref[...]), send_ref, keep_ref)


def last_finish_kernel(
    seq_size,
    up_ref,
    gmp_ref,
    coef_ref,
    sa_ref,
    table_ref,
    x_ref,
    w_in_ref,
    w_bc_ref,
    gu_ref,
    gcoef_ref,
    lag_ref,
    kept_half_ref,
    kept_red_ref,
    hpp_ref,
    weight_ref,
    *refs,
):
    recv_refs, (part_ref, red_ref) = refs[: seq_size - 1], refs[seq_size - 1 :]
    back, red = finish(
        gather_adjoint(recv_refs, weight_ref),
        hpp_ref[...],
        gu_ref[...],
        gcoef_ref[...],
        lag_ref[...],
        up_ref,
        gmp_ref,
        coef_ref,
        sa_ref,
        table_ref,
        x_ref,
        w_in_ref,
        w_bc_ref,
    )
    active = lax.axis_index("section") == 0
    low = lax.axis_index("mp") == 0
    half = kept_half_ref[...]
    zero = jnp.zeros_like(half)
    done = jnp.concatenate([jnp.where(low, half, zero), jnp.where(low, zero, half)], axis=1)
    part_ref[...] = jnp.where(active, back.astype(BF16), done)
    red_ref[...] = jnp.where(active, red, kept_red_ref[...]).astype(BF16)


def output_kernel(part_ref, part2_ref, mine_ref, other_ref, red_ref, red2_ref, out_ref, sum_ref):
    active = lax.axis_index("section") == 0
    g = joined(mine_ref[...], other_ref[...]).astype(F32)
    g = jnp.where(active, g, 0.0)
    out_ref[0] = (g + (part_ref[...].astype(F32) + part2_ref[...].astype(F32))).astype(BF16)
    rows = red_ref.shape[0]
    own, other = red_ref[...].astype(F32), red2_ref[...].astype(F32)
    is_rate = lax.broadcasted_iota(jnp.int32, (rows, 1), 0) >= rows - 8
    sum_ref[...] = jnp.where(is_rate, own, own + other).astype(BF16)


def total_kernel(seq_size, heads, *refs):
    pieces, (w_ref, rate_ref) = refs[:seq_size], refs[seq_size:]
    me = lax.axis_index("seq")
    data = [r[...].astype(F32) for r in pieces]
    source = [lax.rem(me - k + seq_size, seq_size) for k in range(seq_size)]
    total = None
    for j in range(seq_size):
        term = data[0]
        for k in range(1, seq_size):
            term = jnp.where(source[k] == j, data[k], term)
        total = term if total is None else total + term
    rows, channels = total.shape
    w_ref[0] = total[: rows - 8, :].T
    width = channels // heads
    row = total[rows - 8 : rows - 7, :]
    lane = lax.broadcasted_iota(jnp.int32, (heads, channels), 1) // width
    head = lax.broadcasted_iota(jnp.int32, (heads, channels), 0)
    rate_ref[...] = jnp.sum(jnp.where(lane == head, row, 0.0), axis=1, keepdims=True)


def shards(section_inputs, cotangent, w_in, w_bc, w_out, decay_rates, resets):
    tokens, width = cotangent.shape
    channels = w_in.shape[2]
    coefs = w_bc.shape[2]
    states = coefs // 2
    heads = decay_rates.shape[1]
    seq_size = lax.axis_size("seq")
    sections = lax.axis_size("section")
    half = width // 2
    big = 2 * tokens * width * channels
    vec = ((tokens, channels), F32)

    up, gmp, coef, a, sa, table, *pay = call(
        functools.partial(start_kernel, seq_size),
        [
            ((tokens, channels), BF16),
            ((tokens, channels), BF16),
            ((tokens, coefs), BF16),
            vec,
            vec,
            ((TABLE_ROWS, channels), F32),
        ]
        + [((states + 8, channels), BF16)] * (seq_size - 1),
        [
            section_inputs,
            cotangent,
            w_in,
            w_bc,
            w_out,
            decay_rates,
            resets.reshape(1, tokens),
        ],
        smem=(5,),
        flops=2 * big,
        bytes_accessed=4 * width * channels,
        name="start",
    )
    recv = [rotate(p, "seq", k + 1) for k, p in enumerate(pay)]

    def local(gradient):
        return call(
            local_kernel,
            [vec, ((tokens, coefs), F32), ((1, channels), F32)],
            [up, gradient, coef],
            flops=big,
            bytes_accessed=4 * tokens * channels,
            name="local",
        )

    shared = lambda gradient: [up, gradient, coef, sa, table, section_inputs, w_in, w_bc]
    reduced = ((coefs + 8, channels), F32)
    section = lax.axis_index("section")
    send, keep, red, hpp, weight = call(
        functools.partial(first_finish_kernel, seq_size),
        [
            ((tokens, half), BF16),
            ((tokens, half), F32),
            reduced,
            ((states, channels), F32),
            ((seq_size - 1, channels), F32),
        ],
        [*shared(gmp), *local(gmp), cotangent, *recv],
        flops=big,
        bytes_accessed=2 * width * channels,
        name="first",
    )
    kept_half, kept_red = None, None
    for moment in range(1, sections):
        half_result = (keep + swap(send, "mp").astype(F32)).astype(BF16)
        was_active = section == sections - moment
        if kept_half is None:
            kept_half, kept_red = half_result, red
        else:
            kept_half = jnp.where(was_active, half_result, kept_half)
            kept_red = jnp.where(was_active, red, kept_red)
        mine = rotate(half_result, "section", -1)
        other = swap(mine, "mp")
        gmp, adjoint = call(
            hop_kernel,
            [((tokens, channels), BF16), ((states, channels), BF16)],
            [mine, other, w_out, coef, a, table],
            flops=big,
            bytes_accessed=2 * width * channels,
            name="hop",
        )
        recv = [rotate(adjoint, "seq", k) for k in range(1, seq_size)]
        if moment < sections - 1:
            send, keep, red = call(
                functools.partial(middle_finish_kernel, seq_size),
                [((tokens, half), BF16), ((tokens, half), F32), reduced],
                [*shared(gmp), *local(gmp), mine, other, hpp, weight, *recv],
                flops=big,
                bytes_accessed=2 * width * channels,
                name="middle",
            )
    part, red = call(
        functools.partial(last_finish_kernel, seq_size),
        [((tokens, width), BF16), ((coefs + 8, channels), BF16)],
        [*shared(gmp), *local(gmp), kept_half, kept_red, hpp, weight, *recv],
        flops=big,
        bytes_accessed=2 * width * channels,
        name="last",
    )
    out, red = call(
        output_kernel,
        [((1, tokens, width), BF16), ((coefs + 8, channels), BF16)],
        [part, swap(part, "mp"), mine, other, red, swap(red, "mp")],
        name="output",
    )
    grad_w, grad_rates = call(
        functools.partial(total_kernel, seq_size, heads),
        [((1, width, coefs), F32), ((heads, 1), F32)],
        [red] + [rotate(red, "seq", k) for k in range(1, seq_size)],
        name="total",
    )
    return out, grad_w, grad_rates.reshape(1, heads)


def solution(mesh):
    return jax.shard_map(
        shards,
        mesh=mesh,
        in_specs=(
            P("section", ("groups", "seq"), None),
            P(("groups", "seq"), None),
            P("section", None, "mp"),
            P("section", None, None),
            P("section", "mp", None),
            P("section", "mp"),
            P(("groups", "seq")),
        ),
        out_specs=(
            P("section", ("groups", "seq"), None),
            P("section", "groups", None),
            P("section", ("groups", "mp")),
        ),
        check_vma=False,
    )
```

time: 202 us -> 50.4 us (0.25)
  blocking collectives: 73 us -> 0 us
  matrix products: 35.2 us -> 0 us
  waiting for transfers between devices: 48.9 us -> 17.9 us
  between operations: 15.6 us -> 0.74 us
  starting transfers between devices: 2.71 us -> 16.2 us
  other arithmetic: 13.9 us -> 0.65 us
  Pallas kernels: 0 us -> 7.09 us
  local copies, waits for them, and re-layouts: 10.5 us -> 7.47 us
    all_gather x4 -> x0, blocking collectives: 53.7 us -> none  [the longest x2 27.6 us: advance(): all_adjoint = lax.all_gather(local_adjoint[None], 'seq', axis=0, tiled=True)]
    dot_general x28 -> x0, matrix products: 35.2 us -> none  [the longest x4 11.2 us: forward_over_span(): jnp.einsum('hts,shp->thp', weights, scaled, precision=highest)]
    psum x3 -> x0, waiting for transfers between devices: 33.7 us -> none  [the longest x1 23.6 us: shards(): rate_total, coef_total = lax.psum((kept_rate, coef_grad), 'seq')]
    psum x3 -> x0, blocking collectives: 19.3 us -> none  [the longest x1 12.5 us: shards(): rate_total, coef_total = lax.psum((kept_rate, coef_grad), 'seq')]
    ppermute x2 -> x14, starting transfers between devices: 2.58 us -> 16.2 us  [rotate(): return lax.ppermute(value, axis, [(i, (i + by) % n) for i in range(n)])]
    pallas_call x0 -> x8, Pallas kernels: none -> 7.09 us  [call(): pl.pallas_call(kernel, out_shape=[jax.ShapeDtypeStruct(s, d) for s, d in...]
    unnamed x14 -> x22, local copies, waits for them, and re-layouts: 3.81 us -> 7.47 us
    ppermute x2 -> x14, waiting for transfers between devices: 15.1 us -> 17.9 us  [rotate(): return lax.ppermute(value, axis, [(i, (i + by) % n) for i in range(n)])]
  transfers between devices with their start and end apart: 5 -> 14, of which waited for: 5 -> 10; matrix products, arithmetic and copies ran while one was open for 9% -> 0% of each run, Pallas kernels for 0% -> 3%
where the time goes in v1:
time: 50.4 us; the launch traced here: 50.1 us
  waiting for transfers between devices  17.9 us (36%)
  starting transfers between devices  16.2 us (32%)
  local copies, waits for them, and re-layouts  7.47 us (15%)
  Pallas kernels  7.09 us (14%)
  between operations  0.74 us (1%)
  other arithmetic  0.65 us (1%)
    ppermute x14, waiting for transfers between devices, rotate(): return lax.ppermute(value, axis, [(i, (i + by) % n) for i in range(n)])  17.9 us
    ppermute x14, starting transfers between devices, rotate(): return lax.ppermute(value, axis, [(i, (i + by) % n) for i in range(n)])  16.2 us
    unnamed x22, local copies, waits for them, and re-layouts  7.47 us
    pallas_call x8, Pallas kernels, call(): pl.pallas_call(kernel, out_shape=[jax.ShapeDtypeStruct(s, d) for s, d in...  7.09 us
  transfers between devices with their start and end apart: 14, of which 10 were waited for; matrix products, arithmetic and copies ran while one was open for 0% of the time, Pallas kernels for 3%

profile of v1, /device:TPU:0, one launch (start us, length us, event | category | flops | bytes accessed | tf_op | source)
XLA Modules:
  0.0 50.1 jit_solution(4793612129564546543)
XLA Ops:
  0.6 1.0 %copy.14.w_bc_ref = bf16[1,768,32]{2,1,0:T(8,128)(2,1)S(1)} copy(bf16[1,768,32]{1,2,0:T(8,128)(2,1)} %param.10) | data formatting | bytes 98304 | tf_op args[3]
  1.6 1.3 %copy-done = bf16[1,768,768]{2,1,0:T(8,128)(2,1)S(1)} copy-done((bf16[1,768,768]{2,1,0:T(8,128)(2,1)S(1)}, bf16[1,768,768]{2,1,0:T(8,128)(2,1)}, u32[]{:S(2)}) %copy-start) | copy-done | bytes 1179672
  2.9 1.3 %copy-done.2 = bf16[1,768,768]{2,1,0:T(8,128)(2,1)S(1)} copy-done((bf16[1,768,768]{2,1,0:T(8,128)(2,1)S(1)}, bf16[1,768,768]{2,1,0:T(8,128)(2,1)}, u32[]{:S(2)}) %copy-start.2) | copy-done | bytes 1179672
  4.1 0.9 %copy-done.4 = bf16[1,128,768]{2,1,0:T(8,128)(2,1)S(1)} copy-done((bf16[1,128,768]{2,1,0:T(8,128)(2,1)S(1)}, bf16[1,128,768]{2,1,0:T(8,128)(2,1)}, u32[]{:S(2)}) %copy-start.4) | copy-done | bytes 196632
  5.1 0.9 %copy-done.6 = bf16[128,768]{1,0:T(8,128)(2,1)S(1)} copy-done((bf16[128,768]{1,0:T(8,128)(2,1)S(1)}, bf16[128,768]{1,0:T(8,128)(2,1)}, u32[]{:S(2)}) %copy-start.6) | copy-done | bytes 196632
  7.3 1.4 %start.1 = (bf16[128,768]{1,0:T(8,128)(2,1)S(1)}, bf16[128,768]{1,0:T(8,128)(2,1)S(1)}, bf16[128,32]{1,0:T(8,128)(2,1)S(1)}, f32[128,768]{1,0:T(8,128)S(1)}, f32...) custom-call(bf16[1,128,768]{2,1,0:T(8,128)(2,1)S(1)} %copy-done.4, ...), custom_call_target="tpu_custom_call" | custom-call | flops 301989888 | bytes 2359296 | tf_op jit(solution)/shard_map/start/pallas_call | solution.py:53
  8.8 3.1 %collective-permute-start = (bf16[24,768]{1,0:T(8,128)(2,1)S(1)}, bf16[24,768]{1,0:T(8,128)(2,1)S(1)}, u32[]{:S(2)}, u32[]{:S(2)}) collective-permute-start(bf16[24,768]{1,0:T(8,128)(2,1)S(1)} %get-tuple-element.39), channel_id=1, source_target_pairs={{0,4},{4,8},{8,12},{12,0},{1,5},{5,9},{9,13},{13,1},{2,6},{6,10},{... | collective-permute-start | bytes 110600 | tf_op jit(solution)/shard_map/ppermute | solution.py:29
  11.8 2.6 %collective-permute-start.1 = (bf16[24,768]{1,0:T(8,128)(2,1)S(1)}, bf16[24,768]{1,0:T(8,128)(2,1)S(1)}, u32[]{:S(2)}, u32[]{:S(2)}) collective-permute-start(bf16[24,768]{1,0:T(8,128)(2,1)S(1)} %get-tuple-element.40), channel_id=1, source_target_pairs={{0,8},{4,12},{8,0},{12,4},{1,9},{5,13},{9,1},{13,5},{2,10},{6,14},... | collective-permute-start | bytes 110600 | tf_op jit(solution)/shard_map/ppermute | solution.py:29
  14.4 1.3 %collective-permute-start.2 = (bf16[24,768]{1,0:T(8,128)(2,1)S(1)}, bf16[24,768]{1,0:T(8,128)(2,1)S(1)}, u32[]{:S(2)}, u32[]{:S(2)}) collective-permute-start(bf16[24,768]{1,0:T(8,128)(2,1)S(1)} %get-tuple-element.41), channel_id=1, source_target_pairs={{0,12},{4,0},{8,4},{12,8},{1,13},{5,1},{9,5},{13,9},{2,14},{6,2},{... | collective-permute-start | bytes 110600 | tf_op jit(solution)/shard_map/ppermute | solution.py:29
  15.8 0.8 %local.2 = (f32[128,768]{1,0:T(8,128)S(1)}, f32[128,32]{1,0:T(8,128)S(1)}, f32[1,768]{1,0:T(1,128)S(1)}) custom-call(bf16[128,768]{1,0:T(8,128)(2,1)S(1)} %get-tuple-element.31.up_ref, bf16[128,768]{1,0:T(8,128)(2,1)S(1)} %get-tuple-element.32.gmp_ref, bf16[128,32]{1,0:T(8,128)(2,1)S(1)} %get-tuple-element.33.coef_ref), custom_call_target="tpu_custom_call" | custom-call | flops 150994944 | bytes 393216 | tf_op jit(solution)/shard_map/local/pallas_call | solution.py:53
  17.1 1.3 %collective-permute-done.2.refs_2_ = bf16[24,768]{1,0:T(8,128)(2,1)S(1)} collective-permute-done((bf16[24,768]{1,0:T(8,128)(2,1)S(1)}, bf16[24,768]{1,0:T(8,128)(2,1)S(1)}, u32[]{:S(2)}, u32[]{:S(2)}) %collective-permute-start.2) | collective-permute-done | bytes 36896 | tf_op jit(solution)/shard_map/ppermute | solution.py:29
  18.4 1.2 %first.1 = (bf16[128,384]{1,0:T(8,128)(2,1)S(1)}, f32[128,384]{1,0:T(8,128)S(1)}, f32[40,768]{1,0:T(8,128)S(1)}, f32[16,768]{1,0:T(8,128)S(1)}, f32[3,768]{1,0:T(4,128)S(1)}) custom-call(bf16[128,768]{1,0:T(8,128)(2,1)S(1)} %get-tuple-element.31.up_ref, bf16[128,768]{1,0:T(8,128)(2,1)S(1)} %get-tuple-element.32.gmp_ref, ...), custom_call_target="tpu_custom_call" | custom-call | flops 150994944 | bytes 1179648 | tf_op jit(solution)/shard_map/first/pallas_call | solution.py:53
  19.7 1.3 %collective-permute-done.3 = bf16[128,384]{1,0:T(8,128)(2,1)S(1)} collective-permute-done((bf16[128,384]{1,0:T(8,128)(2,1)S(1)}, bf16[128,384]{1,0:T(8,128)(2,1)S(1)}, u32[]{:S(2)}, u32[]{:S(2)}) %collective-permute-start.3) | collective-permute-done | bytes 98336 | tf_op jit(solution)/shard_map/ppermute | solution.py:29
  21.0 1.6 %collective-permute-start.4 = (bf16[128,384]{1,0:T(8,128)(2,1)S(1)}, bf16[128,384]{1,0:T(8,128)(2,1)S(1)}, u32[]{:S(2)}, u32[]{:S(2)}) collective-permute-start(bf16[128,384]{1,0:T(8,128)(2,1)S(1)} %add_convert_fusion.kept_half_ref), channel_id=1, source_target_pairs={{0,2},{2,0},{1,3},{3,1},{4,6},{6,4},{5,7},{7,5},{8,10},{10,8},{9,1... | collective-permute-start | bytes 294920 | tf_op jit(solution)/shard_map/ppermute | solution.py:29
  22.6 3.4 %collective-permute-done.4.mine_ref = bf16[128,384]{1,0:T(8,128)(2,1)S(1)} collective-permute-done((bf16[128,384]{1,0:T(8,128)(2,1)S(1)}, bf16[128,384]{1,0:T(8,128)(2,1)S(1)}, u32[]{:S(2)}, u32[]{:S(2)}) %collective-permute-start.4) | collective-permute-done | bytes 98336 | tf_op jit(solution)/shard_map/ppermute | solution.py:29
  25.9 1.3 %collective-permute-done.5.other_ref = bf16[128,384]{1,0:T(8,128)(2,1)S(1)} collective-permute-done((bf16[128,384]{1,0:T(8,128)(2,1)S(1)}, bf16[128,384]{1,0:T(8,128)(2,1)S(1)}, u32[]{:S(2)}, u32[]{:S(2)}) %collective-permute-start.5) | collective-permute-done | bytes 98336 | tf_op jit(solution)/shard_map/ppermute | solution.py:29
  27.8 3.2 %collective-permute-start.8 = (bf16[16,768]{1,0:T(8,128)(2,1)S(1)}, bf16[16,768]{1,0:T(8,128)(2,1)S(1)}, u32[]{:S(2)}, u32[]{:S(2)}) collective-permute-start(bf16[16,768]{1,0:T(8,128)(2,1)S(1)} %get-tuple-element.52), channel_id=1, source_target_pairs={{0,12},{4,0},{8,4},{12,8},{1,13},{5,1},{9,5},{13,9},{2,14},{6,2},{... | collective-permute-start | bytes 73736 | tf_op jit(solution)/shard_map/ppermute | solution.py:29
  31.7 0.8 %local.3 = (f32[128,768]{1,0:T(8,128)S(1)}, f32[128,32]{1,0:T(8,128)S(1)}, f32[1,768]{1,0:T(1,128)S(1)}) custom-call(bf16[128,768]{1,0:T(8,128)(2,1)S(1)} %get-tuple-element.31.up_ref, bf16[128,768]{1,0:T(8,128)(2,1)S(1)} %get-tuple-element.45.gmp_ref, bf16[128,32]{1,0:T(8,128)(2,1)S(1)} %get-tuple-element.33.coef_ref), custom_call_target="tpu_custom_call" | custom-call | flops 150994944 | bytes 393216 | tf_op jit(solution)/shard_map/local/pallas_call | solution.py:53
  32.6 3.3 %collective-permute-done.7.refs_1_ = bf16[16,768]{1,0:T(8,128)(2,1)S(1)} collective-permute-done((bf16[16,768]{1,0:T(8,128)(2,1)S(1)}, bf16[16,768]{1,0:T(8,128)(2,1)S(1)}, u32[]{:S(2)}, u32[]{:S(2)}) %collective-permute-start.7) | collective-permute-done | bytes 24608 | tf_op jit(solution)/shard_map/ppermute | solution.py:29
  36.7 1.2 %last.1 = (bf16[128,768]{1,0:T(8,128)(2,1)S(1)}, bf16[40,768]{1,0:T(8,128)(2,1)S(1)}) custom-call(bf16[128,768]{1,0:T(8,128)(2,1)S(1)} %get-tuple-element.31.up_ref, bf16[128,768]{1,0:T(8,128)(2,1)S(1)} %get-tuple-element.45.gmp_ref, bf16[128,32]{1,0:T(8,128)(2,1)S(1)} %get-tuple-element.33.coef_ref, f32[128,768]{1,0:T(8,128)S(1)} %get-tuple-element.34.sa_ref, ...), custom_call_target="tpu_custom_call" | custom-call | flops 150994944 | bytes 1179648 | tf_op jit(solution)/shard_map/last/pallas_call | solution.py:53
  38.5 1.0 %collective-permute-done.10.red2_ref = bf16[40,768]{1,0:T(8,128)(2,1)S(1)} collective-permute-done((bf16[40,768]{1,0:T(8,128)(2,1)S(1)}, bf16[40,768]{1,0:T(8,128)(2,1)S(1)}, u32[]{:S(2)}, u32[]{:S(2)}) %collective-permute-start.10) | collective-permute-done | bytes 61472 | tf_op jit(solution)/shard_map/ppermute | solution.py:29
  41.4 2.0 %collective-permute-start.11 = (bf16[40,768]{1,0:T(8,128)(2,1)S(1)}, bf16[40,768]{1,0:T(8,128)(2,1)S(1)}, u32[]{:S(2)}, u32[]{:S(2)}) collective-permute-start(bf16[40,768]{1,0:T(8,128)(2,1)S(1)} %get-tuple-element.56.refs_0_), channel_id=1, source_target_pairs={{0,4},{4,8},{8,12},{12,0},{1,5},{5,9},{9,13},{13,1},{2,6},{6,10},{... | collective-permute-start | bytes 184328 | tf_op jit(solution)/shard_map/ppermute | solution.py:29
  43.4 1.7 %collective-permute-done.13.refs_3_ = bf16[40,768]{1,0:T(8,128)(2,1)S(1)} collective-permute-done((bf16[40,768]{1,0:T(8,128)(2,1)S(1)}, bf16[40,768]{1,0:T(8,128)(2,1)S(1)}, u32[]{:S(2)}, u32[]{:S(2)}) %collective-permute-start.13) | collective-permute-done | bytes 61472 | tf_op jit(solution)/shard_map/ppermute | solution.py:29
  45.1 3.3 %collective-permute-done.12.refs_2_ = bf16[40,768]{1,0:T(8,128)(2,1)S(1)} collective-permute-done((bf16[40,768]{1,0:T(8,128)(2,1)S(1)}, bf16[40,768]{1,0:T(8,128)(2,1)S(1)}, u32[]{:S(2)}, u32[]{:S(2)}) %collective-permute-start.12) | collective-permute-done | bytes 61472 | tf_op jit(solution)/shard_map/ppermute | solution.py:29
  (36 shorter events, 8.1 us)
Async XLA Ops:
  1.6 1.3 %copy-start = (bf16[1,768,768]{2,1,0:T(8,128)(2,1)S(1)}, bf16[1,768,768]{2,1,0:T(8,128)(2,1)}, u32[]{:S(2)}) copy-start(bf16[1,768,768]{2,1,0:T(8,128)(2,1)} %w_in_ref.5) | copy-start | bytes 3538948
  2.9 1.3 %copy-start.2 = (bf16[1,768,768]{2,1,0:T(8,128)(2,1)S(1)}, bf16[1,768,768]{2,1,0:T(8,128)(2,1)}, u32[]{:S(2)}) copy-start(bf16[1,768,768]{2,1,0:T(8,128)(2,1)} %w_out_ref.3) | copy-start | bytes 3538948
  4.1 0.9 %copy-start.4 = (bf16[1,128,768]{2,1,0:T(8,128)(2,1)S(1)}, bf16[1,128,768]{2,1,0:T(8,128)(2,1)}, u32[]{:S(2)}) copy-start(bf16[1,128,768]{2,1,0:T(8,128)(2,1)} %x_ref.5) | copy-start | bytes 589828
  5.1 0.9 %copy-start.6 = (bf16[128,768]{1,0:T(8,128)(2,1)S(1)}, bf16[128,768]{1,0:T(8,128)(2,1)}, u32[]{:S(2)}) copy-start(bf16[128,768]{1,0:T(8,128)(2,1)} %g_ref.3) | copy-start | bytes 589828
  6.0 0.7 %copy-start.8 = (f32[1,12]{1,0:T(1,128)S(1)}, f32[1,12]{1,0:T(1,128)}, u32[]{:S(2)}) copy-start(f32[1,12]{1,0:T(1,128)} %rates_ref.1) | copy-start | bytes 148
  6.7 0.7 %copy-start.9 = (s32[128]{0:T(128)S(1)}, s32[128]{0:T(128)}, u32[]{:S(2)}) copy-start(s32[128]{0:T(128)} %param.13) | copy-start | bytes 1540
  7.3 11.1 %copy-start.1 = (bf16[1,768,768]{2,1,0:T(8,128)(2,1)S(1)}, bf16[1,768,768]{2,1,0:T(8,128)(2,1)}, u32[]{:S(2)}) copy-start(bf16[1,768,768]{2,1,0:T(8,128)(2,1)} %w_in_ref.5) | copy-start | bytes 3538948
  7.3 11.1 %copy-start.5 = (bf16[1,128,768]{2,1,0:T(8,128)(2,1)S(1)}, bf16[1,128,768]{2,1,0:T(8,128)(2,1)}, u32[]{:S(2)}) copy-start(bf16[1,128,768]{2,1,0:T(8,128)(2,1)} %x_ref.5) | copy-start | bytes 589828
  7.3 11.1 %copy-start.7 = (bf16[128,768]{1,0:T(8,128)(2,1)S(1)}, bf16[128,768]{1,0:T(8,128)(2,1)}, u32[]{:S(2)}) copy-start(bf16[128,768]{1,0:T(8,128)(2,1)} %g_ref.3) | copy-start | bytes 589828
  8.8 7.9 %collective-permute-start = (bf16[24,768]{1,0:T(8,128)(2,1)S(1)}, bf16[24,768]{1,0:T(8,128)(2,1)S(1)}, u32[]{:S(2)}, u32[]{:S(2)}) collective-permute-start(bf16[24,768]{1,0:T(8,128)(2,1)S(1)} %get-tuple-element.39), channel_id=1, source_target_pairs={{0,4},{4,8},{8,12},{12,0},{1,5},{5,9},{9,13},{13,1},{2,6},{6,10},{... | collective-permute-start | bytes 110600 | tf_op jit(solution)/shard_map/ppermute | solution.py:29
  11.8 5.3 %collective-permute-start.1 = (bf16[24,768]{1,0:T(8,128)(2,1)S(1)}, bf16[24,768]{1,0:T(8,128)(2,1)S(1)}, u32[]{:S(2)}, u32[]{:S(2)}) collective-permute-start(bf16[24,768]{1,0:T(8,128)(2,1)S(1)} %get-tuple-element.40), channel_id=1, source_target_pairs={{0,8},{4,12},{8,0},{12,4},{1,9},{5,13},{9,1},{13,5},{2,10},{6,14},... | collective-permute-start | bytes 110600 | tf_op jit(solution)/shard_map/ppermute | solution.py:29
  14.4 4.0 %collective-permute-start.2 = (bf16[24,768]{1,0:T(8,128)(2,1)S(1)}, bf16[24,768]{1,0:T(8,128)(2,1)S(1)}, u32[]{:S(2)}, u32[]{:S(2)}) collective-permute-start(bf16[24,768]{1,0:T(8,128)(2,1)S(1)} %get-tuple-element.41), channel_id=1, source_target_pairs={{0,12},{4,0},{8,4},{12,8},{1,13},{5,1},{9,5},{13,9},{2,14},{6,2},{... | collective-permute-start | bytes 110600 | tf_op jit(solution)/shard_map/ppermute | solution.py:29
  18.4 8.8 %copy-start.3 = (bf16[1,768,768]{2,1,0:T(8,128)(2,1)S(1)}, bf16[1,768,768]{2,1,0:T(8,128)(2,1)}, u32[]{:S(2)}) copy-start(bf16[1,768,768]{2,1,0:T(8,128)(2,1)} %w_out_ref.3) | copy-start | bytes 3538948
  19.6 1.4 %collective-permute-start.3 = (bf16[128,384]{1,0:T(8,128)(2,1)S(1)}, bf16[128,384]{1,0:T(8,128)(2,1)S(1)}, u32[]{:S(2)}, u32[]{:S(2)}) collective-permute-start(bf16[128,384]{1,0:T(8,128)(2,1)S(1)} %get-tuple-element.43), channel_id=1, source_target_pairs={{0,1},{1,0},{2,3},{3,2},{4,5},{5,4},{6,7},{7,6},{8,9},{9,8},{10,11... | collective-permute-start | bytes 294920 | tf_op jit(solution)/shard_map/ppermute | solution.py:29
  21.0 4.9 %collective-permute-start.4 = (bf16[128,384]{1,0:T(8,128)(2,1)S(1)}, bf16[128,384]{1,0:T(8,128)(2,1)S(1)}, u32[]{:S(2)}, u32[]{:S(2)}) collective-permute-start(bf16[128,384]{1,0:T(8,128)(2,1)S(1)} %add_convert_fusion.kept_half_ref), channel_id=1, source_target_pairs={{0,2},{2,0},{1,3},{3,1},{4,6},{6,4},{5,7},{7,5},{8,10},{10,8},{9,1... | collective-permute-start | bytes 294920 | tf_op jit(solution)/shard_map/ppermute | solution.py:29
  25.9 1.3 %collective-permute-start.5 = (bf16[128,384]{1,0:T(8,128)(2,1)S(1)}, bf16[128,384]{1,0:T(8,128)(2,1)S(1)}, u32[]{:S(2)}, u32[]{:S(2)}) collective-permute-start(bf16[128,384]{1,0:T(8,128)(2,1)S(1)} %collective-permute-done.4.mine_ref), channel_id=1, source_target_pairs={{0,1},{1,0},{2,3},{3,2},{4,5},{5,4},{6,7},{7,6},{8,9},{9,8},{10,11... | collective-permute-start | bytes 294920 | tf_op jit(solution)/shard_map/ppermute | solution.py:29
  27.8 4.7 %collective-permute-start.8 = (bf16[16,768]{1,0:T(8,128)(2,1)S(1)}, bf16[16,768]{1,0:T(8,128)(2,1)S(1)}, u32[]{:S(2)}, u32[]{:S(2)}) collective-permute-start(bf16[16,768]{1,0:T(8,128)(2,1)S(1)} %get-tuple-element.52), channel_id=1, source_target_pairs={{0,12},{4,0},{8,4},{12,8},{1,13},{5,1},{9,5},{13,9},{2,14},{6,2},{... | collective-permute-start | bytes 73736 | tf_op jit(solution)/shard_map/ppermute | solution.py:29
  31.1 4.8 %collective-permute-start.7 = (bf16[16,768]{1,0:T(8,128)(2,1)S(1)}, bf16[16,768]{1,0:T(8,128)(2,1)S(1)}, u32[]{:S(2)}, u32[]{:S(2)}) collective-permute-start(bf16[16,768]{1,0:T(8,128)(2,1)S(1)} %get-tuple-element.52), channel_id=1, source_target_pairs={{0,8},{4,12},{8,0},{12,4},{1,9},{5,13},{9,1},{13,5},{2,10},{6,14},... | collective-permute-start | bytes 73736 | tf_op jit(solution)/shard_map/ppermute | solution.py:29
  31.1 5.6 %collective-permute-start.6 = (bf16[16,768]{1,0:T(8,128)(2,1)S(1)}, bf16[16,768]{1,0:T(8,128)(2,1)S(1)}, u32[]{:S(2)}, u32[]{:S(2)}) collective-permute-start(bf16[16,768]{1,0:T(8,128)(2,1)S(1)} %get-tuple-element.52), channel_id=1, source_target_pairs={{0,4},{4,8},{8,12},{12,0},{1,5},{5,9},{9,13},{13,1},{2,6},{6,10},{... | collective-permute-start | bytes 73736 | tf_op jit(solution)/shard_map/ppermute | solution.py:29
  37.9 1.6 %collective-permute-start.9 = (bf16[128,768]{1,0:T(8,128)(2,1)S(1)}, bf16[128,768]{1,0:T(8,128)(2,1)S(1)}, u32[]{:S(2)}, u32[]{:S(2)}) collective-permute-start(bf16[128,768]{1,0:T(8,128)(2,1)S(1)} %get-tuple-element.53.part_ref), channel_id=1, source_target_pairs={{0,1},{1,0},{2,3},{3,2},{4,5},{5,4},{6,7},{7,6},{8,9},{9,8},{10,11... | collective-permute-start | bytes 589832 | tf_op jit(solution)/shard_map/ppermute | solution.py:29
  38.0 1.5 %collective-permute-start.10 = (bf16[40,768]{1,0:T(8,128)(2,1)S(1)}, bf16[40,768]{1,0:T(8,128)(2,1)S(1)}, u32[]{:S(2)}, u32[]{:S(2)}) collective-permute-start(bf16[40,768]{1,0:T(8,128)(2,1)S(1)} %get-tuple-element.54.red_ref), channel_id=1, source_target_pairs={{0,1},{1,0},{2,3},{3,2},{4,5},{5,4},{6,7},{7,6},{8,9},{9,8},{10,11... | collective-permute-start | bytes 184328 | tf_op jit(solution)/shard_map/ppermute | solution.py:29
  40.3 4.9 %collective-permute-start.13 = (bf16[40,768]{1,0:T(8,128)(2,1)S(1)}, bf16[40,768]{1,0:T(8,128)(2,1)S(1)}, u32[]{:S(2)}, u32[]{:S(2)}) collective-permute-start(bf16[40,768]{1,0:T(8,128)(2,1)S(1)} %get-tuple-element.56.refs_0_), channel_id=1, source_target_pairs={{0,12},{4,0},{8,4},{12,8},{1,13},{5,1},{9,5},{13,9},{2,14},{6,2},{... | collective-permute-start | bytes 184328 | tf_op jit(solution)/shard_map/ppermute | solution.py:29
  40.8 7.6 %collective-permute-start.12 = (bf16[40,768]{1,0:T(8,128)(2,1)S(1)}, bf16[40,768]{1,0:T(8,128)(2,1)S(1)}, u32[]{:S(2)}, u32[]{:S(2)}) collective-permute-start(bf16[40,768]{1,0:T(8,128)(2,1)S(1)} %get-tuple-element.56.refs_0_), channel_id=1, source_target_pairs={{0,8},{4,12},{8,0},{12,4},{1,9},{5,13},{9,1},{13,5},{2,10},{6,14},... | collective-permute-start | bytes 184328 | tf_op jit(solution)/shard_map/ppermute | solution.py:29
  41.4 7.1 %collective-permute-start.11 = (bf16[40,768]{1,0:T(8,128)(2,1)S(1)}, bf16[40,768]{1,0:T(8,128)(2,1)S(1)}, u32[]{:S(2)}, u32[]{:S(2)}) collective-permute-start(bf16[40,768]{1,0:T(8,128)(2,1)S(1)} %get-tuple-element.56.refs_0_), channel_id=1, source_target_pairs={{0,4},{4,8},{8,12},{12,0},{1,5},{5,9},{9,13},{13,1},{2,6},{6,10},{... | collective-permute-start | bytes 184328 | tf_op jit(solution)/shard_map/ppermute | solution.py:29

commit v2 on v1

v2 whole, which is shorter than its diff:
```python
import functools
import math

import jax
import jax.numpy as jnp
from jax import lax
from jax.experimental import pallas as pl
from jax.experimental.pallas import tpu as pltpu
from jax.sharding import PartitionSpec as P

LOG_KEEP = math.log(0.6)
F32 = jnp.float32
BF16 = jnp.bfloat16

NN = (((1,), (0,)), ((), ()))
NT = (((1,), (1,)), ((), ()))
TN = (((0,), (0,)), ((), ()))

RATE, EMID, ATOT, INV, COUNT = 0, 1, 2, 3, 4
TABLE_ROWS = 8
OUT_CHUNKS, IN_CHUNKS = 2, 2


def mm(a, b, dims):
    return lax.dot_general(a, b, dims, preferred_element_type=F32)


def rotate(value, axis, by):
    n = lax.axis_size(axis)
    return lax.ppermute(value, axis, [(i, (i + by) % n) for i in range(n)])


def partner(value, axis, k):
    n = lax.axis_size(axis)
    return lax.ppermute(value, axis, [(i, i ^ k) for i in range(n)])


def swap(value, axis):
    return rotate(value, axis, 1)


def expm1_small(y):
    return y * (1 + y / 2 * (1 + y / 3 * (1 + y / 4 * (1 + y / 5 * (1 + y / 6)))))


def column(tokens):
    return lax.broadcasted_iota(jnp.int32, (tokens, 1), 0).astype(F32)


def tril_mask(tokens):
    t = lax.broadcasted_iota(jnp.int32, (tokens, tokens), 0)
    s = lax.broadcasted_iota(jnp.int32, (tokens, tokens), 1)
    return t, s


def call(kernel, outs, args, *, space=pltpu.VMEM, scratch=(), flops=0, bytes_accessed=0, name=None):
    if space is pltpu.HBM:
        args = [pltpu.with_memory_space_constraint(a, space) for a in args]
    return pl.pallas_call(
        kernel,
        out_shape=[jax.ShapeDtypeStruct(s, d) for s, d in outs],
        in_specs=[pl.BlockSpec(memory_space=space) for _ in args],
        out_specs=[pl.BlockSpec(memory_space=pltpu.VMEM) for _ in outs],
        scratch_shapes=list(scratch),
        compiler_params=pltpu.CompilerParams(vmem_limit_bytes=24 << 20),
        cost_estimate=pl.CostEstimate(
            flops=flops, bytes_accessed=bytes_accessed, transcendentals=0
        ),
        name=name,
    )(*args)


def start_kernel(
    seq_size,
    x_hbm,
    g_hbm,
    w_in_hbm,
    w_bc_hbm,
    w_out_hbm,
    rates_hbm,
    resets_hbm,
    up_ref,
    gmp_ref,
    coef_ref,
    a_ref,
    sa_ref,
    table_ref,
    *refs,
):
    pay_refs = refs[: seq_size - 1]
    x_ref, g_ref, w_in_ref, w_bc_ref, w_out_ref, rates_ref, resets_ref, small_sem, wide_sem = refs[
        seq_size - 1 :
    ]
    tokens = x_hbm.shape[1]
    channels = w_in_hbm.shape[2]
    heads = rates_hbm.shape[1]
    width = channels // heads
    states = w_bc_hbm.shape[1] // 2
    small = [
        pltpu.make_async_copy(src, dst, small_sem.at[i])
        for i, (src, dst) in enumerate(
            [
                (rates_hbm, rates_ref),
                (resets_hbm, resets_ref),
                (g_hbm, g_ref),
                (x_hbm.at[0], x_ref),
                (w_bc_hbm.at[0], w_bc_ref),
            ]
        )
    ]
    rows, cols = channels // OUT_CHUNKS, channels // IN_CHUNKS
    out_parts = [slice(c * rows, (c + 1) * rows) for c in range(OUT_CHUNKS)]
    in_parts = [slice(c * cols, (c + 1) * cols) for c in range(IN_CHUNKS)]
    from_out = [
        pltpu.make_async_copy(w_out_hbm.at[0, p, :], w_out_ref.at[p, :], wide_sem.at[i])
        for i, p in enumerate(out_parts)
    ]
    from_in = [
        pltpu.make_async_copy(w_in_hbm.at[0, :, p], w_in_ref.at[:, p], wide_sem.at[OUT_CHUNKS + i])
        for i, p in enumerate(in_parts)
    ]
    for copy in small[:3] + from_out + small[3:] + from_in:
        copy.start()
    small[0].wait()
    small[1].wait()

    lane_head = lax.broadcasted_iota(jnp.int32, (1, channels), 1) // width
    rate = jnp.zeros((1, channels), F32)
    for k in range(heads):
        rate = jnp.where(lane_head == k, rates_ref[0, k], rate)
    t, s = tril_mask(tokens)
    resets = resets_ref[...].astype(F32)
    count = jnp.sum(jnp.where(s <= t, resets, 0.0), axis=1, keepdims=True)
    log = count * LOG_KEEP - (column(tokens) + 1.0) * rate
    mid = log[tokens // 2 - 1 : tokens // 2, :]
    a = jnp.exp(log - mid)
    growth = expm1_small(2.0 * rate)
    scale = jnp.sqrt(growth / (1.0 + growth))
    emid = jnp.exp(mid)
    atot = a[tokens - 1 : tokens, :]
    a_ref[...] = a
    total = jnp.broadcast_to(count[tokens - 1 : tokens, :], (1, channels))
    table_ref[...] = jnp.concatenate(
        [rate, emid, atot, 1.0 / growth, total, jnp.zeros((TABLE_ROWS - 5, channels), F32)], axis=0
    )

    small[2].wait()
    g = g_ref[...]
    for copy, part in zip(from_out, out_parts):
        copy.wait()
        gmp_ref[:, part] = (mm(g, w_out_ref[part, :], NT) * a[:, part]).astype(BF16)
    small[3].wait()
    small[4].wait()
    x = x_ref[...]
    coef = mm(x, w_bc_ref[...], NT).astype(BF16)
    coef_ref[...] = coef
    adjoint = emid * mm(coef, gmp_ref[...], TN)[states:, :]
    sa = scale / a
    sa_ref[...] = sa
    state = []
    for copy, part in zip(from_in, in_parts):
        copy.wait()
        inner = mm(x, w_in_ref[:, part], NN)
        up = (inner.astype(BF16).astype(F32) * sa[:, part]).astype(BF16)
        up_ref[:, part] = up
        state.append(atot[:, part] * mm(coef, up, TN)[:states, :])
    state = jnp.concatenate(state, axis=1)
    me = lax.axis_index("seq")
    tail = jnp.broadcast_to(count[tokens - 1 : tokens, :], (states, 128)).astype(BF16)
    for k in range(1, seq_size):
        forward = (me ^ k) > me
        pay_refs[k - 1][:, :channels] = jnp.where(forward, state, adjoint).astype(BF16)
        pay_refs[k - 1][:, channels:] = tail


def split(value):
    half = value.shape[1] // 2
    low = lax.axis_index("mp") == 0
    left, right = value[:, :half], value[:, half:]
    return jnp.where(low, left, right), jnp.where(low, right, left)


def joined(mine, other):
    low = lax.axis_index("mp") == 0
    return jnp.concatenate([jnp.where(low, mine, other), jnp.where(low, other, mine)], axis=1)


def coef_grads(gs, b_part, c_part):
    return jnp.concatenate([mm(gs, c_part, TN), mm(gs, b_part, NN)], axis=1)


def local_kernel(up_ref, gmp_ref, coef_ref, gu_ref, gcoef_ref, lag_ref):
    tokens = up_ref.shape[0]
    states = coef_ref.shape[1] // 2
    up, gmp = up_ref[...], gmp_ref[...]
    coef = coef_ref[...]
    b_part, c_part = coef[:, :states], coef[:, states:]
    t, s = tril_mask(tokens)
    causal = s <= t
    scores = jnp.where(causal, mm(c_part, b_part, NT), 0.0)
    gu_ref[...] = mm(scores.astype(BF16), gmp, TN)
    lagged = (scores * (t - s).astype(F32)).astype(BF16)
    lag_ref[...] = jnp.sum(gmp.astype(F32) * mm(lagged, up, NN), axis=0, keepdims=True)
    gs = jnp.where(causal, mm(gmp, up, NT), 0.0).astype(BF16)
    gcoef_ref[...] = coef_grads(gs, b_part, c_part)


def unpack(seq_size, recv_refs, table_ref, states, tokens):
    channels = table_ref.shape[1]
    rate = table_ref[RATE : RATE + 1, :]
    me = lax.axis_index("seq")
    source = [me ^ k for k in range(1, seq_size)]
    data = [r[:, :channels].astype(F32) for r in recv_refs]
    gap = [
        r[:1, channels : channels + 1].astype(F32) * LOG_KEEP - tokens * rate for r in recv_refs
    ]
    h_in = jnp.zeros((states, channels), F32)
    adj = jnp.zeros((states, channels), F32)
    weights = []
    for i, src in enumerate(source):
        forward = src < me
        low, high = jnp.minimum(src, me), jnp.maximum(src, me)
        log = jnp.zeros((1, channels), F32)
        for j, other in enumerate(source):
            if j != i:
                between = jnp.logical_and(other > low, other < high)
                log = log + jnp.where(between, gap[j], 0.0)
        weight = jnp.exp(log)
        term = weight * data[i]
        h_in = h_in + jnp.where(forward, term, 0.0)
        adj = adj + jnp.where(forward, 0.0, term)
        weights.append(jnp.where(forward, 0.0, weight))
    return h_in, adj, weights


def state_rows(hpp):
    return jnp.concatenate([jnp.zeros_like(hpp), hpp], axis=0).astype(BF16)


def input_gradient(rows, gu, gcoef, coef, sa_ref, w_in_ref, w_bc_ref):
    grad_inner = (sa_ref[...] * (gu + mm(coef, rows, NN))).astype(BF16)
    return mm(grad_inner, w_in_ref[0], NT) + mm(gcoef, w_bc_ref[0], NN)


def adjoint_rows(adj, table_ref):
    adjp = table_ref[ATOT : ATOT + 1, :] * adj
    return jnp.concatenate([adjp, jnp.zeros_like(adjp)], axis=0).astype(BF16)


def coef_total(rows, h_rows, gcoef_ref, up, gmp):
    return (gcoef_ref[...] + mm(gmp, h_rows, NT) + mm(up, rows, NT)).astype(BF16)


def parameter_gradients(
    adj, hpp, gu_ref, gcoef_ref, lag_ref, up_ref, gmp_ref, coef_ref, table_ref, x_ref
):
    tokens, channels = up_ref.shape
    up, gmp, coef = up_ref[...], gmp_ref[...], coef_ref[...]
    adjp = table_ref[ATOT : ATOT + 1, :] * adj
    rows, h_rows = adjoint_rows(adj, table_ref), state_rows(hpp)
    gcoef = coef_total(rows, h_rows, gcoef_ref, up, gmp)
    dw = mm(gcoef, x_ref[0], TN)
    v = mm(coef, rows, NN)
    ch = mm(coef, h_rows, NN)
    place = column(tokens)
    up_f, gmp_f = up.astype(F32), gmp.astype(F32)
    lag = (
        lag_ref[...]
        + jnp.sum(gmp_f * ((place + 1.0) * ch), axis=0, keepdims=True)
        + jnp.sum(up_f * ((tokens - 1.0 - place) * v), axis=0, keepdims=True)
        + tokens * jnp.sum(hpp * adjp, axis=0, keepdims=True)
    )
    total = jnp.sum(up_f * (gu_ref[...] + v), axis=0, keepdims=True)
    rate_row = total * table_ref[INV : INV + 1, :] - lag
    red = jnp.concatenate([dw, jnp.broadcast_to(rate_row, (8, channels))], axis=0)
    return red, rows, gcoef


def first_kernel(
    seq_size,
    up_ref,
    gmp_ref,
    coef_ref,
    table_ref,
    sa_ref,
    w_in_ref,
    w_bc_ref,
    gu_ref,
    gcoef_ref,
    g_ref,
    *refs,
):
    recv_refs, (keep_ref, send_ref, adj_ref, hpp_ref, weight_ref) = (
        refs[: seq_size - 1],
        refs[seq_size - 1 :],
    )
    tokens = up_ref.shape[0]
    states = coef_ref.shape[1] // 2
    recv_refs = recv_refs[::-1]
    h_in, adj, weights = unpack(seq_size, recv_refs, table_ref, states, tokens)
    hpp = table_ref[EMID : EMID + 1, :] * h_in
    hpp_ref[...] = hpp
    for k, weight in enumerate(weights):
        weight_ref[k : k + 1, :] = weight
    adj_ref[...] = adj
    rows = adjoint_rows(adj, table_ref)
    gcoef = coef_total(rows, state_rows(hpp), gcoef_ref, up_ref[...], gmp_ref[...])
    back = input_gradient(rows, gu_ref[...], gcoef, coef_ref[...], sa_ref, w_in_ref, w_bc_ref)
    store_split(back, g_ref[...], keep_ref, send_ref)


def store_split(back, g, keep_ref, send_ref):
    keep, send = split(back)
    keep_ref[...] = keep + split(g)[0].astype(F32)
    send_ref[...] = send.astype(BF16)


def gather_adjoint(recv_refs, weight_ref):
    adj = None
    for k, r in enumerate(recv_refs):
        term = weight_ref[k : k + 1, :] * r[...].astype(F32)
        adj = term if adj is None else adj + term
    return adj


def first_parameter_kernel(
    up_ref,
    gmp_ref,
    coef_ref,
    table_ref,
    x_ref,
    gu_ref,
    gcoef_ref,
    lag_ref,
    hpp_ref,
    adj_ref,
    red_ref,
):
    red_ref[...] = parameter_gradients(
        adj_ref[...],
        hpp_ref[...],
        gu_ref,
        gcoef_ref,
        lag_ref,
        up_ref,
        gmp_ref,
        coef_ref,
        table_ref,
        x_ref,
    )[0]


def parameter_kernel(
    last,
    seq_size,
    up_ref,
    gmp_ref,
    coef_ref,
    table_ref,
    x_ref,
    gu_ref,
    gcoef_in_ref,
    lag_ref,
    hpp_ref,
    weight_ref,
    kept_ref,
    *refs,
):
    recv_refs, (rows_ref, gcoef_ref, *out_refs) = refs[: seq_size - 1], refs[seq_size - 1 :]
    red, rows_ref[...], gcoef_ref[...] = parameter_gradients(
        gather_adjoint(recv_refs, weight_ref),
        hpp_ref[...],
        gu_ref,
        gcoef_in_ref,
        lag_ref,
        up_ref,
        gmp_ref,
        coef_ref,
        table_ref,
        x_ref,
    )
    if not last:
        out_refs[0][...] = red
        return
    red = jnp.where(lax.axis_index("section") == 0, red, kept_ref[...])
    keep_ref, send_ref = out_refs
    coefs = red.shape[0] - 8
    half = red.shape[1] // 2
    keep, send = split(red[:coefs, :])
    send_ref[...] = send.astype(BF16)
    keep_ref[:coefs, :] = keep
    rate = red[coefs:, :]
    keep_ref[coefs : coefs + 1, :] = rate[:1, :half]
    keep_ref[coefs + 1 : coefs + 2, :] = rate[:1, half:]
    keep_ref[coefs + 2 :, :] = jnp.zeros((6, half), F32)


def middle_input_kernel(
    rows_ref, gu_ref, gcoef_ref, coef_ref, sa_ref, w_in_ref, w_bc_ref, mine_ref, other_ref, keep_ref, send_ref
):
    back = input_gradient(
        rows_ref[...], gu_ref[...], gcoef_ref[...], coef_ref[...], sa_ref, w_in_ref, w_bc_ref
    )
    store_split(back, joined(mine_ref[...], other_ref[...]), keep_ref, send_ref)


def last_input_kernel(
    rows_ref, gu_ref, gcoef_ref, coef_ref, sa_ref, w_in_ref, w_bc_ref, kept_ref, part_ref
):
    back = input_gradient(
        rows_ref[...], gu_ref[...], gcoef_ref[...], coef_ref[...], sa_ref, w_in_ref, w_bc_ref
    )
    half = kept_ref[...]
    zero = jnp.zeros_like(half)
    low = lax.axis_index("mp") == 0
    done = jnp.concatenate([jnp.where(low, half, zero), jnp.where(low, zero, half)], axis=1)
    part_ref[...] = jnp.where(lax.axis_index("section") == 0, back.astype(BF16), done)


def scaled_gradient(g, w_out_ref, coef, a_ref, table_ref):
    gmp = (a_ref[...] * mm(g, w_out_ref[0], NT)).astype(BF16)
    states = coef.shape[1] // 2
    adjoint = table_ref[EMID : EMID + 1, :] * mm(coef, gmp, TN)[states:, :]
    return gmp, adjoint


def hop_kernel(
    w_out_ref, coef_ref, a_ref, table_ref, mine_ref, other_ref, gmp_ref, adjoint_ref
):
    g = joined(mine_ref[...], other_ref[...])
    gmp, adjoint = scaled_gradient(g, w_out_ref, coef_ref[...], a_ref, table_ref)
    gmp_ref[...] = gmp
    adjoint_ref[...] = adjoint.astype(BF16)


def pair_kernel(keep_ref, other_ref, sum_ref):
    coefs = other_ref.shape[0]
    sum_ref[:coefs, :] = (keep_ref[:coefs, :] + other_ref[...].astype(F32)).astype(BF16)
    sum_ref[coefs:, :] = keep_ref[coefs:, :].astype(BF16)


def total_kernel(seq_size, *refs):
    pieces, (w_ref, rate_ref) = refs[:seq_size], refs[seq_size:]
    heads = rate_ref.shape[1]
    terms = [r[...].astype(F32) for r in pieces]
    while len(terms) > 1:
        terms = [x + y for x, y in zip(terms[::2], terms[1::2])]
    total = terms[0]
    coefs, half = w_ref.shape
    channels = 2 * half
    w_ref[...] = total[:coefs, :]
    row = jnp.concatenate([total[coefs : coefs + 1, :], total[coefs + 1 : coefs + 2, :]], axis=1)
    lane = lax.broadcasted_iota(jnp.int32, (heads, channels), 1) // (channels // heads)
    head = lax.broadcasted_iota(jnp.int32, (heads, channels), 0)
    col = jnp.sum(jnp.where(lane == head, row, 0.0), axis=1, keepdims=True)
    i = lax.broadcasted_iota(jnp.int32, (heads, heads), 0)
    j = lax.broadcasted_iota(jnp.int32, (heads, heads), 1)
    rate_ref[...] = jnp.sum(jnp.where(i == j, col, 0.0), axis=0, keepdims=True)


def output_kernel(part_ref, part2_ref, mine_ref, other_ref, out_ref):
    active = lax.axis_index("section") == 0
    g = jnp.where(active, joined(mine_ref[...], other_ref[...]).astype(F32), 0.0)
    out_ref[0] = (g + (part_ref[...].astype(F32) + part2_ref[...].astype(F32))).astype(BF16)


def join_kernel(mine_ref, other_ref, out_ref):
    out_ref[0] = joined(mine_ref[...], other_ref[...])


def shards(section_inputs, cotangent, w_in, w_bc, w_out, decay_rates, resets):
    tokens, width = cotangent.shape
    channels = w_in.shape[2]
    coefs = w_bc.shape[2]
    w_bc = jnp.swapaxes(w_bc, 1, 2)
    states = coefs // 2
    heads = decay_rates.shape[1]
    seq_size = lax.axis_size("seq")
    sections = lax.axis_size("section")
    others = seq_size - 1
    big = 2 * tokens * width * channels
    vec, low = ((tokens, channels), F32), ((tokens, channels), BF16)
    row = ((1, channels), F32)
    few = ((tokens, coefs), F32)
    reduced = ((coefs + 8, channels), F32)

    up, gmp, coef, a, sa, table, *pay = call(
        functools.partial(start_kernel, seq_size),
        [low, low, ((tokens, coefs), BF16), vec, vec, ((TABLE_ROWS, channels), F32)]
        + [((states, channels + 128), BF16)] * others,
        [
            section_inputs,
            cotangent,
            w_in,
            w_bc,
            w_out,
            decay_rates,
            resets.reshape(1, tokens),
        ],
        space=pltpu.HBM,
        scratch=[
            pltpu.VMEM((tokens, width), BF16),
            pltpu.VMEM((tokens, width), BF16),
            pltpu.VMEM((width, channels), BF16),
            pltpu.VMEM((coefs, width), BF16),
            pltpu.VMEM((channels, width), BF16),
            pltpu.SMEM((1, heads), F32),
            pltpu.VMEM((1, tokens), jnp.int32),
            pltpu.SemaphoreType.DMA((5,)),
            pltpu.SemaphoreType.DMA((OUT_CHUNKS + IN_CHUNKS,)),
        ],
        flops=2 * big,
        bytes_accessed=4 * width * channels,
        name="start",
    )
    recv = [partner(pay[k - 1], "seq", k) for k in range(1, seq_size)]

    def local(gradient):
        return call(
            local_kernel,
            [vec, few, row],
            [up, gradient, coef],
            flops=big,
            bytes_accessed=4 * tokens * channels,
            name="local",
        )

    gu, gcoef, lag = local(gmp)
    state = ((states, channels), F32)
    half = width // 2
    halves = [((tokens, half), F32), ((tokens, half), BF16)]
    keep, send, adj, hpp, weight = call(
        functools.partial(first_kernel, seq_size),
        [*halves, state, state, ((others, channels), F32)],
        [up, gmp, coef, table, sa, w_in, w_bc, gu, gcoef, cotangent, *recv[::-1]],
        flops=big,
        bytes_accessed=2 * width * channels,
        name="first",
    )
    (red,) = call(
        first_parameter_kernel,
        [reduced],
        [up, gmp, coef, table, section_inputs, gu, gcoef, lag, hpp, adj],
        flops=big // 4,
        bytes_accessed=4 * tokens * channels,
        name="first_parameters",
    )
    section = lax.axis_index("section")
    kept, kept_red = None, red
    for moment in range(1, sections):
        result = (keep + swap(send, "mp").astype(F32)).astype(BF16)
        if kept is None:
            kept = result
        else:
            was_active = section == sections - moment
            kept = jnp.where(was_active, result, kept)
            kept_red = jnp.where(was_active, red, kept_red)
        mine = rotate(result, "section", -1)
        other = swap(mine, "mp")
        gmp, adjoint = call(
            hop_kernel,
            [low, ((states, channels), BF16)],
            [w_out, coef, a, table, mine, other],
            flops=big,
            bytes_accessed=2 * width * channels,
            name="hop",
        )
        recv = [partner(adjoint, "seq", k) for k in range(1, seq_size)]
        gu, gcoef, lag = local(gmp)
        last = moment == sections - 1
        rows, gcoef, *red = call(
            functools.partial(parameter_kernel, last, seq_size),
            [((coefs, channels), BF16), ((tokens, coefs), BF16)]
            + ([((coefs + 8, half), F32), ((coefs, half), BF16)] if last else [reduced]),
            [up, gmp, coef, table, section_inputs, gu, gcoef, lag, hpp, weight, kept_red, *recv],
            flops=big // 4,
            bytes_accessed=4 * tokens * channels,
            name="parameters",
        )
        if not last:
            (red,) = red
            keep, send = call(
                middle_input_kernel,
                halves,
                [rows, gu, gcoef, coef, sa, w_in, w_bc, mine, other],
                flops=big,
                bytes_accessed=2 * width * channels,
                name="middle_input",
            )
    (red,) = call(
        pair_kernel, [((coefs + 8, half), BF16)], [red[0], swap(red[1], "mp")], name="pair"
    )
    rows, red = lax.optimization_barrier((rows, red))
    (part,) = call(
        last_input_kernel,
        [low],
        [rows, gu, gcoef, coef, sa, w_in, w_bc, kept],
        flops=big,
        bytes_accessed=2 * width * channels,
        name="last_input",
    )
    (out,) = call(
        output_kernel,
        [((1, tokens, width), BF16)],
        [part, swap(part, "mp"), mine, other],
        name="output",
    )
    pieces = [partner(red, "seq", k) for k in range(1, seq_size)]
    red, out = lax.optimization_barrier((red, out))
    grad_w, grad_rates = call(
        functools.partial(total_kernel, seq_size),
        [((coefs, half), F32), ((1, heads), F32)],
        [red, *pieces],
        name="total",
    )
    (grad_w,) = call(
        join_kernel, [((1, coefs, width), F32)], [grad_w, swap(grad_w, "mp")], name="join"
    )
    return out, jnp.swapaxes(grad_w, 1, 2), grad_rates


def solution(mesh):
    return jax.shard_map(
        shards,
        mesh=mesh,
        in_specs=(
            P("section", ("groups", "seq"), None),
            P(("groups", "seq"), None),
            P("section", None, "mp"),
            P("section", None, None),
            P("section", "mp", None),
            P("section", "mp"),
            P(("groups", "seq")),
        ),
        out_specs=(
            P("section", ("groups", "seq"), None),
            P("section", "groups", None),
            P("section", ("groups", "mp")),
        ),
        check_vma=False,
    )
```

time: 50.4 us -> 42.6 us (0.85)
  local copies, waits for them, and re-layouts: 7.47 us -> 0.03 us
  Pallas kernels: 7.09 us -> 10.7 us
  waiting for transfers between devices: 17.9 us -> 14.4 us
  other arithmetic: 0.65 us -> 0.03 us
    ppermute x0 -> x9, starting transfers between devices: none -> 14.6 us  [partner(): return lax.ppermute(value, axis, [(i, i ^ k) for i in range(n)])]
    ppermute x14 -> x6, starting transfers between devices: 16.2 us -> 1.93 us  [rotate(): return lax.ppermute(value, axis, [(i, (i + by) % n) for i in range(n)])]
    ppermute x14 -> x6, waiting for transfers between devices: 17.9 us -> 8.36 us  [rotate(): return lax.ppermute(value, axis, [(i, (i + by) % n) for i in range(n)])]
    unnamed x22 -> x10, local copies, waits for them, and re-layouts: 7.47 us -> 0.03 us
    ppermute x0 -> x9, waiting for transfers between devices: none -> 6.05 us  [partner(): return lax.ppermute(value, axis, [(i, i ^ k) for i in range(n)])]
    pallas_call x8 -> x12, Pallas kernels: 7.09 us -> 10.7 us  [call(): pl.pallas_call(kernel, out_shape=[jax.ShapeDtypeStruct(s, d) for s, d in...]
    pallas_call x1 -> x0, other arithmetic: 0.63 us -> none  [call(): pl.pallas_call(kernel, out_shape=[jax.ShapeDtypeStruct(s, d) for s, d in...]
  transfers between devices with their start and end apart: 14 -> 15, of which waited for: 10 -> 12; matrix products, arithmetic and copies ran while one was open for 0% -> 0% of each run, Pallas kernels for 3% -> 7%
where the time goes in v2:
time: 42.6 us; the launch traced here: 42.4 us
  starting transfers between devices  16.5 us (39%)
  waiting for transfers between devices  14.4 us (34%)
  Pallas kernels  10.7 us (25%)
  between operations  0.78 us (2%)
    ppermute x9, starting transfers between devices, partner(): return lax.ppermute(value, axis, [(i, i ^ k) for i in range(n)])  14.6 us
    pallas_call x12, Pallas kernels, call(): pl.pallas_call(kernel, out_shape=[jax.ShapeDtypeStruct(s, d) for s, d in...  10.7 us
    ppermute x6, waiting for transfers between devices, rotate(): return lax.ppermute(value, axis, [(i, (i + by) % n) for i in range(n)])  8.36 us
    ppermute x9, waiting for transfers between devices, partner(): return lax.ppermute(value, axis, [(i, i ^ k) for i in range(n)])  6.05 us
    ppermute x6, starting transfers between devices, rotate(): return lax.ppermute(value, axis, [(i, (i + by) % n) for i in range(n)])  1.93 us
  transfers between devices with their start and end apart: 15, of which 12 were waited for; matrix products, arithmetic and copies ran while one was open for 0% of the time, Pallas kernels for 7%

profile of v2, /device:TPU:0, one launch (start us, length us, event | category | flops | bytes accessed | tf_op | source)
XLA Modules:
  0.0 42.4 jit_solution(18199502426797788350)
XLA Ops:
  0.7 3.3 %start.1 = (bf16[128,768]{1,0:T(8,128)(2,1)S(1)}, bf16[128,768]{1,0:T(8,128)(2,1)S(1)}, bf16[128,32]{1,0:T(8,128)(2,1)S(1)}, f32[128,768]{1,0:T(8,128)S(1)}, f32...) custom-call(bf16[1,128,768]{2,1,0:T(8,128)(2,1)} %x_ref.3, ...), custom_call_target="tpu_custom_call" | custom-call | flops 301989888 | bytes 2359296 | tf_op jit(solution)/shard_map/start/pallas_call | solution.py:59
  3.9 5.1 %collective-permute-start = (bf16[16,896]{1,0:T(8,128)(2,1)S(1)}, bf16[16,896]{1,0:T(8,128)(2,1)S(1)}, u32[]{:S(2)}, u32[]{:S(2)}) collective-permute-start(bf16[16,896]{1,0:T(8,128)(2,1)S(1)} %get-tuple-element.43), channel_id=1, source_target_pairs={{0,12},{4,8},{8,4},{12,0},{1,13},{5,9},{9,5},{13,1},{2,14},{6,10},... | collective-permute-start | bytes 86024 | tf_op jit(solution)/shard_map/ppermute | solution.py:35
  9.0 0.6 %collective-permute-start.2 = (bf16[16,896]{1,0:T(8,128)(2,1)S(1)}, bf16[16,896]{1,0:T(8,128)(2,1)S(1)}, u32[]{:S(2)}, u32[]{:S(2)}) collective-permute-start(bf16[16,896]{1,0:T(8,128)(2,1)S(1)} %get-tuple-element.45), channel_id=1, source_target_pairs={{0,4},{4,0},{8,12},{12,8},{1,5},{5,1},{9,13},{13,9},{2,6},{6,2},{1... | collective-permute-start | bytes 86024 | tf_op jit(solution)/shard_map/ppermute | solution.py:35
  9.7 0.8 %local.2 = (f32[128,768]{1,0:T(8,128)S(1)}, f32[128,32]{1,0:T(8,128)S(1)}, f32[1,768]{1,0:T(1,128)S(1)}) custom-call(bf16[128,768]{1,0:T(8,128)(2,1)S(1)} %get-tuple-element.35.up_ref, bf16[128,768]{1,0:T(8,128)(2,1)S(1)} %get-tuple-element.39.gmp_ref, bf16[128,32]{1,0:T(8,128)(2,1)S(1)} %get-tuple-element.36.coef_ref), custom_call_target="tpu_custom_call" | custom-call | flops 150994944 | bytes 393216 | tf_op jit(solution)/shard_map/local/pallas_call | solution.py:59
  10.9 2.9 %collective-permute-done.1.refs_1_ = bf16[16,896]{1,0:T(8,128)(2,1)S(1)} collective-permute-done((bf16[16,896]{1,0:T(8,128)(2,1)S(1)}, bf16[16,896]{1,0:T(8,128)(2,1)S(1)}, u32[]{:S(2)}, u32[]{:S(2)}) %collective-permute-start.1) | collective-permute-done | bytes 28704 | tf_op jit(solution)/shard_map/ppermute | solution.py:35
  13.8 1.0 %first.1 = (f32[128,384]{1,0:T(8,128)S(1)}, bf16[128,384]{1,0:T(8,128)(2,1)S(1)}, f32[16,768]{1,0:T(8,128)S(1)}, f32[16,768]{1,0:T(8,128)S(1)}, f32[3,768]{1,0:T(4,128)S(1)}) custom-call(bf16[128,768]{1,0:T(8,128)(2,1)S(1)} %get-tuple-element.35.up_ref, bf16[128,768]{1,0:T(8,128)(2,1)S(1)} %get-tuple-element.39.gmp_ref, ...), custom_call_target="tpu_custom_call" | custom-call | flops 150994944 | bytes 1179648 | tf_op jit(solution)/shard_map/first/pallas_call | solution.py:59
  14.9 1.3 %collective-permute-done.3 = bf16[128,384]{1,0:T(8,128)(2,1)S(1)} collective-permute-done((bf16[128,384]{1,0:T(8,128)(2,1)S(1)}, bf16[128,384]{1,0:T(8,128)(2,1)S(1)}, u32[]{:S(2)}, u32[]{:S(2)}) %collective-permute-start.3) | collective-permute-done | bytes 98336 | tf_op jit(solution)/shard_map/ppermute | solution.py:30
  16.3 1.6 %collective-permute-start.4 = (bf16[128,384]{1,0:T(8,128)(2,1)S(1)}, bf16[128,384]{1,0:T(8,128)(2,1)S(1)}, u32[]{:S(2)}, u32[]{:S(2)}) collective-permute-start(bf16[128,384]{1,0:T(8,128)(2,1)S(1)} %add_convert_fusion.kept_ref), channel_id=1, source_target_pairs={{0,2},{2,0},{1,3},{3,1},{4,6},{6,4},{5,7},{7,5},{8,10},{10,8},{9,1... | collective-permute-start | bytes 294920 | tf_op jit(solution)/shard_map/ppermute | solution.py:30
  17.8 3.4 %collective-permute-done.4.mine_ref = bf16[128,384]{1,0:T(8,128)(2,1)S(1)} collective-permute-done((bf16[128,384]{1,0:T(8,128)(2,1)S(1)}, bf16[128,384]{1,0:T(8,128)(2,1)S(1)}, u32[]{:S(2)}, u32[]{:S(2)}) %collective-permute-start.4) | collective-permute-done | bytes 98336 | tf_op jit(solution)/shard_map/ppermute | solution.py:30
  21.2 1.3 %collective-permute-done.5.other_ref = bf16[128,384]{1,0:T(8,128)(2,1)S(1)} collective-permute-done((bf16[128,384]{1,0:T(8,128)(2,1)S(1)}, bf16[128,384]{1,0:T(8,128)(2,1)S(1)}, u32[]{:S(2)}, u32[]{:S(2)}) %collective-permute-start.5) | collective-permute-done | bytes 98336 | tf_op jit(solution)/shard_map/ppermute | solution.py:30
  23.1 1.5 %collective-permute-start.8 = (bf16[16,768]{1,0:T(8,128)(2,1)S(1)}, bf16[16,768]{1,0:T(8,128)(2,1)S(1)}, u32[]{:S(2)}, u32[]{:S(2)}) collective-permute-start(bf16[16,768]{1,0:T(8,128)(2,1)S(1)} %get-tuple-element.56), channel_id=1, source_target_pairs={{0,12},{4,8},{8,4},{12,0},{1,13},{5,9},{9,5},{13,1},{2,14},{6,10},... | collective-permute-start | bytes 73736 | tf_op jit(solution)/shard_map/ppermute | solution.py:35
  25.2 2.3 %collective-permute-start.6 = (bf16[16,768]{1,0:T(8,128)(2,1)S(1)}, bf16[16,768]{1,0:T(8,128)(2,1)S(1)}, u32[]{:S(2)}, u32[]{:S(2)}) collective-permute-start(bf16[16,768]{1,0:T(8,128)(2,1)S(1)} %get-tuple-element.56), channel_id=1, source_target_pairs={{0,4},{4,0},{8,12},{12,8},{1,5},{5,1},{9,13},{13,9},{2,6},{6,2},{1... | collective-permute-start | bytes 73736 | tf_op jit(solution)/shard_map/ppermute | solution.py:35
  27.6 0.7 %first_parameters.1.kept_ref = f32[40,768]{1,0:T(8,128)S(1)} custom-call(bf16[128,768]{1,0:T(8,128)(2,1)S(1)} %get-tuple-element.35.up_ref, bf16[128,768]{1,0:T(8,128)(2,1)S(1)} %get-tuple-element.39.gmp_ref, bf16[128,32]{1,0:T(8,128)(2,1)S(1)} %get-tuple-element.36.coef_ref, f32[8,768]{1,0:T(8,128)S(1)} %get-tuple-element.38.table_ref, ...), custom_call_target="tpu_custom_call" | custom-call | flops 37748736 | bytes 393216 | tf_op jit(solution)/shard_map/first_parameters/pallas_call | solution.py:59
  28.3 0.8 %local.3 = (f32[128,768]{1,0:T(8,128)S(1)}, f32[128,32]{1,0:T(8,128)S(1)}, f32[1,768]{1,0:T(1,128)S(1)}) custom-call(bf16[128,768]{1,0:T(8,128)(2,1)S(1)} %get-tuple-element.35.up_ref, bf16[128,768]{1,0:T(8,128)(2,1)S(1)} %get-tuple-element.48.gmp_ref, bf16[128,32]{1,0:T(8,128)(2,1)S(1)} %get-tuple-element.36.coef_ref), custom_call_target="tpu_custom_call" | custom-call | flops 150994944 | bytes 393216 | tf_op jit(solution)/shard_map/local/pallas_call | solution.py:59
  29.6 0.7 %parameters.1 = (bf16[32,768]{1,0:T(8,128)(2,1)S(1)}, bf16[128,32]{1,0:T(8,128)(2,1)S(1)}, f32[40,384]{1,0:T(8,128)S(1)}, bf16[32,384]{1,0:T(8,128)(2,1)S(1)}) custom-call(bf16[128,768]{1,0:T(8,128)(2,1)S(1)} %get-tuple-element.35.up_ref, bf16[128,768]{1,0:T(8,128)(2,1)S(1)} %get-tuple-element.48.gmp_ref, bf16[128,32]{1,0:T(8,128)(2,1)S(1)} %get-tuple-element.36.coef_ref, ...), custom_call_target="tpu_custom_call" | custom-call | flops 37748736 | bytes 393216 | tf_op jit(solution)/shard_map/parameters/pallas_call | solution.py:59
  30.4 1.2 %collective-permute-done.9.other_ref = bf16[32,384]{1,0:T(8,128)(2,1)S(1)} collective-permute-done((bf16[32,384]{1,0:T(8,128)(2,1)S(1)}, bf16[32,384]{1,0:T(8,128)(2,1)S(1)}, u32[]{:S(2)}, u32[]{:S(2)}) %collective-permute-start.9) | collective-permute-done | bytes 24608 | tf_op jit(solution)/shard_map/ppermute | solution.py:30
  32.5 2.4 %collective-permute-start.13 = (bf16[40,384]{1,0:T(8,128)(2,1)S(1)}, bf16[40,384]{1,0:T(8,128)(2,1)S(1)}, u32[]{:S(2)}, u32[]{:S(2)}) collective-permute-start(bf16[40,384]{1,0:T(8,128)(2,1)S(1)} %pair.1.refs_0_), channel_id=1, source_target_pairs={{0,12},{4,8},{8,4},{12,0},{1,13},{5,9},{9,5},{13,1},{2,14},{6,10},... | collective-permute-start | bytes 92168 | tf_op jit(solution)/shard_map/ppermute | solution.py:35
  34.8 0.9 %collective-permute-start.12 = (bf16[40,384]{1,0:T(8,128)(2,1)S(1)}, bf16[40,384]{1,0:T(8,128)(2,1)S(1)}, u32[]{:S(2)}, u32[]{:S(2)}) collective-permute-start(bf16[40,384]{1,0:T(8,128)(2,1)S(1)} %pair.1.refs_0_), channel_id=1, source_target_pairs={{0,8},{4,12},{8,0},{12,4},{1,9},{5,13},{9,1},{13,5},{2,10},{6,14},... | collective-permute-start | bytes 92168 | tf_op jit(solution)/shard_map/ppermute | solution.py:35
  35.7 1.1 %collective-permute-start.11 = (bf16[40,384]{1,0:T(8,128)(2,1)S(1)}, bf16[40,384]{1,0:T(8,128)(2,1)S(1)}, u32[]{:S(2)}, u32[]{:S(2)}) collective-permute-start(bf16[40,384]{1,0:T(8,128)(2,1)S(1)} %pair.1.refs_0_), channel_id=1, source_target_pairs={{0,4},{4,0},{8,12},{12,8},{1,5},{5,1},{9,13},{13,9},{2,6},{6,2},{1... | collective-permute-start | bytes 92168 | tf_op jit(solution)/shard_map/ppermute | solution.py:35
  36.9 0.8 %output.1 = bf16[1,128,768]{2,1,0:T(8,128)(2,1)} custom-call(bf16[128,768]{1,0:T(8,128)(2,1)S(1)} %last_input.1.part_ref, bf16[128,768]{1,0:T(8,128)(2,1)S(1)} %collective-permute-done.10.part2_ref, bf16[128,384]{1,0:T(8,128)(2,1)S(1)} %collective-permute-done.4.mine_ref, bf16[128,384]{1,0:T(8,128)(2,1)S(1)} %collective-permute-done.5.other_ref), custom_call_target="tpu_custom_call" | custom-call | tf_op jit(solution)/shard_map/output/pallas_call | solution.py:59
  37.6 1.0 %collective-permute-done.13.refs_3_ = bf16[40,384]{1,0:T(8,128)(2,1)S(1)} collective-permute-done((bf16[40,384]{1,0:T(8,128)(2,1)S(1)}, bf16[40,384]{1,0:T(8,128)(2,1)S(1)}, u32[]{:S(2)}, u32[]{:S(2)}) %collective-permute-start.13) | collective-permute-done | bytes 30752 | tf_op jit(solution)/shard_map/ppermute | solution.py:35
  38.6 1.1 %collective-permute-done.12.refs_2_ = bf16[40,384]{1,0:T(8,128)(2,1)S(1)} collective-permute-done((bf16[40,384]{1,0:T(8,128)(2,1)S(1)}, bf16[40,384]{1,0:T(8,128)(2,1)S(1)}, u32[]{:S(2)}, u32[]{:S(2)}) %collective-permute-start.12) | collective-permute-done | bytes 30752 | tf_op jit(solution)/shard_map/ppermute | solution.py:35
  40.5 1.2 %collective-permute-done.14.other_ref = f32[32,384]{1,0:T(8,128)S(1)} collective-permute-done((f32[32,384]{1,0:T(8,128)S(1)}, f32[32,384]{1,0:T(8,128)S(1)}, u32[]{:S(2)}, u32[]{:S(2)}) %collective-permute-start.14) | collective-permute-done | bytes 49184 | tf_op jit(solution)/shard_map/ppermute | solution.py:30
  41.8 0.7 %join.1 = f32[1,32,768]{2,1,0:T(8,128)} custom-call(f32[32,384]{1,0:T(8,128)S(1)} %get-tuple-element.65.mine_ref, f32[32,384]{1,0:T(8,128)S(1)} %collective-permute-done.14.other_ref), custom_call_target="tpu_custom_call" | custom-call | tf_op jit(solution)/shard_map/join/pallas_call | solution.py:59
  (29 shorter events, 4.0 us)
Async XLA Ops:
  0.6 13.2 %copy-start = (bf16[1,768,768]{2,1,0:T(8,128)(2,1)S(1)}, bf16[1,768,768]{2,1,0:T(8,128)(2,1)}, u32[]{:S(2)}) copy-start(bf16[1,768,768]{2,1,0:T(8,128)(2,1)} %w_in_ref.3) | copy-start | bytes 3538948
  0.6 13.2 %copy-start.3 = (bf16[128,768]{1,0:T(8,128)(2,1)S(1)}, bf16[128,768]{1,0:T(8,128)(2,1)}, u32[]{:S(2)}) copy-start(bf16[128,768]{1,0:T(8,128)(2,1)} %g_ref.1) | copy-start | bytes 589828
  0.7 13.2 %copy-start.4 = (bf16[1,768,32]{1,2,0:T(8,128)(2,1)S(1)}, bf16[1,768,32]{1,2,0:T(8,128)(2,1)}, u32[]{:S(2)}) copy-start(bf16[1,768,32]{1,2,0:T(8,128)(2,1)} %param.10) | copy-start | bytes 147460
  3.9 7.0 %collective-permute-start = (bf16[16,896]{1,0:T(8,128)(2,1)S(1)}, bf16[16,896]{1,0:T(8,128)(2,1)S(1)}, u32[]{:S(2)}, u32[]{:S(2)}) collective-permute-start(bf16[16,896]{1,0:T(8,128)(2,1)S(1)} %get-tuple-element.43), channel_id=1, source_target_pairs={{0,12},{4,8},{8,4},{12,0},{1,13},{5,9},{9,5},{13,1},{2,14},{6,10},... | collective-permute-start | bytes 86024 | tf_op jit(solution)/shard_map/ppermute | solution.py:35
  9.0 4.8 %collective-permute-start.1 = (bf16[16,896]{1,0:T(8,128)(2,1)S(1)}, bf16[16,896]{1,0:T(8,128)(2,1)S(1)}, u32[]{:S(2)}, u32[]{:S(2)}) collective-permute-start(bf16[16,896]{1,0:T(8,128)(2,1)S(1)} %get-tuple-element.44), channel_id=1, source_target_pairs={{0,8},{4,12},{8,0},{12,4},{1,9},{5,13},{9,1},{13,5},{2,10},{6,14},... | collective-permute-start | bytes 86024 | tf_op jit(solution)/shard_map/ppermute | solution.py:35
  9.0 4.8 %collective-permute-start.2 = (bf16[16,896]{1,0:T(8,128)(2,1)S(1)}, bf16[16,896]{1,0:T(8,128)(2,1)S(1)}, u32[]{:S(2)}, u32[]{:S(2)}) collective-permute-start(bf16[16,896]{1,0:T(8,128)(2,1)S(1)} %get-tuple-element.45), channel_id=1, source_target_pairs={{0,4},{4,0},{8,12},{12,8},{1,5},{5,1},{9,13},{13,9},{2,6},{6,2},{1... | collective-permute-start | bytes 86024 | tf_op jit(solution)/shard_map/ppermute | solution.py:35
  13.8 8.7 %copy-start.1 = (bf16[1,768,768]{2,1,0:T(8,128)(2,1)S(1)}, bf16[1,768,768]{2,1,0:T(8,128)(2,1)}, u32[]{:S(2)}) copy-start(bf16[1,768,768]{2,1,0:T(8,128)(2,1)} %w_out_ref.1) | copy-start | bytes 3538948
  14.9 12.7 %copy-start.2 = (bf16[1,128,768]{2,1,0:T(8,128)(2,1)S(1)}, bf16[1,128,768]{2,1,0:T(8,128)(2,1)}, u32[]{:S(2)}) copy-start(bf16[1,128,768]{2,1,0:T(8,128)(2,1)} %x_ref.3) | copy-start | bytes 589828
  14.9 1.4 %collective-permute-start.3 = (bf16[128,384]{1,0:T(8,128)(2,1)S(1)}, bf16[128,384]{1,0:T(8,128)(2,1)S(1)}, u32[]{:S(2)}, u32[]{:S(2)}) collective-permute-start(bf16[128,384]{1,0:T(8,128)(2,1)S(1)} %get-tuple-element.47), channel_id=1, source_target_pairs={{0,1},{1,0},{2,3},{3,2},{4,5},{5,4},{6,7},{7,6},{8,9},{9,8},{10,11... | collective-permute-start | bytes 294920 | tf_op jit(solution)/shard_map/ppermute | solution.py:30
  16.3 4.9 %collective-permute-start.4 = (bf16[128,384]{1,0:T(8,128)(2,1)S(1)}, bf16[128,384]{1,0:T(8,128)(2,1)S(1)}, u32[]{:S(2)}, u32[]{:S(2)}) collective-permute-start(bf16[128,384]{1,0:T(8,128)(2,1)S(1)} %add_convert_fusion.kept_ref), channel_id=1, source_target_pairs={{0,2},{2,0},{1,3},{3,1},{4,6},{6,4},{5,7},{7,5},{8,10},{10,8},{9,1... | collective-permute-start | bytes 294920 | tf_op jit(solution)/shard_map/ppermute | solution.py:30
  21.2 1.3 %collective-permute-start.5 = (bf16[128,384]{1,0:T(8,128)(2,1)S(1)}, bf16[128,384]{1,0:T(8,128)(2,1)S(1)}, u32[]{:S(2)}, u32[]{:S(2)}) collective-permute-start(bf16[128,384]{1,0:T(8,128)(2,1)S(1)} %collective-permute-done.4.mine_ref), channel_id=1, source_target_pairs={{0,1},{1,0},{2,3},{3,2},{4,5},{5,4},{6,7},{7,6},{8,9},{9,8},{10,11... | collective-permute-start | bytes 294920 | tf_op jit(solution)/shard_map/ppermute | solution.py:30
  23.1 6.0 %collective-permute-start.8 = (bf16[16,768]{1,0:T(8,128)(2,1)S(1)}, bf16[16,768]{1,0:T(8,128)(2,1)S(1)}, u32[]{:S(2)}, u32[]{:S(2)}) collective-permute-start(bf16[16,768]{1,0:T(8,128)(2,1)S(1)} %get-tuple-element.56), channel_id=1, source_target_pairs={{0,12},{4,8},{8,4},{12,0},{1,13},{5,9},{9,5},{13,1},{2,14},{6,10},... | collective-permute-start | bytes 73736 | tf_op jit(solution)/shard_map/ppermute | solution.py:35
  24.6 4.7 %collective-permute-start.7 = (bf16[16,768]{1,0:T(8,128)(2,1)S(1)}, bf16[16,768]{1,0:T(8,128)(2,1)S(1)}, u32[]{:S(2)}, u32[]{:S(2)}) collective-permute-start(bf16[16,768]{1,0:T(8,128)(2,1)S(1)} %get-tuple-element.56), channel_id=1, source_target_pairs={{0,8},{4,12},{8,0},{12,4},{1,9},{5,13},{9,1},{13,5},{2,10},{6,14},... | collective-permute-start | bytes 73736 | tf_op jit(solution)/shard_map/ppermute | solution.py:35
  25.2 4.3 %collective-permute-start.6 = (bf16[16,768]{1,0:T(8,128)(2,1)S(1)}, bf16[16,768]{1,0:T(8,128)(2,1)S(1)}, u32[]{:S(2)}, u32[]{:S(2)}) collective-permute-start(bf16[16,768]{1,0:T(8,128)(2,1)S(1)} %get-tuple-element.56), channel_id=1, source_target_pairs={{0,4},{4,0},{8,12},{12,8},{1,5},{5,1},{9,13},{13,9},{2,6},{6,2},{1... | collective-permute-start | bytes 73736 | tf_op jit(solution)/shard_map/ppermute | solution.py:35
  30.3 1.3 %collective-permute-start.9 = (bf16[32,384]{1,0:T(8,128)(2,1)S(1)}, bf16[32,384]{1,0:T(8,128)(2,1)S(1)}, u32[]{:S(2)}, u32[]{:S(2)}) collective-permute-start(bf16[32,384]{1,0:T(8,128)(2,1)S(1)} %get-tuple-element.59), channel_id=1, source_target_pairs={{0,1},{1,0},{2,3},{3,2},{4,5},{5,4},{6,7},{7,6},{8,9},{9,8},{10,11... | collective-permute-start | bytes 73736 | tf_op jit(solution)/shard_map/ppermute | solution.py:30
  32.2 4.6 %collective-permute-start.10 = (bf16[128,768]{1,0:T(8,128)(2,1)S(1)}, bf16[128,768]{1,0:T(8,128)(2,1)S(1)}, u32[]{:S(2)}, u32[]{:S(2)}) collective-permute-start(bf16[128,768]{1,0:T(8,128)(2,1)S(1)} %last_input.1.part_ref), channel_id=1, source_target_pairs={{0,1},{1,0},{2,3},{3,2},{4,5},{5,4},{6,7},{7,6},{8,9},{9,8},{10,11... | collective-permute-start | bytes 589832 | tf_op jit(solution)/shard_map/ppermute | solution.py:30
  32.5 6.1 %collective-permute-start.13 = (bf16[40,384]{1,0:T(8,128)(2,1)S(1)}, bf16[40,384]{1,0:T(8,128)(2,1)S(1)}, u32[]{:S(2)}, u32[]{:S(2)}) collective-permute-start(bf16[40,384]{1,0:T(8,128)(2,1)S(1)} %pair.1.refs_0_), channel_id=1, source_target_pairs={{0,12},{4,8},{8,4},{12,0},{1,13},{5,9},{9,5},{13,1},{2,14},{6,10},... | collective-permute-start | bytes 92168 | tf_op jit(solution)/shard_map/ppermute | solution.py:35
  34.8 4.8 %collective-permute-start.12 = (bf16[40,384]{1,0:T(8,128)(2,1)S(1)}, bf16[40,384]{1,0:T(8,128)(2,1)S(1)}, u32[]{:S(2)}, u32[]{:S(2)}) collective-permute-start(bf16[40,384]{1,0:T(8,128)(2,1)S(1)} %pair.1.refs_0_), channel_id=1, source_target_pairs={{0,8},{4,12},{8,0},{12,4},{1,9},{5,13},{9,1},{13,5},{2,10},{6,14},... | collective-permute-start | bytes 92168 | tf_op jit(solution)/shard_map/ppermute | solution.py:35
  35.7 4.2 %collective-permute-start.11 = (bf16[40,384]{1,0:T(8,128)(2,1)S(1)}, bf16[40,384]{1,0:T(8,128)(2,1)S(1)}, u32[]{:S(2)}, u32[]{:S(2)}) collective-permute-start(bf16[40,384]{1,0:T(8,128)(2,1)S(1)} %pair.1.refs_0_), channel_id=1, source_target_pairs={{0,4},{4,0},{8,12},{12,8},{1,5},{5,1},{9,13},{13,9},{2,6},{6,2},{1... | collective-permute-start | bytes 92168 | tf_op jit(solution)/shard_map/ppermute | solution.py:35
  40.5 1.2 %collective-permute-start.14 = (f32[32,384]{1,0:T(8,128)S(1)}, f32[32,384]{1,0:T(8,128)S(1)}, u32[]{:S(2)}, u32[]{:S(2)}) collective-permute-start(f32[32,384]{1,0:T(8,128)S(1)} %get-tuple-element.65.mine_ref), channel_id=1, source_target_pairs={{0,1},{1,0},{2,3},{3,2},{4,5},{5,4},{6,7},{7,6},{8,9},{9,8},{10,11... | collective-permute-start | bytes 147464 | tf_op jit(solution)/shard_map/ppermute | solution.py:30

commit v3 on v2

--- a/solution.py
+++ b/solution.py
@@ -18,7 +18,12 @@
 
 RATE, EMID, ATOT, INV, COUNT = 0, 1, 2, 3, 4
 TABLE_ROWS = 8
-OUT_CHUNKS, IN_CHUNKS = 2, 2
+ORDERS = (
+    lambda n: range(n - 1, 0, -1),
+    lambda n: (1, *range(n - 1, 1, -1)),
+    lambda n: (1, *range(n - 1, 1, -1)),
+)
+OUT_CHUNKS, IN_CHUNKS = 1, 1
 
 
 def mm(a, b, dims):
@@ -209,7 +214,7 @@
     channels = table_ref.shape[1]
     rate = table_ref[RATE : RATE + 1, :]
     me = lax.axis_index("seq")
-    source = [me ^ k for k in range(1, seq_size)]
+    source = [me ^ k for k in ORDERS[0](seq_size)]
     data = [r[:, :channels].astype(F32) for r in recv_refs]
     gap = [
         r[:1, channels : channels + 1].astype(F32) * LOG_KEEP - tokens * rate for r in recv_refs
@@ -251,19 +256,14 @@
     return (gcoef_ref[...] + mm(gmp, h_rows, NT) + mm(up, rows, NT)).astype(BF16)
 
 
-def parameter_gradients(
-    adj, hpp, gu_ref, gcoef_ref, lag_ref, up_ref, gmp_ref, coef_ref, table_ref, x_ref
-):
-    tokens, channels = up_ref.shape
-    up, gmp, coef = up_ref[...], gmp_ref[...], coef_ref[...]
+def rate_gradients(adj, hpp, gu_ref, lag_ref, up_ref, gmp_ref, coef_ref, table_ref):
+    tokens = up_ref.shape[0]
+    coef = coef_ref[...]
     adjp = table_ref[ATOT : ATOT + 1, :] * adj
-    rows, h_rows = adjoint_rows(adj, table_ref), state_rows(hpp)
-    gcoef = coef_total(rows, h_rows, gcoef_ref, up, gmp)
-    dw = mm(gcoef, x_ref[0], TN)
-    v = mm(coef, rows, NN)
-    ch = mm(coef, h_rows, NN)
+    v = mm(coef, adjoint_rows(adj, table_ref), NN)
+    ch = mm(coef, state_rows(hpp), NN)
     place = column(tokens)
-    up_f, gmp_f = up.astype(F32), gmp.astype(F32)
+    up_f, gmp_f = up_ref[...].astype(F32), gmp_ref[...].astype(F32)
     lag = (
         lag_ref[...]
         + jnp.sum(gmp_f * ((place + 1.0) * ch), axis=0, keepdims=True)
@@ -271,9 +271,7 @@
         + tokens * jnp.sum(hpp * adjp, axis=0, keepdims=True)
     )
     total = jnp.sum(up_f * (gu_ref[...] + v), axis=0, keepdims=True)
-    rate_row = total * table_ref[INV : INV + 1, :] - lag
-    red = jnp.concatenate([dw, jnp.broadcast_to(rate_row, (8, channels))], axis=0)
-    return red, rows, gcoef
+    return total * table_ref[INV : INV + 1, :] - lag
 
 
 def first_kernel(
@@ -296,12 +294,11 @@
     )
     tokens = up_ref.shape[0]
     states = coef_ref.shape[1] // 2
-    recv_refs = recv_refs[::-1]
     h_in, adj, weights = unpack(seq_size, recv_refs, table_ref, states, tokens)
     hpp = table_ref[EMID : EMID + 1, :] * h_in
     hpp_ref[...] = hpp
-    for k, weight in enumerate(weights):
-        weight_ref[k : k + 1, :] = weight
+    for k, weight in zip(ORDERS[0](seq_size), weights):
+        weight_ref[k - 1 : k, :] = weight
     adj_ref[...] = adj
     rows = adjoint_rows(adj, table_ref)
     gcoef = coef_total(rows, state_rows(hpp), gcoef_ref, up_ref[...], gmp_ref[...])
@@ -317,8 +314,8 @@
 
 def gather_adjoint(recv_refs, weight_ref):
     adj = None
-    for k, r in enumerate(recv_refs):
-        term = weight_ref[k : k + 1, :] * r[...].astype(F32)
+    for k, r in zip(ORDERS[1](len(recv_refs) + 1), recv_refs):
+        term = weight_ref[k - 1 : k, :] * r[...].astype(F32)
         adj = term if adj is None else adj + term
     return adj
 
@@ -334,20 +331,17 @@
     lag_ref,
     hpp_ref,
     adj_ref,
-    red_ref,
-):
-    red_ref[...] = parameter_gradients(
-        adj_ref[...],
-        hpp_ref[...],
-        gu_ref,
-        gcoef_ref,
-        lag_ref,
-        up_ref,
-        gmp_ref,
-        coef_ref,
-        table_ref,
-        x_ref,
-    )[0]
+    dw_ref,
+    rate_ref,
+):
+    adj, hpp = adj_ref[...], hpp_ref[...]
+    gcoef = coef_total(
+        adjoint_rows(adj, table_ref), state_rows(hpp), gcoef_ref, up_ref[...], gmp_ref[...]
+    )
+    dw_ref[...] = mm(gcoef, x_ref[0], TN)
+    rate_ref[...] = rate_gradients(
+        adj, hpp, gu_ref, lag_ref, up_ref, gmp_ref, coef_ref, table_ref
+    )
 
 
 def parameter_kernel(
@@ -355,44 +349,49 @@
     seq_size,
     up_ref,
     gmp_ref,
-    coef_ref,
     table_ref,
     x_ref,
-    gu_ref,
     gcoef_in_ref,
-    lag_ref,
     hpp_ref,
     weight_ref,
     kept_ref,
     *refs,
 ):
-    recv_refs, (rows_ref, gcoef_ref, *out_refs) = refs[: seq_size - 1], refs[seq_size - 1 :]
-    red, rows_ref[...], gcoef_ref[...] = parameter_gradients(
-        gather_adjoint(recv_refs, weight_ref),
-        hpp_ref[...],
-        gu_ref,
-        gcoef_in_ref,
-        lag_ref,
-        up_ref,
-        gmp_ref,
-        coef_ref,
-        table_ref,
-        x_ref,
-    )
+    recv_refs, (adj_ref, rows_ref, gcoef_ref, *out_refs) = refs[: seq_size - 1], refs[seq_size - 1 :]
+    adj = gather_adjoint(recv_refs, weight_ref)
+    adj_ref[...] = adj
+    rows = adjoint_rows(adj, table_ref)
+    rows_ref[...] = rows
+    gcoef = coef_total(rows, state_rows(hpp_ref[...]), gcoef_in_ref, up_ref[...], gmp_ref[...])
+    gcoef_ref[...] = gcoef
+    dw = mm(gcoef, x_ref[0], TN)
     if not last:
-        out_refs[0][...] = red
+        out_refs[0][...] = dw
         return
-    red = jnp.where(lax.axis_index("section") == 0, red, kept_ref[...])
     keep_ref, send_ref = out_refs
-    coefs = red.shape[0] - 8
-    half = red.shape[1] // 2
-    keep, send = split(red[:coefs, :])
+    keep_ref[...], send = split(jnp.where(lax.axis_index("section") == 0, dw, kept_ref[...]))
     send_ref[...] = send.astype(BF16)
-    keep_ref[:coefs, :] = keep
-    rate = red[coefs:, :]
-    keep_ref[coefs : coefs + 1, :] = rate[:1, :half]
-    keep_ref[coefs + 1 : coefs + 2, :] = rate[:1, half:]
-    keep_ref[coefs + 2 :, :] = jnp.zeros((6, half), F32)
+
+
+def rate_kernel(
+    last,
+    up_ref,
+    gmp_ref,
+    coef_ref,
+    table_ref,
+    gu_ref,
+    lag_ref,
+    hpp_ref,
+    adj_ref,
+    kept_ref,
+    rate_ref,
+):
+    rate = rate_gradients(
+        adj_ref[...], hpp_ref[...], gu_ref, lag_ref, up_ref, gmp_ref, coef_ref, table_ref
+    )
+    if last:
+        rate = jnp.where(lax.axis_index("section") == 0, rate, kept_ref[...])
+    rate_ref[...] = rate
 
 
 def middle_input_kernel(
@@ -433,23 +432,28 @@
     adjoint_ref[...] = adjoint.astype(BF16)
 
 
-def pair_kernel(keep_ref, other_ref, sum_ref):
-    coefs = other_ref.shape[0]
-    sum_ref[:coefs, :] = (keep_ref[:coefs, :] + other_ref[...].astype(F32)).astype(BF16)
-    sum_ref[coefs:, :] = keep_ref[coefs:, :].astype(BF16)
+def pair_kernel(keep_ref, other_ref, rate_ref, sum_ref):
+    coefs, half = keep_ref.shape
+    sum_ref[:coefs, :] = (keep_ref[...] + other_ref[...].astype(F32)).astype(BF16)
+    rate = jnp.concatenate([rate_ref[:, :half], rate_ref[:, half:], jnp.zeros((6, half), F32)], axis=0)
+    sum_ref[coefs:, :] = rate.astype(BF16)
 
 
 def total_kernel(seq_size, *refs):
     pieces, (w_ref, rate_ref) = refs[:seq_size], refs[seq_size:]
-    heads = rate_ref.shape[1]
-    terms = [r[...].astype(F32) for r in pieces]
+    ranges = [0, *ORDERS[2](seq_size)]
+    terms = [pieces[ranges.index(k)][...].astype(F32) for k in range(seq_size)]
     while len(terms) > 1:
         terms = [x + y for x, y in zip(terms[::2], terms[1::2])]
     total = terms[0]
-    coefs, half = w_ref.shape
-    channels = 2 * half
+    coefs = w_ref.shape[0]
     w_ref[...] = total[:coefs, :]
-    row = jnp.concatenate([total[coefs : coefs + 1, :], total[coefs + 1 : coefs + 2, :]], axis=1)
+    rate_ref[...] = total[coefs:, :]
+
+
+def head_kernel(row_ref, rate_ref):
+    heads, channels = rate_ref.shape[1], 2 * row_ref.shape[1]
+    row = jnp.concatenate([row_ref[:1, :], row_ref[1:2, :]], axis=1)
     lane = lax.broadcasted_iota(jnp.int32, (heads, channels), 1) // (channels // heads)
     head = lax.broadcasted_iota(jnp.int32, (heads, channels), 0)
     col = jnp.sum(jnp.where(lane == head, row, 0.0), axis=1, keepdims=True)
@@ -482,7 +486,7 @@
     vec, low = ((tokens, channels), F32), ((tokens, channels), BF16)
     row = ((1, channels), F32)
     few = ((tokens, coefs), F32)
-    reduced = ((coefs + 8, channels), F32)
+    wide = ((coefs, width), F32)
 
     up, gmp, coef, a, sa, table, *pay = call(
         functools.partial(start_kernel, seq_size),
@@ -513,7 +517,7 @@
         bytes_accessed=4 * width * channels,
         name="start",
     )
-    recv = [partner(pay[k - 1], "seq", k) for k in range(1, seq_size)]
+    recv = [partner(pay[k - 1], "seq", k) for k in ORDERS[0](seq_size)]
 
     def local(gradient):
         return call(
@@ -532,21 +536,21 @@
     keep, send, adj, hpp, weight = call(
         functools.partial(first_kernel, seq_size),
         [*halves, state, state, ((others, channels), F32)],
-        [up, gmp, coef, table, sa, w_in, w_bc, gu, gcoef, cotangent, *recv[::-1]],
+        [up, gmp, coef, table, sa, w_in, w_bc, gu, gcoef, cotangent, *recv],
         flops=big,
         bytes_accessed=2 * width * channels,
         name="first",
     )
-    (red,) = call(
+    dw, rate = call(
         first_parameter_kernel,
-        [reduced],
+        [wide, row],
         [up, gmp, coef, table, section_inputs, gu, gcoef, lag, hpp, adj],
         flops=big // 4,
         bytes_accessed=4 * tokens * channels,
         name="first_parameters",
     )
     section = lax.axis_index("section")
-    kept, kept_red = None, red
+    kept, kept_dw, kept_rate = None, dw, rate
     for moment in range(1, sections):
         result = (keep + swap(send, "mp").astype(F32)).astype(BF16)
         if kept is None:
@@ -554,8 +558,11 @@
         else:
             was_active = section == sections - moment
             kept = jnp.where(was_active, result, kept)
-            kept_red = jnp.where(was_active, red, kept_red)
+            kept_dw = jnp.where(was_active, dw, kept_dw)
+            kept_rate = jnp.where(was_active, rate, kept_rate)
         mine = rotate(result, "section", -1)
+        if moment == 1:
+            mine, kept_dw, kept_rate = lax.optimization_barrier((mine, kept_dw, kept_rate))
         other = swap(mine, "mp")
         gmp, adjoint = call(
             hop_kernel,
@@ -565,20 +572,28 @@
             bytes_accessed=2 * width * channels,
             name="hop",
         )
-        recv = [partner(adjoint, "seq", k) for k in range(1, seq_size)]
+        recv = [partner(adjoint, "seq", k) for k in ORDERS[1](seq_size)]
         gu, gcoef, lag = local(gmp)
         last = moment == sections - 1
-        rows, gcoef, *red = call(
+        adj, rows, gcoef, *dw = call(
             functools.partial(parameter_kernel, last, seq_size),
-            [((coefs, channels), BF16), ((tokens, coefs), BF16)]
-            + ([((coefs + 8, half), F32), ((coefs, half), BF16)] if last else [reduced]),
-            [up, gmp, coef, table, section_inputs, gu, gcoef, lag, hpp, weight, kept_red, *recv],
+            [state, ((coefs, channels), BF16), ((tokens, coefs), BF16)]
+            + ([((coefs, half), F32), ((coefs, half), BF16)] if last else [wide]),
+            [up, gmp, table, section_inputs, gcoef, hpp, weight, kept_dw, *recv],
             flops=big // 4,
             bytes_accessed=4 * tokens * channels,
             name="parameters",
         )
+        (rate,) = call(
+            functools.partial(rate_kernel, last),
+            [row],
+            [up, gmp, coef, table, gu, lag, hpp, adj, kept_rate],
+            flops=big // 8,
+            bytes_accessed=4 * tokens * channels,
+            name="rates",
+        )
         if not last:
-            (red,) = red
+            (dw,) = dw
             keep, send = call(
                 middle_input_kernel,
                 halves,
@@ -588,9 +603,8 @@
                 name="middle_input",
             )
     (red,) = call(
-        pair_kernel, [((coefs + 8, half), BF16)], [red[0], swap(red[1], "mp")], name="pair"
-    )
-    rows, red = lax.optimization_barrier((rows, red))
+        pair_kernel, [((coefs + 8, half), BF16)], [dw[0], swap(dw[1], "mp"), rate], name="pair"
+    )
     (part,) = call(
         last_input_kernel,
         [low],
@@ -599,20 +613,22 @@
         bytes_accessed=2 * width * channels,
         name="last_input",
     )
+    part, red = lax.optimization_barrier((part, red))
     (out,) = call(
         output_kernel,
         [((1, tokens, width), BF16)],
         [part, swap(part, "mp"), mine, other],
         name="output",
     )
-    pieces = [partner(red, "seq", k) for k in range(1, seq_size)]
+    pieces = [partner(red, "seq", k) for k in ORDERS[2](seq_size)]
     red, out = lax.optimization_barrier((red, out))
-    grad_w, grad_rates = call(
+    grad_w, rate = call(
         functools.partial(total_kernel, seq_size),
-        [((coefs, half), F32), ((1, heads), F32)],
+        [((coefs, half), F32), ((8, half), F32)],
         [red, *pieces],
         name="total",
     )
+    (grad_rates,) = call(head_kernel, [((1, heads), F32)], [rate], name="heads")
     (grad_w,) = call(
         join_kernel, [((1, coefs, width), F32)], [grad_w, swap(grad_w, "mp")], name="join"
     )

time: 42.6 us -> 41.4 us (0.972)
  starting transfers between devices: 16.5 us -> 14.9 us
  waiting for transfers between devices: 14.4 us -> 14.9 us
    ppermute x9, waiting for transfers between devices: 6.05 us -> 8.86 us  [partner(): return lax.ppermute(value, axis, [(i, i ^ k) for i in range(n)])]
    ppermute x6, waiting for transfers between devices: 8.36 us -> 6.04 us  [rotate(): return lax.ppermute(value, axis, [(i, (i + by) % n) for i in range(n)])]
    ppermute x9, starting transfers between devices: 14.6 us -> 12.8 us  [partner(): return lax.ppermute(value, axis, [(i, i ^ k) for i in range(n)])]
    pallas_call x12 -> x14, Pallas kernels: 10.7 us -> 10.5 us  [call(): pl.pallas_call(kernel, out_shape=[jax.ShapeDtypeStruct(s, d) for s, d in...]
  transfers between devices with their start and end apart: 15 -> 15, of which waited for: 12 -> 11; matrix products, arithmetic and copies ran while one was open for 0% -> 0% of each run, Pallas kernels for 7% -> 11%
where the time goes in v3:
time: 41.4 us; the launch traced here: 41.2 us
  starting transfers between devices  14.9 us (36%)
  waiting for transfers between devices  14.9 us (36%)
  Pallas kernels  10.5 us (25%)
  between operations  0.79 us (2%)
    ppermute x9, starting transfers between devices, partner(): return lax.ppermute(value, axis, [(i, i ^ k) for i in range(n)])  12.8 us
    pallas_call x14, Pallas kernels, call(): pl.pallas_call(kernel, out_shape=[jax.ShapeDtypeStruct(s, d) for s, d in...  10.5 us
    ppermute x9, waiting for transfers between devices, partner(): return lax.ppermute(value, axis, [(i, i ^ k) for i in range(n)])  8.86 us
    ppermute x6, waiting for transfers between devices, rotate(): return lax.ppermute(value, axis, [(i, (i + by) % n) for i in range(n)])  6.04 us
    ppermute x6, starting transfers between devices, rotate(): return lax.ppermute(value, axis, [(i, (i + by) % n) for i in range(n)])  2.13 us
  transfers between devices with their start and end apart: 15, of which 11 were waited for; matrix products, arithmetic and copies ran while one was open for 0% of the time, Pallas kernels for 11%

profile of v3, /device:TPU:0, one launch (start us, length us, event | category | flops | bytes accessed | tf_op | source)
XLA Modules:
  0.0 41.2 jit_solution(7441371303758172733)
XLA Ops:
  0.7 3.1 %start.1 = (bf16[128,768]{1,0:T(8,128)(2,1)S(1)}, bf16[128,768]{1,0:T(8,128)(2,1)S(1)}, bf16[128,32]{1,0:T(8,128)(2,1)S(1)}, f32[128,768]{1,0:T(8,128)S(1)}, f32...) custom-call(bf16[1,128,768]{2,1,0:T(8,128)(2,1)} %x_ref.3, ...), custom_call_target="tpu_custom_call" | custom-call | flops 301989888 | bytes 2359296 | tf_op jit(solution)/shard_map/start/pallas_call | solution.py:64
  3.7 5.1 %collective-permute-start = (bf16[16,896]{1,0:T(8,128)(2,1)S(1)}, bf16[16,896]{1,0:T(8,128)(2,1)S(1)}, u32[]{:S(2)}, u32[]{:S(2)}) collective-permute-start(bf16[16,896]{1,0:T(8,128)(2,1)S(1)} %get-tuple-element.49), channel_id=1, source_target_pairs={{0,12},{4,8},{8,4},{12,0},{1,13},{5,9},{9,5},{13,1},{2,14},{6,10},... | collective-permute-start | bytes 86024 | tf_op jit(solution)/shard_map/ppermute | solution.py:40
  8.9 0.6 %collective-permute-start.2 = (bf16[16,896]{1,0:T(8,128)(2,1)S(1)}, bf16[16,896]{1,0:T(8,128)(2,1)S(1)}, u32[]{:S(2)}, u32[]{:S(2)}) collective-permute-start(bf16[16,896]{1,0:T(8,128)(2,1)S(1)} %get-tuple-element.51), channel_id=1, source_target_pairs={{0,4},{4,0},{8,12},{12,8},{1,5},{5,1},{9,13},{13,9},{2,6},{6,2},{1... | collective-permute-start | bytes 86024 | tf_op jit(solution)/shard_map/ppermute | solution.py:40
  9.5 0.8 %local.2 = (f32[128,768]{1,0:T(8,128)S(1)}, f32[128,32]{1,0:T(8,128)S(1)}, f32[1,768]{1,0:T(1,128)S(1)}) custom-call(bf16[128,768]{1,0:T(8,128)(2,1)S(1)} %get-tuple-element.41.up_ref, bf16[128,768]{1,0:T(8,128)(2,1)S(1)} %get-tuple-element.45.gmp_ref, bf16[128,32]{1,0:T(8,128)(2,1)S(1)} %get-tuple-element.42.coef_ref), custom_call_target="tpu_custom_call" | custom-call | flops 150994944 | bytes 393216 | tf_op jit(solution)/shard_map/local/pallas_call | solution.py:64
  10.7 2.9 %collective-permute-done.1.refs_1_ = bf16[16,896]{1,0:T(8,128)(2,1)S(1)} collective-permute-done((bf16[16,896]{1,0:T(8,128)(2,1)S(1)}, bf16[16,896]{1,0:T(8,128)(2,1)S(1)}, u32[]{:S(2)}, u32[]{:S(2)}) %collective-permute-start.1) | collective-permute-done | bytes 28704 | tf_op jit(solution)/shard_map/ppermute | solution.py:40
  13.7 1.0 %first.1 = (f32[128,384]{1,0:T(8,128)S(1)}, bf16[128,384]{1,0:T(8,128)(2,1)S(1)}, f32[16,768]{1,0:T(8,128)S(1)}, f32[16,768]{1,0:T(8,128)S(1)}, f32[3,768]{1,0:T(4,128)S(1)}) custom-call(bf16[128,768]{1,0:T(8,128)(2,1)S(1)} %get-tuple-element.41.up_ref, bf16[128,768]{1,0:T(8,128)(2,1)S(1)} %get-tuple-element.45.gmp_ref, ...), custom_call_target="tpu_custom_call" | custom-call | flops 150994944 | bytes 1179648 | tf_op jit(solution)/shard_map/first/pallas_call | solution.py:64
  14.8 1.3 %collective-permute-done.3 = bf16[128,384]{1,0:T(8,128)(2,1)S(1)} collective-permute-done((bf16[128,384]{1,0:T(8,128)(2,1)S(1)}, bf16[128,384]{1,0:T(8,128)(2,1)S(1)}, u32[]{:S(2)}, u32[]{:S(2)}) %collective-permute-start.3) | collective-permute-done | bytes 98336 | tf_op jit(solution)/shard_map/ppermute | solution.py:35
  16.1 1.6 %collective-permute-start.4 = (bf16[128,384]{1,0:T(8,128)(2,1)S(1)}, bf16[128,384]{1,0:T(8,128)(2,1)S(1)}, u32[]{:S(2)}, u32[]{:S(2)}) collective-permute-start(bf16[128,384]{1,0:T(8,128)(2,1)S(1)} %add_convert_fusion.kept_ref), channel_id=1, source_target_pairs={{0,2},{2,0},{1,3},{3,1},{4,6},{6,4},{5,7},{7,5},{8,10},{10,8},{9,1... | collective-permute-start | bytes 294920 | tf_op jit(solution)/shard_map/ppermute | solution.py:35
  17.6 0.7 %first_parameters.1 = (f32[32,768]{1,0:T(8,128)S(1)}, f32[1,768]{1,0:T(1,128)S(1)}) custom-call(bf16[128,768]{1,0:T(8,128)(2,1)S(1)} %get-tuple-element.41.up_ref, bf16[128,768]{1,0:T(8,128)(2,1)S(1)} %get-tuple-element.45.gmp_ref, bf16[128,32]{1,0:T(8,128)(2,1)S(1)} %get-tuple-element.42.coef_ref, f32[8,768]{1,0:T(8,128)S(1)} %get-tuple-element.44.table_ref, ...), custom_call_target="tpu_custom_call" | custom-call | flops 37748736 | bytes 393216 | tf_op jit(solution)/shard_map/first_parameters/pallas_call | solution.py:64
  18.3 2.6 %collective-permute-done.4.mine_ref = bf16[128,384]{1,0:T(8,128)(2,1)S(1)} collective-permute-done((bf16[128,384]{1,0:T(8,128)(2,1)S(1)}, bf16[128,384]{1,0:T(8,128)(2,1)S(1)}, u32[]{:S(2)}, u32[]{:S(2)}) %collective-permute-start.4) | collective-permute-done | bytes 98336 | tf_op jit(solution)/shard_map/ppermute | solution.py:35
  21.0 1.3 %collective-permute-done.5.other_ref = bf16[128,384]{1,0:T(8,128)(2,1)S(1)} collective-permute-done((bf16[128,384]{1,0:T(8,128)(2,1)S(1)}, bf16[128,384]{1,0:T(8,128)(2,1)S(1)}, u32[]{:S(2)}, u32[]{:S(2)}) %collective-permute-start.5) | collective-permute-done | bytes 98336 | tf_op jit(solution)/shard_map/ppermute | solution.py:35
  22.9 2.1 %collective-permute-start.8 = (bf16[16,768]{1,0:T(8,128)(2,1)S(1)}, bf16[16,768]{1,0:T(8,128)(2,1)S(1)}, u32[]{:S(2)}, u32[]{:S(2)}) collective-permute-start(bf16[16,768]{1,0:T(8,128)(2,1)S(1)} %get-tuple-element.64), channel_id=1, source_target_pairs={{0,8},{4,12},{8,0},{12,4},{1,9},{5,13},{9,1},{13,5},{2,10},{6,14},... | collective-permute-start | bytes 73736 | tf_op jit(solution)/shard_map/ppermute | solution.py:40
  25.1 1.4 %collective-permute-start.6 = (bf16[16,768]{1,0:T(8,128)(2,1)S(1)}, bf16[16,768]{1,0:T(8,128)(2,1)S(1)}, u32[]{:S(2)}, u32[]{:S(2)}) collective-permute-start(bf16[16,768]{1,0:T(8,128)(2,1)S(1)} %get-tuple-element.64), channel_id=1, source_target_pairs={{0,4},{4,0},{8,12},{12,8},{1,5},{5,1},{9,13},{13,9},{2,6},{6,2},{1... | collective-permute-start | bytes 73736 | tf_op jit(solution)/shard_map/ppermute | solution.py:40
  26.5 0.8 %local.3 = (f32[128,768]{1,0:T(8,128)S(1)}, f32[128,32]{1,0:T(8,128)S(1)}, f32[1,768]{1,0:T(1,128)S(1)}) custom-call(bf16[128,768]{1,0:T(8,128)(2,1)S(1)} %get-tuple-element.41.up_ref, bf16[128,768]{1,0:T(8,128)(2,1)S(1)} %get-tuple-element.60.gmp_ref, bf16[128,32]{1,0:T(8,128)(2,1)S(1)} %get-tuple-element.42.coef_ref), custom_call_target="tpu_custom_call" | custom-call | flops 150994944 | bytes 393216 | tf_op jit(solution)/shard_map/local/pallas_call | solution.py:64
  27.7 2.9 %collective-permute-done.7.refs_1_ = bf16[16,768]{1,0:T(8,128)(2,1)S(1)} collective-permute-done((bf16[16,768]{1,0:T(8,128)(2,1)S(1)}, bf16[16,768]{1,0:T(8,128)(2,1)S(1)}, u32[]{:S(2)}, u32[]{:S(2)}) %collective-permute-start.7) | collective-permute-done | bytes 24608 | tf_op jit(solution)/shard_map/ppermute | solution.py:40
  31.5 0.6 %last_input.1.part_ref = bf16[128,768]{1,0:T(8,128)(2,1)S(1)} custom-call(bf16[32,768]{1,0:T(8,128)(2,1)S(1)} %get-tuple-element.65.rows_ref, f32[128,768]{1,0:T(8,128)S(1)} %get-tuple-element.66.gu_ref, bf16[128,32]{1,0:T(8,128)(2,1)S(1)} %get-tuple-element.67.gcoef_ref, bf16[128,32]{1,0:T(8,128)(2,1)S(1)} %get-tuple-element.42.coef_ref, ...), custom_call_target="tpu_custom_call" | custom-call | flops 150994944 | bytes 1179648 | tf_op jit(solution)/shard_map/last_input/pallas_call | solution.py:64
  32.7 0.8 %collective-permute-start.13 = (bf16[40,384]{1,0:T(8,128)(2,1)S(1)}, bf16[40,384]{1,0:T(8,128)(2,1)S(1)}, u32[]{:S(2)}, u32[]{:S(2)}) collective-permute-start(bf16[40,384]{1,0:T(8,128)(2,1)S(1)} %pair.1.refs_0_), channel_id=1, source_target_pairs={{0,8},{4,12},{8,0},{12,4},{1,9},{5,13},{9,1},{13,5},{2,10},{6,14},... | collective-permute-start | bytes 92168 | tf_op jit(solution)/shard_map/ppermute | solution.py:40
  33.5 1.2 %collective-permute-start.12 = (bf16[40,384]{1,0:T(8,128)(2,1)S(1)}, bf16[40,384]{1,0:T(8,128)(2,1)S(1)}, u32[]{:S(2)}, u32[]{:S(2)}) collective-permute-start(bf16[40,384]{1,0:T(8,128)(2,1)S(1)} %pair.1.refs_0_), channel_id=1, source_target_pairs={{0,12},{4,8},{8,4},{12,0},{1,13},{5,9},{9,5},{13,1},{2,14},{6,10},... | collective-permute-start | bytes 92168 | tf_op jit(solution)/shard_map/ppermute | solution.py:40
  34.8 1.5 %collective-permute-start.11 = (bf16[40,384]{1,0:T(8,128)(2,1)S(1)}, bf16[40,384]{1,0:T(8,128)(2,1)S(1)}, u32[]{:S(2)}, u32[]{:S(2)}) collective-permute-start(bf16[40,384]{1,0:T(8,128)(2,1)S(1)} %pair.1.refs_0_), channel_id=1, source_target_pairs={{0,4},{4,0},{8,12},{12,8},{1,5},{5,1},{9,13},{13,9},{2,6},{6,2},{1... | collective-permute-start | bytes 92168 | tf_op jit(solution)/shard_map/ppermute | solution.py:40
  36.2 0.8 %output.1 = bf16[1,128,768]{2,1,0:T(8,128)(2,1)} custom-call(bf16[128,768]{1,0:T(8,128)(2,1)S(1)} %last_input.1.part_ref, bf16[128,768]{1,0:T(8,128)(2,1)S(1)} %collective-permute-done.10.part2_ref, bf16[128,384]{1,0:T(8,128)(2,1)S(1)} %collective-permute-done.4.mine_ref, bf16[128,384]{1,0:T(8,128)(2,1)S(1)} %collective-permute-done.5.other_ref), custom_call_target="tpu_custom_call" | custom-call | tf_op jit(solution)/shard_map/output/pallas_call | solution.py:64
  37.0 0.8 %collective-permute-done.13.refs_3_ = bf16[40,384]{1,0:T(8,128)(2,1)S(1)} collective-permute-done((bf16[40,384]{1,0:T(8,128)(2,1)S(1)}, bf16[40,384]{1,0:T(8,128)(2,1)S(1)}, u32[]{:S(2)}, u32[]{:S(2)}) %collective-permute-start.13) | collective-permute-done | bytes 30752 | tf_op jit(solution)/shard_map/ppermute | solution.py:40
  37.8 1.5 %collective-permute-done.12.refs_2_ = bf16[40,384]{1,0:T(8,128)(2,1)S(1)} collective-permute-done((bf16[40,384]{1,0:T(8,128)(2,1)S(1)}, bf16[40,384]{1,0:T(8,128)(2,1)S(1)}, u32[]{:S(2)}, u32[]{:S(2)}) %collective-permute-start.12) | collective-permute-done | bytes 30752 | tf_op jit(solution)/shard_map/ppermute | solution.py:40
  39.9 0.6 %collective-permute-done.14.other_ref = f32[32,384]{1,0:T(8,128)S(1)} collective-permute-done((f32[32,384]{1,0:T(8,128)S(1)}, f32[32,384]{1,0:T(8,128)S(1)}, u32[]{:S(2)}, u32[]{:S(2)}) %collective-permute-start.14) | collective-permute-done | bytes 49184 | tf_op jit(solution)/shard_map/ppermute | solution.py:35
  40.6 0.7 %join.1 = f32[1,32,768]{2,1,0:T(8,128)} custom-call(f32[32,384]{1,0:T(8,128)S(1)} %get-tuple-element.77.mine_ref, f32[32,384]{1,0:T(8,128)S(1)} %collective-permute-done.14.other_ref), custom_call_target="tpu_custom_call" | custom-call | tf_op jit(solution)/shard_map/join/pallas_call | solution.py:64
  (31 shorter events, 3.8 us)
Async XLA Ops:
  0.6 13.0 %copy-start = (bf16[1,768,768]{2,1,0:T(8,128)(2,1)S(1)}, bf16[1,768,768]{2,1,0:T(8,128)(2,1)}, u32[]{:S(2)}) copy-start(bf16[1,768,768]{2,1,0:T(8,128)(2,1)} %w_in_ref.3) | copy-start | bytes 3538948
  0.6 13.0 %copy-start.3 = (bf16[128,768]{1,0:T(8,128)(2,1)S(1)}, bf16[128,768]{1,0:T(8,128)(2,1)}, u32[]{:S(2)}) copy-start(bf16[128,768]{1,0:T(8,128)(2,1)} %g_ref.1) | copy-start | bytes 589828
  0.7 13.0 %copy-start.4 = (bf16[1,768,32]{1,2,0:T(8,128)(2,1)S(1)}, bf16[1,768,32]{1,2,0:T(8,128)(2,1)}, u32[]{:S(2)}) copy-start(bf16[1,768,32]{1,2,0:T(8,128)(2,1)} %param.10) | copy-start | bytes 147460
  3.7 7.0 %collective-permute-start = (bf16[16,896]{1,0:T(8,128)(2,1)S(1)}, bf16[16,896]{1,0:T(8,128)(2,1)S(1)}, u32[]{:S(2)}, u32[]{:S(2)}) collective-permute-start(bf16[16,896]{1,0:T(8,128)(2,1)S(1)} %get-tuple-element.49), channel_id=1, source_target_pairs={{0,12},{4,8},{8,4},{12,0},{1,13},{5,9},{9,5},{13,1},{2,14},{6,10},... | collective-permute-start | bytes 86024 | tf_op jit(solution)/shard_map/ppermute | solution.py:40
  8.9 4.8 %collective-permute-start.1 = (bf16[16,896]{1,0:T(8,128)(2,1)S(1)}, bf16[16,896]{1,0:T(8,128)(2,1)S(1)}, u32[]{:S(2)}, u32[]{:S(2)}) collective-permute-start(bf16[16,896]{1,0:T(8,128)(2,1)S(1)} %get-tuple-element.50), channel_id=1, source_target_pairs={{0,8},{4,12},{8,0},{12,4},{1,9},{5,13},{9,1},{13,5},{2,10},{6,14},... | collective-permute-start | bytes 86024 | tf_op jit(solution)/shard_map/ppermute | solution.py:40
  8.9 4.8 %collective-permute-start.2 = (bf16[16,896]{1,0:T(8,128)(2,1)S(1)}, bf16[16,896]{1,0:T(8,128)(2,1)S(1)}, u32[]{:S(2)}, u32[]{:S(2)}) collective-permute-start(bf16[16,896]{1,0:T(8,128)(2,1)S(1)} %get-tuple-element.51), channel_id=1, source_target_pairs={{0,4},{4,0},{8,12},{12,8},{1,5},{5,1},{9,13},{13,9},{2,6},{6,2},{1... | collective-permute-start | bytes 86024 | tf_op jit(solution)/shard_map/ppermute | solution.py:40
  13.6 4.0 %copy-start.2 = (bf16[1,128,768]{2,1,0:T(8,128)(2,1)S(1)}, bf16[1,128,768]{2,1,0:T(8,128)(2,1)}, u32[]{:S(2)}) copy-start(bf16[1,128,768]{2,1,0:T(8,128)(2,1)} %x_ref.3) | copy-start | bytes 589828
  14.7 7.6 %copy-start.1 = (bf16[1,768,768]{2,1,0:T(8,128)(2,1)S(1)}, bf16[1,768,768]{2,1,0:T(8,128)(2,1)}, u32[]{:S(2)}) copy-start(bf16[1,768,768]{2,1,0:T(8,128)(2,1)} %w_out_ref.1) | copy-start | bytes 3538948
  14.7 1.4 %collective-permute-start.3 = (bf16[128,384]{1,0:T(8,128)(2,1)S(1)}, bf16[128,384]{1,0:T(8,128)(2,1)S(1)}, u32[]{:S(2)}, u32[]{:S(2)}) collective-permute-start(bf16[128,384]{1,0:T(8,128)(2,1)S(1)} %get-tuple-element.53), channel_id=1, source_target_pairs={{0,1},{1,0},{2,3},{3,2},{4,5},{5,4},{6,7},{7,6},{8,9},{9,8},{10,11... | collective-permute-start | bytes 294920 | tf_op jit(solution)/shard_map/ppermute | solution.py:35
  16.1 4.9 %collective-permute-start.4 = (bf16[128,384]{1,0:T(8,128)(2,1)S(1)}, bf16[128,384]{1,0:T(8,128)(2,1)S(1)}, u32[]{:S(2)}, u32[]{:S(2)}) collective-permute-start(bf16[128,384]{1,0:T(8,128)(2,1)S(1)} %add_convert_fusion.kept_ref), channel_id=1, source_target_pairs={{0,2},{2,0},{1,3},{3,1},{4,6},{6,4},{5,7},{7,5},{8,10},{10,8},{9,1... | collective-permute-start | bytes 294920 | tf_op jit(solution)/shard_map/ppermute | solution.py:35
  21.0 1.3 %collective-permute-start.5 = (bf16[128,384]{1,0:T(8,128)(2,1)S(1)}, bf16[128,384]{1,0:T(8,128)(2,1)S(1)}, u32[]{:S(2)}, u32[]{:S(2)}) collective-permute-start(bf16[128,384]{1,0:T(8,128)(2,1)S(1)} %collective-permute-done.4.mine_ref), channel_id=1, source_target_pairs={{0,1},{1,0},{2,3},{3,2},{4,5},{5,4},{6,7},{7,6},{8,9},{9,8},{10,11... | collective-permute-start | bytes 294920 | tf_op jit(solution)/shard_map/ppermute | solution.py:35
  22.9 4.8 %collective-permute-start.8 = (bf16[16,768]{1,0:T(8,128)(2,1)S(1)}, bf16[16,768]{1,0:T(8,128)(2,1)S(1)}, u32[]{:S(2)}, u32[]{:S(2)}) collective-permute-start(bf16[16,768]{1,0:T(8,128)(2,1)S(1)} %get-tuple-element.64), channel_id=1, source_target_pairs={{0,8},{4,12},{8,0},{12,4},{1,9},{5,13},{9,1},{13,5},{2,10},{6,14},... | collective-permute-start | bytes 73736 | tf_op jit(solution)/shard_map/ppermute | solution.py:40
  25.0 5.6 %collective-permute-start.7 = (bf16[16,768]{1,0:T(8,128)(2,1)S(1)}, bf16[16,768]{1,0:T(8,128)(2,1)S(1)}, u32[]{:S(2)}, u32[]{:S(2)}) collective-permute-start(bf16[16,768]{1,0:T(8,128)(2,1)S(1)} %get-tuple-element.64), channel_id=1, source_target_pairs={{0,12},{4,8},{8,4},{12,0},{1,13},{5,9},{9,5},{13,1},{2,14},{6,10},... | collective-permute-start | bytes 73736 | tf_op jit(solution)/shard_map/ppermute | solution.py:40
  25.1 5.6 %collective-permute-start.6 = (bf16[16,768]{1,0:T(8,128)(2,1)S(1)}, bf16[16,768]{1,0:T(8,128)(2,1)S(1)}, u32[]{:S(2)}, u32[]{:S(2)}) collective-permute-start(bf16[16,768]{1,0:T(8,128)(2,1)S(1)} %get-tuple-element.64), channel_id=1, source_target_pairs={{0,4},{4,0},{8,12},{12,8},{1,5},{5,1},{9,13},{13,9},{2,6},{6,2},{1... | collective-permute-start | bytes 73736 | tf_op jit(solution)/shard_map/ppermute | solution.py:40
  31.1 1.3 %collective-permute-start.9 = (bf16[32,384]{1,0:T(8,128)(2,1)S(1)}, bf16[32,384]{1,0:T(8,128)(2,1)S(1)}, u32[]{:S(2)}, u32[]{:S(2)}) collective-permute-start(bf16[32,384]{1,0:T(8,128)(2,1)S(1)} %get-tuple-element.69), channel_id=1, source_target_pairs={{0,1},{1,0},{2,3},{3,2},{4,5},{5,4},{6,7},{7,6},{8,9},{9,8},{10,11... | collective-permute-start | bytes 73736 | tf_op jit(solution)/shard_map/ppermute | solution.py:35
  32.4 3.9 %collective-permute-start.10 = (bf16[128,768]{1,0:T(8,128)(2,1)S(1)}, bf16[128,768]{1,0:T(8,128)(2,1)S(1)}, u32[]{:S(2)}, u32[]{:S(2)}) collective-permute-start(bf16[128,768]{1,0:T(8,128)(2,1)S(1)} %last_input.1.part_ref), channel_id=1, source_target_pairs={{0,1},{1,0},{2,3},{3,2},{4,5},{5,4},{6,7},{7,6},{8,9},{9,8},{10,11... | collective-permute-start | bytes 589832 | tf_op jit(solution)/shard_map/ppermute | solution.py:35
  32.7 5.0 %collective-permute-start.13 = (bf16[40,384]{1,0:T(8,128)(2,1)S(1)}, bf16[40,384]{1,0:T(8,128)(2,1)S(1)}, u32[]{:S(2)}, u32[]{:S(2)}) collective-permute-start(bf16[40,384]{1,0:T(8,128)(2,1)S(1)} %pair.1.refs_0_), channel_id=1, source_target_pairs={{0,8},{4,12},{8,0},{12,4},{1,9},{5,13},{9,1},{13,5},{2,10},{6,14},... | collective-permute-start | bytes 92168 | tf_op jit(solution)/shard_map/ppermute | solution.py:40
  33.5 5.7 %collective-permute-start.12 = (bf16[40,384]{1,0:T(8,128)(2,1)S(1)}, bf16[40,384]{1,0:T(8,128)(2,1)S(1)}, u32[]{:S(2)}, u32[]{:S(2)}) collective-permute-start(bf16[40,384]{1,0:T(8,128)(2,1)S(1)} %pair.1.refs_0_), channel_id=1, source_target_pairs={{0,12},{4,8},{8,4},{12,0},{1,13},{5,9},{9,5},{13,1},{2,14},{6,10},... | collective-permute-start | bytes 92168 | tf_op jit(solution)/shard_map/ppermute | solution.py:40
  34.8 4.5 %collective-permute-start.11 = (bf16[40,384]{1,0:T(8,128)(2,1)S(1)}, bf16[40,384]{1,0:T(8,128)(2,1)S(1)}, u32[]{:S(2)}, u32[]{:S(2)}) collective-permute-start(bf16[40,384]{1,0:T(8,128)(2,1)S(1)} %pair.1.refs_0_), channel_id=1, source_target_pairs={{0,4},{4,0},{8,12},{12,8},{1,5},{5,1},{9,13},{13,9},{2,6},{6,2},{1... | collective-permute-start | bytes 92168 | tf_op jit(solution)/shard_map/ppermute | solution.py:40
  39.3 1.3 %collective-permute-start.14 = (f32[32,384]{1,0:T(8,128)S(1)}, f32[32,384]{1,0:T(8,128)S(1)}, u32[]{:S(2)}, u32[]{:S(2)}) collective-permute-start(f32[32,384]{1,0:T(8,128)S(1)} %get-tuple-element.77.mine_ref), channel_id=1, source_target_pairs={{0,1},{1,0},{2,3},{3,2},{4,5},{5,4},{6,7},{7,6},{8,9},{9,8},{10,11... | collective-permute-start | bytes 147464 | tf_op jit(solution)/shard_map/ppermute | solution.py:35

commit v4 on v3

--- a/solution.py
+++ b/solution.py
@@ -18,11 +18,7 @@
 
 RATE, EMID, ATOT, INV, COUNT = 0, 1, 2, 3, 4
 TABLE_ROWS = 8
-ORDERS = (
-    lambda n: range(n - 1, 0, -1),
-    lambda n: (1, *range(n - 1, 1, -1)),
-    lambda n: (1, *range(n - 1, 1, -1)),
-)
+ORDERS = (lambda n: range(n - 1, 0, -1), lambda n: range(1, n), lambda n: range(1, n))
 OUT_CHUNKS, IN_CHUNKS = 1, 1
 
 
@@ -190,6 +186,10 @@
     return jnp.concatenate([jnp.where(low, mine, other), jnp.where(low, other, mine)], axis=1)
 
 
+def turn_kernel(w_ref, after_ref, out_ref):
+    out_ref[...] = w_ref[0].T
+
+
 def coef_grads(gs, b_part, c_part):
     return jnp.concatenate([mm(gs, c_part, TN), mm(gs, b_part, NN)], axis=1)
 
@@ -244,7 +244,7 @@
 
 def input_gradient(rows, gu, gcoef, coef, sa_ref, w_in_ref, w_bc_ref):
     grad_inner = (sa_ref[...] * (gu + mm(coef, rows, NN))).astype(BF16)
-    return mm(grad_inner, w_in_ref[0], NT) + mm(gcoef, w_bc_ref[0], NN)
+    return mm(grad_inner, w_in_ref[...], NN) + mm(gcoef, w_bc_ref[0], NN)
 
 
 def adjoint_rows(adj, table_ref):
@@ -417,7 +417,7 @@
 
 
 def scaled_gradient(g, w_out_ref, coef, a_ref, table_ref):
-    gmp = (a_ref[...] * mm(g, w_out_ref[0], NT)).astype(BF16)
+    gmp = (a_ref[...] * mm(g, w_out_ref[...], NN)).astype(BF16)
     states = coef.shape[1] // 2
     adjoint = table_ref[EMID : EMID + 1, :] * mm(coef, gmp, TN)[states:, :]
     return gmp, adjoint
@@ -529,6 +529,10 @@
             name="local",
         )
 
+    def turned(w, after):
+        return call(turn_kernel, [((w.shape[2], w.shape[1]), BF16)], [w, after], name="turn")[0]
+
+    w_in_t = turned(w_in, table)
     gu, gcoef, lag = local(gmp)
     state = ((states, channels), F32)
     half = width // 2
@@ -536,7 +540,7 @@
     keep, send, adj, hpp, weight = call(
         functools.partial(first_kernel, seq_size),
         [*halves, state, state, ((others, channels), F32)],
-        [up, gmp, coef, table, sa, w_in, w_bc, gu, gcoef, cotangent, *recv],
+        [up, gmp, coef, table, sa, w_in_t, w_bc, gu, gcoef, cotangent, *recv],
         flops=big,
         bytes_accessed=2 * width * channels,
         name="first",
@@ -549,6 +553,7 @@
         bytes_accessed=4 * tokens * channels,
         name="first_parameters",
     )
+    w_out_t = turned(w_out, rate)
     section = lax.axis_index("section")
     kept, kept_dw, kept_rate = None, dw, rate
     for moment in range(1, sections):
@@ -562,12 +567,14 @@
             kept_rate = jnp.where(was_active, rate, kept_rate)
         mine = rotate(result, "section", -1)
         if moment == 1:
-            mine, kept_dw, kept_rate = lax.optimization_barrier((mine, kept_dw, kept_rate))
+            mine, kept_dw, kept_rate, w_out_t = lax.optimization_barrier(
+                (mine, kept_dw, kept_rate, w_out_t)
+            )
         other = swap(mine, "mp")
         gmp, adjoint = call(
             hop_kernel,
             [low, ((states, channels), BF16)],
-            [w_out, coef, a, table, mine, other],
+            [w_out_t, coef, a, table, mine, other],
             flops=big,
             bytes_accessed=2 * width * channels,
             name="hop",
@@ -597,7 +604,7 @@
             keep, send = call(
                 middle_input_kernel,
                 halves,
-                [rows, gu, gcoef, coef, sa, w_in, w_bc, mine, other],
+                [rows, gu, gcoef, coef, sa, w_in_t, w_bc, mine, other],
                 flops=big,
                 bytes_accessed=2 * width * channels,
                 name="middle_input",
@@ -608,7 +615,7 @@
     (part,) = call(
         last_input_kernel,
         [low],
-        [rows, gu, gcoef, coef, sa, w_in, w_bc, kept],
+        [rows, gu, gcoef, coef, sa, w_in_t, w_bc, kept],
         flops=big,
         bytes_accessed=2 * width * channels,
         name="last_input",

time: 41.4 us -> 40.6 us (0.981)
  waiting for transfers between devices: 14.9 us -> 12.2 us
  starting transfers between devices: 14.9 us -> 16.6 us
    ppermute x9, waiting for transfers between devices: 8.86 us -> 6.42 us  [partner(): return lax.ppermute(value, axis, [(i, i ^ k) for i in range(n)])]
    ppermute x9, starting transfers between devices: 12.8 us -> 14.6 us  [partner(): return lax.ppermute(value, axis, [(i, i ^ k) for i in range(n)])]
    pallas_call x14 -> x16, Pallas kernels: 10.5 us -> 10.8 us  [call(): pl.pallas_call(kernel, out_shape=[jax.ShapeDtypeStruct(s, d) for s, d in...]
  transfers between devices with their start and end apart: 15 -> 15, of which waited for: 11 -> 12; matrix products, arithmetic and copies ran while one was open for 0% -> 0% of each run, Pallas kernels for 11% -> 13%
where the time goes in v4:
time: 40.6 us; the launch traced here: 40.5 us
  starting transfers between devices  16.6 us (41%)
  waiting for transfers between devices  12.2 us (30%)
  Pallas kernels  10.8 us (27%)
  between operations  0.8 us (2%)
    ppermute x9, starting transfers between devices, partner(): return lax.ppermute(value, axis, [(i, i ^ k) for i in range(n)])  14.6 us
    pallas_call x16, Pallas kernels, call(): pl.pallas_call(kernel, out_shape=[jax.ShapeDtypeStruct(s, d) for s, d in...  10.8 us
    ppermute x9, waiting for transfers between devices, partner(): return lax.ppermute(value, axis, [(i, i ^ k) for i in range(n)])  6.42 us
    ppermute x6, waiting for transfers between devices, rotate(): return lax.ppermute(value, axis, [(i, (i + by) % n) for i in range(n)])  5.82 us
    ppermute x6, starting transfers between devices, rotate(): return lax.ppermute(value, axis, [(i, (i + by) % n) for i in range(n)])  2 us
  transfers between devices with their start and end apart: 15, of which 12 were waited for; matrix products, arithmetic and copies ran while one was open for 0% of the time, Pallas kernels for 13%

profile of v4, /device:TPU:0, one launch (start us, length us, event | category | flops | bytes accessed | tf_op | source)
XLA Modules:
  0.0 40.5 jit_solution(2590467014320578971)
XLA Ops:
  0.6 3.1 %start.1 = (bf16[128,768]{1,0:T(8,128)(2,1)S(1)}, bf16[128,768]{1,0:T(8,128)(2,1)S(1)}, bf16[128,32]{1,0:T(8,128)(2,1)S(1)}, f32[128,768]{1,0:T(8,128)S(1)}, f32...) custom-call(bf16[1,128,768]{2,1,0:T(8,128)(2,1)} %x_ref.3, ...), custom_call_target="tpu_custom_call" | custom-call | flops 301989888 | bytes 2359296 | tf_op jit(solution)/shard_map/start/pallas_call | solution.py:60
  3.7 5.1 %collective-permute-start = (bf16[16,896]{1,0:T(8,128)(2,1)S(1)}, bf16[16,896]{1,0:T(8,128)(2,1)S(1)}, u32[]{:S(2)}, u32[]{:S(2)}) collective-permute-start(bf16[16,896]{1,0:T(8,128)(2,1)S(1)} %get-tuple-element.49), channel_id=1, source_target_pairs={{0,12},{4,8},{8,4},{12,0},{1,13},{5,9},{9,5},{13,1},{2,14},{6,10},... | collective-permute-start | bytes 86024 | tf_op jit(solution)/shard_map/ppermute | solution.py:36
  8.8 0.6 %collective-permute-start.2 = (bf16[16,896]{1,0:T(8,128)(2,1)S(1)}, bf16[16,896]{1,0:T(8,128)(2,1)S(1)}, u32[]{:S(2)}, u32[]{:S(2)}) collective-permute-start(bf16[16,896]{1,0:T(8,128)(2,1)S(1)} %get-tuple-element.51), channel_id=1, source_target_pairs={{0,4},{4,0},{8,12},{12,8},{1,5},{5,1},{9,13},{13,9},{2,6},{6,2},{1... | collective-permute-start | bytes 86024 | tf_op jit(solution)/shard_map/ppermute | solution.py:36
  9.8 0.8 %local.2 = (f32[128,768]{1,0:T(8,128)S(1)}, f32[128,32]{1,0:T(8,128)S(1)}, f32[1,768]{1,0:T(1,128)S(1)}) custom-call(bf16[128,768]{1,0:T(8,128)(2,1)S(1)} %get-tuple-element.42.up_ref, bf16[128,768]{1,0:T(8,128)(2,1)S(1)} %get-tuple-element.43.gmp_ref, bf16[128,32]{1,0:T(8,128)(2,1)S(1)} %get-tuple-element.44.coef_ref), custom_call_target="tpu_custom_call" | custom-call | flops 150994944 | bytes 393216 | tf_op jit(solution)/shard_map/local/pallas_call | solution.py:60
  10.7 2.9 %collective-permute-done.1.refs_1_ = bf16[16,896]{1,0:T(8,128)(2,1)S(1)} collective-permute-done((bf16[16,896]{1,0:T(8,128)(2,1)S(1)}, bf16[16,896]{1,0:T(8,128)(2,1)S(1)}, u32[]{:S(2)}, u32[]{:S(2)}) %collective-permute-start.1) | collective-permute-done | bytes 28704 | tf_op jit(solution)/shard_map/ppermute | solution.py:36
  13.6 0.9 %first.1 = (f32[128,384]{1,0:T(8,128)S(1)}, bf16[128,384]{1,0:T(8,128)(2,1)S(1)}, f32[16,768]{1,0:T(8,128)S(1)}, f32[16,768]{1,0:T(8,128)S(1)}, f32[3,768]{1,0:T(4,128)S(1)}) custom-call(bf16[128,768]{1,0:T(8,128)(2,1)S(1)} %get-tuple-element.42.up_ref, bf16[128,768]{1,0:T(8,128)(2,1)S(1)} %get-tuple-element.43.gmp_ref, ...), custom_call_target="tpu_custom_call" | custom-call | flops 150994944 | bytes 1179648 | tf_op jit(solution)/shard_map/first/pallas_call | solution.py:60
  14.6 1.3 %collective-permute-done.3 = bf16[128,384]{1,0:T(8,128)(2,1)S(1)} collective-permute-done((bf16[128,384]{1,0:T(8,128)(2,1)S(1)}, bf16[128,384]{1,0:T(8,128)(2,1)S(1)}, u32[]{:S(2)}, u32[]{:S(2)}) %collective-permute-start.3) | collective-permute-done | bytes 98336 | tf_op jit(solution)/shard_map/ppermute | solution.py:31
  15.9 1.6 %collective-permute-start.4 = (bf16[128,384]{1,0:T(8,128)(2,1)S(1)}, bf16[128,384]{1,0:T(8,128)(2,1)S(1)}, u32[]{:S(2)}, u32[]{:S(2)}) collective-permute-start(bf16[128,384]{1,0:T(8,128)(2,1)S(1)} %add_convert_fusion.kept_ref), channel_id=1, source_target_pairs={{0,2},{2,0},{1,3},{3,1},{4,6},{6,4},{5,7},{7,5},{8,10},{10,8},{9,1... | collective-permute-start | bytes 294920 | tf_op jit(solution)/shard_map/ppermute | solution.py:31
  17.5 0.7 %first_parameters.1 = (f32[32,768]{1,0:T(8,128)S(1)}, f32[1,768]{1,0:T(1,128)S(1)}) custom-call(bf16[128,768]{1,0:T(8,128)(2,1)S(1)} %get-tuple-element.42.up_ref, bf16[128,768]{1,0:T(8,128)(2,1)S(1)} %get-tuple-element.43.gmp_ref, bf16[128,32]{1,0:T(8,128)(2,1)S(1)} %get-tuple-element.44.coef_ref, f32[8,768]{1,0:T(8,128)S(1)} %get-tuple-element.45.after_ref.table_ref, ...), custom_call_target="tpu_custom_call" | custom-call | flops 37748736 | bytes 393216 | tf_op jit(solution)/shard_map/first_parameters/pallas_call | solution.py:60
  18.6 2.3 %collective-permute-done.4.mine_ref = bf16[128,384]{1,0:T(8,128)(2,1)S(1)} collective-permute-done((bf16[128,384]{1,0:T(8,128)(2,1)S(1)}, bf16[128,384]{1,0:T(8,128)(2,1)S(1)}, u32[]{:S(2)}, u32[]{:S(2)}) %collective-permute-start.4) | collective-permute-done | bytes 98336 | tf_op jit(solution)/shard_map/ppermute | solution.py:31
  20.8 1.3 %collective-permute-done.5.other_ref = bf16[128,384]{1,0:T(8,128)(2,1)S(1)} collective-permute-done((bf16[128,384]{1,0:T(8,128)(2,1)S(1)}, bf16[128,384]{1,0:T(8,128)(2,1)S(1)}, u32[]{:S(2)}, u32[]{:S(2)}) %collective-permute-start.5) | collective-permute-done | bytes 98336 | tf_op jit(solution)/shard_map/ppermute | solution.py:31
  22.6 1.5 %collective-permute-start.8 = (bf16[16,768]{1,0:T(8,128)(2,1)S(1)}, bf16[16,768]{1,0:T(8,128)(2,1)S(1)}, u32[]{:S(2)}, u32[]{:S(2)}) collective-permute-start(bf16[16,768]{1,0:T(8,128)(2,1)S(1)} %get-tuple-element.66), channel_id=1, source_target_pairs={{0,12},{4,8},{8,4},{12,0},{1,13},{5,9},{9,5},{13,1},{2,14},{6,10},... | collective-permute-start | bytes 73736 | tf_op jit(solution)/shard_map/ppermute | solution.py:36
  24.1 0.6 %collective-permute-start.7 = (bf16[16,768]{1,0:T(8,128)(2,1)S(1)}, bf16[16,768]{1,0:T(8,128)(2,1)S(1)}, u32[]{:S(2)}, u32[]{:S(2)}) collective-permute-start(bf16[16,768]{1,0:T(8,128)(2,1)S(1)} %get-tuple-element.66), channel_id=1, source_target_pairs={{0,8},{4,12},{8,0},{12,4},{1,9},{5,13},{9,1},{13,5},{2,10},{6,14},... | collective-permute-start | bytes 73736 | tf_op jit(solution)/shard_map/ppermute | solution.py:36
  24.7 2.3 %collective-permute-start.6 = (bf16[16,768]{1,0:T(8,128)(2,1)S(1)}, bf16[16,768]{1,0:T(8,128)(2,1)S(1)}, u32[]{:S(2)}, u32[]{:S(2)}) collective-permute-start(bf16[16,768]{1,0:T(8,128)(2,1)S(1)} %get-tuple-element.66), channel_id=1, source_target_pairs={{0,4},{4,0},{8,12},{12,8},{1,5},{5,1},{9,13},{13,9},{2,6},{6,2},{1... | collective-permute-start | bytes 73736 | tf_op jit(solution)/shard_map/ppermute | solution.py:36
  27.0 0.8 %local.3 = (f32[128,768]{1,0:T(8,128)S(1)}, f32[128,32]{1,0:T(8,128)S(1)}, f32[1,768]{1,0:T(1,128)S(1)}) custom-call(bf16[128,768]{1,0:T(8,128)(2,1)S(1)} %get-tuple-element.42.up_ref, bf16[128,768]{1,0:T(8,128)(2,1)S(1)} %get-tuple-element.62.gmp_ref, bf16[128,32]{1,0:T(8,128)(2,1)S(1)} %get-tuple-element.44.coef_ref), custom_call_target="tpu_custom_call" | custom-call | flops 150994944 | bytes 393216 | tf_op jit(solution)/shard_map/local/pallas_call | solution.py:60
  27.8 0.6 %collective-permute-done.8.refs_2_ = bf16[16,768]{1,0:T(8,128)(2,1)S(1)} collective-permute-done((bf16[16,768]{1,0:T(8,128)(2,1)S(1)}, bf16[16,768]{1,0:T(8,128)(2,1)S(1)}, u32[]{:S(2)}, u32[]{:S(2)}) %collective-permute-start.8) | collective-permute-done | bytes 24608 | tf_op jit(solution)/shard_map/ppermute | solution.py:36
  31.0 2.4 %collective-permute-start.13 = (bf16[40,384]{1,0:T(8,128)(2,1)S(1)}, bf16[40,384]{1,0:T(8,128)(2,1)S(1)}, u32[]{:S(2)}, u32[]{:S(2)}) collective-permute-start(bf16[40,384]{1,0:T(8,128)(2,1)S(1)} %pair.1.refs_0_), channel_id=1, source_target_pairs={{0,12},{4,8},{8,4},{12,0},{1,13},{5,9},{9,5},{13,1},{2,14},{6,10},... | collective-permute-start | bytes 92168 | tf_op jit(solution)/shard_map/ppermute | solution.py:36
  33.4 0.9 %collective-permute-start.12 = (bf16[40,384]{1,0:T(8,128)(2,1)S(1)}, bf16[40,384]{1,0:T(8,128)(2,1)S(1)}, u32[]{:S(2)}, u32[]{:S(2)}) collective-permute-start(bf16[40,384]{1,0:T(8,128)(2,1)S(1)} %pair.1.refs_0_), channel_id=1, source_target_pairs={{0,8},{4,12},{8,0},{12,4},{1,9},{5,13},{9,1},{13,5},{2,10},{6,14},... | collective-permute-start | bytes 92168 | tf_op jit(solution)/shard_map/ppermute | solution.py:36
  34.3 1.1 %collective-permute-start.11 = (bf16[40,384]{1,0:T(8,128)(2,1)S(1)}, bf16[40,384]{1,0:T(8,128)(2,1)S(1)}, u32[]{:S(2)}, u32[]{:S(2)}) collective-permute-start(bf16[40,384]{1,0:T(8,128)(2,1)S(1)} %pair.1.refs_0_), channel_id=1, source_target_pairs={{0,4},{4,0},{8,12},{12,8},{1,5},{5,1},{9,13},{13,9},{2,6},{6,2},{1... | collective-permute-start | bytes 92168 | tf_op jit(solution)/shard_map/ppermute | solution.py:36
  35.4 0.8 %output.1 = bf16[1,128,768]{2,1,0:T(8,128)(2,1)} custom-call(bf16[128,768]{1,0:T(8,128)(2,1)S(1)} %last_input.1.part_ref, bf16[128,768]{1,0:T(8,128)(2,1)S(1)} %collective-permute-done.10.part2_ref, bf16[128,384]{1,0:T(8,128)(2,1)S(1)} %collective-permute-done.4.mine_ref, bf16[128,384]{1,0:T(8,128)(2,1)S(1)} %collective-permute-done.5.other_ref), custom_call_target="tpu_custom_call" | custom-call | tf_op jit(solution)/shard_map/output/pallas_call | solution.py:60
  36.2 1.0 %collective-permute-done.13.refs_3_ = bf16[40,384]{1,0:T(8,128)(2,1)S(1)} collective-permute-done((bf16[40,384]{1,0:T(8,128)(2,1)S(1)}, bf16[40,384]{1,0:T(8,128)(2,1)S(1)}, u32[]{:S(2)}, u32[]{:S(2)}) %collective-permute-start.13) | collective-permute-done | bytes 30752 | tf_op jit(solution)/shard_map/ppermute | solution.py:36
  37.2 1.1 %collective-permute-done.12.refs_2_ = bf16[40,384]{1,0:T(8,128)(2,1)S(1)} collective-permute-done((bf16[40,384]{1,0:T(8,128)(2,1)S(1)}, bf16[40,384]{1,0:T(8,128)(2,1)S(1)}, u32[]{:S(2)}, u32[]{:S(2)}) %collective-permute-start.12) | collective-permute-done | bytes 30752 | tf_op jit(solution)/shard_map/ppermute | solution.py:36
  39.2 0.6 %collective-permute-done.14.other_ref = f32[32,384]{1,0:T(8,128)S(1)} collective-permute-done((f32[32,384]{1,0:T(8,128)S(1)}, f32[32,384]{1,0:T(8,128)S(1)}, u32[]{:S(2)}, u32[]{:S(2)}) %collective-permute-start.14) | collective-permute-done | bytes 49184 | tf_op jit(solution)/shard_map/ppermute | solution.py:31
  39.8 0.7 %join.1 = f32[1,32,768]{2,1,0:T(8,128)} custom-call(f32[32,384]{1,0:T(8,128)S(1)} %get-tuple-element.79.mine_ref, f32[32,384]{1,0:T(8,128)S(1)} %collective-permute-done.14.other_ref), custom_call_target="tpu_custom_call" | custom-call | tf_op jit(solution)/shard_map/join/pallas_call | solution.py:60
  (33 shorter events, 4.7 us)
Async XLA Ops:
  0.6 8.8 %copy-start.1 = (bf16[1,768,768]{2,1,0:T(8,128)(2,1)S(1)}, bf16[1,768,768]{2,1,0:T(8,128)(2,1)}, u32[]{:S(2)}) copy-start(bf16[1,768,768]{2,1,0:T(8,128)(2,1)} %w_ref.2) | copy-start | bytes 3538948
  3.7 7.0 %collective-permute-start = (bf16[16,896]{1,0:T(8,128)(2,1)S(1)}, bf16[16,896]{1,0:T(8,128)(2,1)S(1)}, u32[]{:S(2)}, u32[]{:S(2)}) collective-permute-start(bf16[16,896]{1,0:T(8,128)(2,1)S(1)} %get-tuple-element.49), channel_id=1, source_target_pairs={{0,12},{4,8},{8,4},{12,0},{1,13},{5,9},{9,5},{13,1},{2,14},{6,10},... | collective-permute-start | bytes 86024 | tf_op jit(solution)/shard_map/ppermute | solution.py:36
  8.8 4.8 %collective-permute-start.1 = (bf16[16,896]{1,0:T(8,128)(2,1)S(1)}, bf16[16,896]{1,0:T(8,128)(2,1)S(1)}, u32[]{:S(2)}, u32[]{:S(2)}) collective-permute-start(bf16[16,896]{1,0:T(8,128)(2,1)S(1)} %get-tuple-element.50), channel_id=1, source_target_pairs={{0,8},{4,12},{8,0},{12,4},{1,9},{5,13},{9,1},{13,5},{2,10},{6,14},... | collective-permute-start | bytes 86024 | tf_op jit(solution)/shard_map/ppermute | solution.py:36
  8.8 4.8 %collective-permute-start.2 = (bf16[16,896]{1,0:T(8,128)(2,1)S(1)}, bf16[16,896]{1,0:T(8,128)(2,1)S(1)}, u32[]{:S(2)}, u32[]{:S(2)}) collective-permute-start(bf16[16,896]{1,0:T(8,128)(2,1)S(1)} %get-tuple-element.51), channel_id=1, source_target_pairs={{0,4},{4,0},{8,12},{12,8},{1,5},{5,1},{9,13},{13,9},{2,6},{6,2},{1... | collective-permute-start | bytes 86024 | tf_op jit(solution)/shard_map/ppermute | solution.py:36
  9.5 4.1 %copy-start.3 = (bf16[128,768]{1,0:T(8,128)(2,1)S(1)}, bf16[128,768]{1,0:T(8,128)(2,1)}, u32[]{:S(2)}) copy-start(bf16[128,768]{1,0:T(8,128)(2,1)} %g_ref.1) | copy-start | bytes 589828
  9.5 4.1 %copy-start.4 = (bf16[1,768,32]{1,2,0:T(8,128)(2,1)S(1)}, bf16[1,768,32]{1,2,0:T(8,128)(2,1)}, u32[]{:S(2)}) copy-start(bf16[1,768,32]{1,2,0:T(8,128)(2,1)} %param.10) | copy-start | bytes 147460
  13.6 3.9 %copy-start.2 = (bf16[1,128,768]{2,1,0:T(8,128)(2,1)S(1)}, bf16[1,128,768]{2,1,0:T(8,128)(2,1)}, u32[]{:S(2)}) copy-start(bf16[1,128,768]{2,1,0:T(8,128)(2,1)} %x_ref.3) | copy-start | bytes 589828
  14.5 3.7 %copy-start = (bf16[1,768,768]{2,1,0:T(8,128)(2,1)S(1)}, bf16[1,768,768]{2,1,0:T(8,128)(2,1)}, u32[]{:S(2)}) copy-start(bf16[1,768,768]{2,1,0:T(8,128)(2,1)} %w_ref.3) | copy-start | bytes 3538948
  14.5 1.4 %collective-permute-start.3 = (bf16[128,384]{1,0:T(8,128)(2,1)S(1)}, bf16[128,384]{1,0:T(8,128)(2,1)S(1)}, u32[]{:S(2)}, u32[]{:S(2)}) collective-permute-start(bf16[128,384]{1,0:T(8,128)(2,1)S(1)} %get-tuple-element.53), channel_id=1, source_target_pairs={{0,1},{1,0},{2,3},{3,2},{4,5},{5,4},{6,7},{7,6},{8,9},{9,8},{10,11... | collective-permute-start | bytes 294920 | tf_op jit(solution)/shard_map/ppermute | solution.py:31
  15.9 4.9 %collective-permute-start.4 = (bf16[128,384]{1,0:T(8,128)(2,1)S(1)}, bf16[128,384]{1,0:T(8,128)(2,1)S(1)}, u32[]{:S(2)}, u32[]{:S(2)}) collective-permute-start(bf16[128,384]{1,0:T(8,128)(2,1)S(1)} %add_convert_fusion.kept_ref), channel_id=1, source_target_pairs={{0,2},{2,0},{1,3},{3,1},{4,6},{6,4},{5,7},{7,5},{8,10},{10,8},{9,1... | collective-permute-start | bytes 294920 | tf_op jit(solution)/shard_map/ppermute | solution.py:31
  20.8 1.3 %collective-permute-start.5 = (bf16[128,384]{1,0:T(8,128)(2,1)S(1)}, bf16[128,384]{1,0:T(8,128)(2,1)S(1)}, u32[]{:S(2)}, u32[]{:S(2)}) collective-permute-start(bf16[128,384]{1,0:T(8,128)(2,1)S(1)} %collective-permute-done.4.mine_ref), channel_id=1, source_target_pairs={{0,1},{1,0},{2,3},{3,2},{4,5},{5,4},{6,7},{7,6},{8,9},{9,8},{10,11... | collective-permute-start | bytes 294920 | tf_op jit(solution)/shard_map/ppermute | solution.py:31
  22.6 5.9 %collective-permute-start.8 = (bf16[16,768]{1,0:T(8,128)(2,1)S(1)}, bf16[16,768]{1,0:T(8,128)(2,1)S(1)}, u32[]{:S(2)}, u32[]{:S(2)}) collective-permute-start(bf16[16,768]{1,0:T(8,128)(2,1)S(1)} %get-tuple-element.66), channel_id=1, source_target_pairs={{0,12},{4,8},{8,4},{12,0},{1,13},{5,9},{9,5},{13,1},{2,14},{6,10},... | collective-permute-start | bytes 73736 | tf_op jit(solution)/shard_map/ppermute | solution.py:36
  24.1 4.7 %collective-permute-start.7 = (bf16[16,768]{1,0:T(8,128)(2,1)S(1)}, bf16[16,768]{1,0:T(8,128)(2,1)S(1)}, u32[]{:S(2)}, u32[]{:S(2)}) collective-permute-start(bf16[16,768]{1,0:T(8,128)(2,1)S(1)} %get-tuple-element.66), channel_id=1, source_target_pairs={{0,8},{4,12},{8,0},{12,4},{1,9},{5,13},{9,1},{13,5},{2,10},{6,14},... | collective-permute-start | bytes 73736 | tf_op jit(solution)/shard_map/ppermute | solution.py:36
  24.7 4.3 %collective-permute-start.6 = (bf16[16,768]{1,0:T(8,128)(2,1)S(1)}, bf16[16,768]{1,0:T(8,128)(2,1)S(1)}, u32[]{:S(2)}, u32[]{:S(2)}) collective-permute-start(bf16[16,768]{1,0:T(8,128)(2,1)S(1)} %get-tuple-element.66), channel_id=1, source_target_pairs={{0,4},{4,0},{8,12},{12,8},{1,5},{5,1},{9,13},{13,9},{2,6},{6,2},{1... | collective-permute-start | bytes 73736 | tf_op jit(solution)/shard_map/ppermute | solution.py:36
  29.5 1.3 %collective-permute-start.9 = (bf16[32,384]{1,0:T(8,128)(2,1)S(1)}, bf16[32,384]{1,0:T(8,128)(2,1)S(1)}, u32[]{:S(2)}, u32[]{:S(2)}) collective-permute-start(bf16[32,384]{1,0:T(8,128)(2,1)S(1)} %get-tuple-element.71), channel_id=1, source_target_pairs={{0,1},{1,0},{2,3},{3,2},{4,5},{5,4},{6,7},{7,6},{8,9},{9,8},{10,11... | collective-permute-start | bytes 73736 | tf_op jit(solution)/shard_map/ppermute | solution.py:31
  30.8 4.6 %collective-permute-start.10 = (bf16[128,768]{1,0:T(8,128)(2,1)S(1)}, bf16[128,768]{1,0:T(8,128)(2,1)S(1)}, u32[]{:S(2)}, u32[]{:S(2)}) collective-permute-start(bf16[128,768]{1,0:T(8,128)(2,1)S(1)} %last_input.1.part_ref), channel_id=1, source_target_pairs={{0,1},{1,0},{2,3},{3,2},{4,5},{5,4},{6,7},{7,6},{8,9},{9,8},{10,11... | collective-permute-start | bytes 589832 | tf_op jit(solution)/shard_map/ppermute | solution.py:31
  31.0 6.1 %collective-permute-start.13 = (bf16[40,384]{1,0:T(8,128)(2,1)S(1)}, bf16[40,384]{1,0:T(8,128)(2,1)S(1)}, u32[]{:S(2)}, u32[]{:S(2)}) collective-permute-start(bf16[40,384]{1,0:T(8,128)(2,1)S(1)} %pair.1.refs_0_), channel_id=1, source_target_pairs={{0,12},{4,8},{8,4},{12,0},{1,13},{5,9},{9,5},{13,1},{2,14},{6,10},... | collective-permute-start | bytes 92168 | tf_op jit(solution)/shard_map/ppermute | solution.py:36
  33.4 4.8 %collective-permute-start.12 = (bf16[40,384]{1,0:T(8,128)(2,1)S(1)}, bf16[40,384]{1,0:T(8,128)(2,1)S(1)}, u32[]{:S(2)}, u32[]{:S(2)}) collective-permute-start(bf16[40,384]{1,0:T(8,128)(2,1)S(1)} %pair.1.refs_0_), channel_id=1, source_target_pairs={{0,8},{4,12},{8,0},{12,4},{1,9},{5,13},{9,1},{13,5},{2,10},{6,14},... | collective-permute-start | bytes 92168 | tf_op jit(solution)/shard_map/ppermute | solution.py:36
  34.3 4.2 %collective-permute-start.11 = (bf16[40,384]{1,0:T(8,128)(2,1)S(1)}, bf16[40,384]{1,0:T(8,128)(2,1)S(1)}, u32[]{:S(2)}, u32[]{:S(2)}) collective-permute-start(bf16[40,384]{1,0:T(8,128)(2,1)S(1)} %pair.1.refs_0_), channel_id=1, source_target_pairs={{0,4},{4,0},{8,12},{12,8},{1,5},{5,1},{9,13},{13,9},{2,6},{6,2},{1... | collective-permute-start | bytes 92168 | tf_op jit(solution)/shard_map/ppermute | solution.py:36
  38.5 1.3 %collective-permute-start.14 = (f32[32,384]{1,0:T(8,128)S(1)}, f32[32,384]{1,0:T(8,128)S(1)}, u32[]{:S(2)}, u32[]{:S(2)}) collective-permute-start(f32[32,384]{1,0:T(8,128)S(1)} %get-tuple-element.79.mine_ref), channel_id=1, source_target_pairs={{0,1},{1,0},{2,3},{3,2},{4,5},{5,4},{6,7},{7,6},{8,9},{9,8},{10,11... | collective-permute-start | bytes 147464 | tf_op jit(solution)/shard_map/ppermute | solution.py:31

commit v5 on v4

--- a/solution.py
+++ b/solution.py
@@ -194,7 +194,8 @@
     return jnp.concatenate([mm(gs, c_part, TN), mm(gs, b_part, NN)], axis=1)
 
 
-def local_kernel(up_ref, gmp_ref, coef_ref, gu_ref, gcoef_ref, lag_ref):
+def local_kernel(up_ref, gmp_ref, coef_ref, *refs):
+    hpp_refs, (gu_ref, gcoef_ref, lag_ref) = refs[:-3], refs[-3:]
     tokens = up_ref.shape[0]
     states = coef_ref.shape[1] // 2
     up, gmp = up_ref[...], gmp_ref[...]
@@ -207,7 +208,10 @@
     lagged = (scores * (t - s).astype(F32)).astype(BF16)
     lag_ref[...] = jnp.sum(gmp.astype(F32) * mm(lagged, up, NN), axis=0, keepdims=True)
     gs = jnp.where(causal, mm(gmp, up, NT), 0.0).astype(BF16)
-    gcoef_ref[...] = coef_grads(gs, b_part, c_part)
+    gcoef = coef_grads(gs, b_part, c_part)
+    for hpp_ref in hpp_refs:
+        gcoef = gcoef + mm(gmp, state_rows(hpp_ref[...]), NT)
+    gcoef_ref[...] = gcoef
 
 
 def unpack(seq_size, recv_refs, table_ref, states, tokens):
@@ -348,11 +352,9 @@
     last,
     seq_size,
     up_ref,
-    gmp_ref,
     table_ref,
     x_ref,
     gcoef_in_ref,
-    hpp_ref,
     weight_ref,
     kept_ref,
     *refs,
@@ -362,7 +364,7 @@
     adj_ref[...] = adj
     rows = adjoint_rows(adj, table_ref)
     rows_ref[...] = rows
-    gcoef = coef_total(rows, state_rows(hpp_ref[...]), gcoef_in_ref, up_ref[...], gmp_ref[...])
+    gcoef = (gcoef_in_ref[...] + mm(up_ref[...], rows, NT)).astype(BF16)
     gcoef_ref[...] = gcoef
     dw = mm(gcoef, x_ref[0], TN)
     if not last:
@@ -416,18 +418,22 @@
     part_ref[...] = jnp.where(lax.axis_index("section") == 0, back.astype(BF16), done)
 
 
-def scaled_gradient(g, w_out_ref, coef, a_ref, table_ref):
-    gmp = (a_ref[...] * mm(g, w_out_ref[...], NN)).astype(BF16)
-    states = coef.shape[1] // 2
-    adjoint = table_ref[EMID : EMID + 1, :] * mm(coef, gmp, TN)[states:, :]
-    return gmp, adjoint
+def half_product(g_ref, w_ref, which):
+    half = g_ref.shape[1]
+    return mm(g_ref[...], w_ref[pl.ds(pl.multiple_of(which * half, half), half), :], NN)
+
+
+def near_kernel(w_out_ref, mine_ref, near_ref):
+    near_ref[...] = half_product(mine_ref, w_out_ref, lax.axis_index("mp"))
 
 
 def hop_kernel(
-    w_out_ref, coef_ref, a_ref, table_ref, mine_ref, other_ref, gmp_ref, adjoint_ref
-):
-    g = joined(mine_ref[...], other_ref[...])
-    gmp, adjoint = scaled_gradient(g, w_out_ref, coef_ref[...], a_ref, table_ref)
+    w_out_ref, coef_ref, a_ref, table_ref, near_ref, other_ref, gmp_ref, adjoint_ref
+):
+    gm = near_ref[...] + half_product(other_ref, w_out_ref, 1 - lax.axis_index("mp"))
+    gmp = (a_ref[...] * gm).astype(BF16)
+    states = coef_ref.shape[1] // 2
+    adjoint = table_ref[EMID : EMID + 1, :] * mm(coef_ref[...], gmp, TN)[states:, :]
     gmp_ref[...] = gmp
     adjoint_ref[...] = adjoint.astype(BF16)
 
@@ -519,11 +525,11 @@
     )
     recv = [partner(pay[k - 1], "seq", k) for k in ORDERS[0](seq_size)]
 
-    def local(gradient):
+    def local(gradient, *state_in):
         return call(
             local_kernel,
             [vec, few, row],
-            [up, gradient, coef],
+            [up, gradient, coef, *state_in],
             flops=big,
             bytes_accessed=4 * tokens * channels,
             name="local",
@@ -571,22 +577,23 @@
                 (mine, kept_dw, kept_rate, w_out_t)
             )
         other = swap(mine, "mp")
+        (near,) = call(near_kernel, [vec], [w_out_t, mine], name="near")
         gmp, adjoint = call(
             hop_kernel,
             [low, ((states, channels), BF16)],
-            [w_out_t, coef, a, table, mine, other],
+            [w_out_t, coef, a, table, near, other],
             flops=big,
             bytes_accessed=2 * width * channels,
             name="hop",
         )
         recv = [partner(adjoint, "seq", k) for k in ORDERS[1](seq_size)]
-        gu, gcoef, lag = local(gmp)
+        gu, gcoef, lag = local(gmp, hpp)
         last = moment == sections - 1
         adj, rows, gcoef, *dw = call(
             functools.partial(parameter_kernel, last, seq_size),
             [state, ((coefs, channels), BF16), ((tokens, coefs), BF16)]
             + ([((coefs, half), F32), ((coefs, half), BF16)] if last else [wide]),
-            [up, gmp, table, section_inputs, gcoef, hpp, weight, kept_dw, *recv],
+            [up, table, section_inputs, gcoef, weight, kept_dw, *recv],
             flops=big // 4,
             bytes_accessed=4 * tokens * channels,
             name="parameters",

time: 40.6 us -> 40.5 us (level)
    pallas_call x16 -> x17, Pallas kernels: 10.8 us -> 10.9 us  [call(): pl.pallas_call(kernel, out_shape=[jax.ShapeDtypeStruct(s, d) for s, d in...]
  transfers between devices with their start and end apart: 15 -> 15, of which waited for: 12 -> 12; matrix products, arithmetic and copies ran while one was open for 0% -> 0% of each run, Pallas kernels for 13% -> 14%
where the time goes in v5:
time: 40.5 us; the launch traced here: 40.4 us
  starting transfers between devices  16.6 us (41%)
  waiting for transfers between devices  12 us (30%)
  Pallas kernels  10.9 us (27%)
  between operations  0.8 us (2%)
    ppermute x9, starting transfers between devices, partner(): return lax.ppermute(value, axis, [(i, i ^ k) for i in range(n)])  14.6 us
    pallas_call x17, Pallas kernels, call(): pl.pallas_call(kernel, out_shape=[jax.ShapeDtypeStruct(s, d) for s, d in...  10.9 us
    ppermute x9, waiting for transfers between devices, partner(): return lax.ppermute(value, axis, [(i, i ^ k) for i in range(n)])  6.41 us
    ppermute x6, waiting for transfers between devices, rotate(): return lax.ppermute(value, axis, [(i, (i + by) % n) for i in range(n)])  5.55 us
    ppermute x6, starting transfers between devices, rotate(): return lax.ppermute(value, axis, [(i, (i + by) % n) for i in range(n)])  2 us
  transfers between devices with their start and end apart: 15, of which 12 were waited for; matrix products, arithmetic and copies ran while one was open for 0% of the time, Pallas kernels for 14%

profile of v5, /device:TPU:0, one launch (start us, length us, event | category | flops | bytes accessed | tf_op | source)
XLA Modules:
  0.0 40.4 jit_solution(17158305303670969685)
XLA Ops:
  0.6 3.1 %start.1 = (bf16[128,768]{1,0:T(8,128)(2,1)S(1)}, bf16[128,768]{1,0:T(8,128)(2,1)S(1)}, bf16[128,32]{1,0:T(8,128)(2,1)S(1)}, f32[128,768]{1,0:T(8,128)S(1)}, f32...) custom-call(bf16[1,128,768]{2,1,0:T(8,128)(2,1)} %x_ref.3, ...), custom_call_target="tpu_custom_call" | custom-call | flops 301989888 | bytes 2359296 | tf_op jit(solution)/shard_map/start/pallas_call | solution.py:60
  3.7 5.1 %collective-permute-start = (bf16[16,896]{1,0:T(8,128)(2,1)S(1)}, bf16[16,896]{1,0:T(8,128)(2,1)S(1)}, u32[]{:S(2)}, u32[]{:S(2)}) collective-permute-start(bf16[16,896]{1,0:T(8,128)(2,1)S(1)} %get-tuple-element.49), channel_id=1, source_target_pairs={{0,12},{4,8},{8,4},{12,0},{1,13},{5,9},{9,5},{13,1},{2,14},{6,10},... | collective-permute-start | bytes 86024 | tf_op jit(solution)/shard_map/ppermute | solution.py:36
  8.8 0.6 %collective-permute-start.2 = (bf16[16,896]{1,0:T(8,128)(2,1)S(1)}, bf16[16,896]{1,0:T(8,128)(2,1)S(1)}, u32[]{:S(2)}, u32[]{:S(2)}) collective-permute-start(bf16[16,896]{1,0:T(8,128)(2,1)S(1)} %get-tuple-element.51), channel_id=1, source_target_pairs={{0,4},{4,0},{8,12},{12,8},{1,5},{5,1},{9,13},{13,9},{2,6},{6,2},{1... | collective-permute-start | bytes 86024 | tf_op jit(solution)/shard_map/ppermute | solution.py:36
  9.8 0.8 %local.2 = (f32[128,768]{1,0:T(8,128)S(1)}, f32[128,32]{1,0:T(8,128)S(1)}, f32[1,768]{1,0:T(1,128)S(1)}) custom-call(bf16[128,768]{1,0:T(8,128)(2,1)S(1)} %get-tuple-element.42.up_ref, bf16[128,768]{1,0:T(8,128)(2,1)S(1)} %get-tuple-element.44.gmp_ref, bf16[128,32]{1,0:T(8,128)(2,1)S(1)} %get-tuple-element.45.coef_ref), custom_call_target="tpu_custom_call" | custom-call | flops 150994944 | bytes 393216 | tf_op jit(solution)/shard_map/local/pallas_call | solution.py:60
  10.7 2.9 %collective-permute-done.1.refs_1_ = bf16[16,896]{1,0:T(8,128)(2,1)S(1)} collective-permute-done((bf16[16,896]{1,0:T(8,128)(2,1)S(1)}, bf16[16,896]{1,0:T(8,128)(2,1)S(1)}, u32[]{:S(2)}, u32[]{:S(2)}) %collective-permute-start.1) | collective-permute-done | bytes 28704 | tf_op jit(solution)/shard_map/ppermute | solution.py:36
  13.6 0.9 %first.1 = (f32[128,384]{1,0:T(8,128)S(1)}, bf16[128,384]{1,0:T(8,128)(2,1)S(1)}, f32[16,768]{1,0:T(8,128)S(1)}, f32[16,768]{1,0:T(8,128)S(1)}, f32[3,768]{1,0:T(4,128)S(1)}) custom-call(bf16[128,768]{1,0:T(8,128)(2,1)S(1)} %get-tuple-element.42.up_ref, bf16[128,768]{1,0:T(8,128)(2,1)S(1)} %get-tuple-element.44.gmp_ref, ...), custom_call_target="tpu_custom_call" | custom-call | flops 150994944 | bytes 1179648 | tf_op jit(solution)/shard_map/first/pallas_call | solution.py:60
  14.6 1.3 %collective-permute-done.3 = bf16[128,384]{1,0:T(8,128)(2,1)S(1)} collective-permute-done((bf16[128,384]{1,0:T(8,128)(2,1)S(1)}, bf16[128,384]{1,0:T(8,128)(2,1)S(1)}, u32[]{:S(2)}, u32[]{:S(2)}) %collective-permute-start.3) | collective-permute-done | bytes 98336 | tf_op jit(solution)/shard_map/ppermute | solution.py:31
  15.9 1.6 %collective-permute-start.4 = (bf16[128,384]{1,0:T(8,128)(2,1)S(1)}, bf16[128,384]{1,0:T(8,128)(2,1)S(1)}, u32[]{:S(2)}, u32[]{:S(2)}) collective-permute-start(bf16[128,384]{1,0:T(8,128)(2,1)S(1)} %add_convert_fusion.kept_ref), channel_id=1, source_target_pairs={{0,2},{2,0},{1,3},{3,1},{4,6},{6,4},{5,7},{7,5},{8,10},{10,8},{9,1... | collective-permute-start | bytes 294920 | tf_op jit(solution)/shard_map/ppermute | solution.py:31
  17.5 0.7 %first_parameters.1 = (f32[32,768]{1,0:T(8,128)S(1)}, f32[1,768]{1,0:T(1,128)S(1)}) custom-call(bf16[128,768]{1,0:T(8,128)(2,1)S(1)} %get-tuple-element.42.up_ref, bf16[128,768]{1,0:T(8,128)(2,1)S(1)} %get-tuple-element.44.gmp_ref, bf16[128,32]{1,0:T(8,128)(2,1)S(1)} %get-tuple-element.45.coef_ref, f32[8,768]{1,0:T(8,128)S(1)} %get-tuple-element.43.after_ref.table_ref, ...), custom_call_target="tpu_custom_call" | custom-call | flops 37748736 | bytes 393216 | tf_op jit(solution)/shard_map/first_parameters/pallas_call | solution.py:60
  18.6 2.3 %collective-permute-done.4.mine_ref = bf16[128,384]{1,0:T(8,128)(2,1)S(1)} collective-permute-done((bf16[128,384]{1,0:T(8,128)(2,1)S(1)}, bf16[128,384]{1,0:T(8,128)(2,1)S(1)}, u32[]{:S(2)}, u32[]{:S(2)}) %collective-permute-start.4) | collective-permute-done | bytes 98336 | tf_op jit(solution)/shard_map/ppermute | solution.py:31
  21.1 1.0 %collective-permute-done.5.other_ref = bf16[128,384]{1,0:T(8,128)(2,1)S(1)} collective-permute-done((bf16[128,384]{1,0:T(8,128)(2,1)S(1)}, bf16[128,384]{1,0:T(8,128)(2,1)S(1)}, u32[]{:S(2)}, u32[]{:S(2)}) %collective-permute-start.5) | collective-permute-done | bytes 98336 | tf_op jit(solution)/shard_map/ppermute | solution.py:31
  22.5 1.5 %collective-permute-start.8 = (bf16[16,768]{1,0:T(8,128)(2,1)S(1)}, bf16[16,768]{1,0:T(8,128)(2,1)S(1)}, u32[]{:S(2)}, u32[]{:S(2)}) collective-permute-start(bf16[16,768]{1,0:T(8,128)(2,1)S(1)} %get-tuple-element.66), channel_id=1, source_target_pairs={{0,12},{4,8},{8,4},{12,0},{1,13},{5,9},{9,5},{13,1},{2,14},{6,10},... | collective-permute-start | bytes 73736 | tf_op jit(solution)/shard_map/ppermute | solution.py:36
  24.0 0.6 %collective-permute-start.7 = (bf16[16,768]{1,0:T(8,128)(2,1)S(1)}, bf16[16,768]{1,0:T(8,128)(2,1)S(1)}, u32[]{:S(2)}, u32[]{:S(2)}) collective-permute-start(bf16[16,768]{1,0:T(8,128)(2,1)S(1)} %get-tuple-element.66), channel_id=1, source_target_pairs={{0,8},{4,12},{8,0},{12,4},{1,9},{5,13},{9,1},{13,5},{2,10},{6,14},... | collective-permute-start | bytes 73736 | tf_op jit(solution)/shard_map/ppermute | solution.py:36
  24.7 2.3 %collective-permute-start.6 = (bf16[16,768]{1,0:T(8,128)(2,1)S(1)}, bf16[16,768]{1,0:T(8,128)(2,1)S(1)}, u32[]{:S(2)}, u32[]{:S(2)}) collective-permute-start(bf16[16,768]{1,0:T(8,128)(2,1)S(1)} %get-tuple-element.66), channel_id=1, source_target_pairs={{0,4},{4,0},{8,12},{12,8},{1,5},{5,1},{9,13},{13,9},{2,6},{6,2},{1... | collective-permute-start | bytes 73736 | tf_op jit(solution)/shard_map/ppermute | solution.py:36
  27.0 0.8 %local.3 = (f32[128,768]{1,0:T(8,128)S(1)}, f32[128,32]{1,0:T(8,128)S(1)}, f32[1,768]{1,0:T(1,128)S(1)}) custom-call(bf16[128,768]{1,0:T(8,128)(2,1)S(1)} %get-tuple-element.42.up_ref, bf16[128,768]{1,0:T(8,128)(2,1)S(1)} %get-tuple-element.62.gmp_ref, bf16[128,32]{1,0:T(8,128)(2,1)S(1)} %get-tuple-element.45.coef_ref, ...), custom_call_target="tpu_custom_call" | custom-call | flops 150994944 | bytes 393216 | tf_op jit(solution)/shard_map/local/pallas_call | solution.py:60
  27.8 0.6 %collective-permute-done.8.refs_2_ = bf16[16,768]{1,0:T(8,128)(2,1)S(1)} collective-permute-done((bf16[16,768]{1,0:T(8,128)(2,1)S(1)}, bf16[16,768]{1,0:T(8,128)(2,1)S(1)}, u32[]{:S(2)}, u32[]{:S(2)}) %collective-permute-start.8) | collective-permute-done | bytes 24608 | tf_op jit(solution)/shard_map/ppermute | solution.py:36
  30.9 2.4 %collective-permute-start.13 = (bf16[40,384]{1,0:T(8,128)(2,1)S(1)}, bf16[40,384]{1,0:T(8,128)(2,1)S(1)}, u32[]{:S(2)}, u32[]{:S(2)}) collective-permute-start(bf16[40,384]{1,0:T(8,128)(2,1)S(1)} %pair.1.refs_0_), channel_id=1, source_target_pairs={{0,12},{4,8},{8,4},{12,0},{1,13},{5,9},{9,5},{13,1},{2,14},{6,10},... | collective-permute-start | bytes 92168 | tf_op jit(solution)/shard_map/ppermute | solution.py:36
  33.3 0.9 %collective-permute-start.12 = (bf16[40,384]{1,0:T(8,128)(2,1)S(1)}, bf16[40,384]{1,0:T(8,128)(2,1)S(1)}, u32[]{:S(2)}, u32[]{:S(2)}) collective-permute-start(bf16[40,384]{1,0:T(8,128)(2,1)S(1)} %pair.1.refs_0_), channel_id=1, source_target_pairs={{0,8},{4,12},{8,0},{12,4},{1,9},{5,13},{9,1},{13,5},{2,10},{6,14},... | collective-permute-start | bytes 92168 | tf_op jit(solution)/shard_map/ppermute | solution.py:36
  34.2 1.1 %collective-permute-start.11 = (bf16[40,384]{1,0:T(8,128)(2,1)S(1)}, bf16[40,384]{1,0:T(8,128)(2,1)S(1)}, u32[]{:S(2)}, u32[]{:S(2)}) collective-permute-start(bf16[40,384]{1,0:T(8,128)(2,1)S(1)} %pair.1.refs_0_), channel_id=1, source_target_pairs={{0,4},{4,0},{8,12},{12,8},{1,5},{5,1},{9,13},{13,9},{2,6},{6,2},{1... | collective-permute-start | bytes 92168 | tf_op jit(solution)/shard_map/ppermute | solution.py:36
  35.3 0.8 %output.1 = bf16[1,128,768]{2,1,0:T(8,128)(2,1)} custom-call(bf16[128,768]{1,0:T(8,128)(2,1)S(1)} %last_input.1.part_ref, bf16[128,768]{1,0:T(8,128)(2,1)S(1)} %collective-permute-done.10.part2_ref, bf16[128,384]{1,0:T(8,128)(2,1)S(1)} %collective-permute-done.4.mine_ref, bf16[128,384]{1,0:T(8,128)(2,1)S(1)} %collective-permute-done.5.other_ref), custom_call_target="tpu_custom_call" | custom-call | tf_op jit(solution)/shard_map/output/pallas_call | solution.py:60
  36.1 1.0 %collective-permute-done.13.refs_3_ = bf16[40,384]{1,0:T(8,128)(2,1)S(1)} collective-permute-done((bf16[40,384]{1,0:T(8,128)(2,1)S(1)}, bf16[40,384]{1,0:T(8,128)(2,1)S(1)}, u32[]{:S(2)}, u32[]{:S(2)}) %collective-permute-start.13) | collective-permute-done | bytes 30752 | tf_op jit(solution)/shard_map/ppermute | solution.py:36
  37.0 1.1 %collective-permute-done.12.refs_2_ = bf16[40,384]{1,0:T(8,128)(2,1)S(1)} collective-permute-done((bf16[40,384]{1,0:T(8,128)(2,1)S(1)}, bf16[40,384]{1,0:T(8,128)(2,1)S(1)}, u32[]{:S(2)}, u32[]{:S(2)}) %collective-permute-start.12) | collective-permute-done | bytes 30752 | tf_op jit(solution)/shard_map/ppermute | solution.py:36
  39.1 0.6 %collective-permute-done.14.other_ref = f32[32,384]{1,0:T(8,128)S(1)} collective-permute-done((f32[32,384]{1,0:T(8,128)S(1)}, f32[32,384]{1,0:T(8,128)S(1)}, u32[]{:S(2)}, u32[]{:S(2)}) %collective-permute-start.14) | collective-permute-done | bytes 49184 | tf_op jit(solution)/shard_map/ppermute | solution.py:31
  39.7 0.7 %join.1 = f32[1,32,768]{2,1,0:T(8,128)} custom-call(f32[32,384]{1,0:T(8,128)S(1)} %get-tuple-element.79.mine_ref, f32[32,384]{1,0:T(8,128)S(1)} %collective-permute-done.14.other_ref), custom_call_target="tpu_custom_call" | custom-call | tf_op jit(solution)/shard_map/join/pallas_call | solution.py:60
  (34 shorter events, 4.9 us)
Async XLA Ops:
  0.6 8.8 %copy-start.1 = (bf16[1,768,768]{2,1,0:T(8,128)(2,1)S(1)}, bf16[1,768,768]{2,1,0:T(8,128)(2,1)}, u32[]{:S(2)}) copy-start(bf16[1,768,768]{2,1,0:T(8,128)(2,1)} %w_ref.2) | copy-start | bytes 3538948
  3.7 7.0 %collective-permute-start = (bf16[16,896]{1,0:T(8,128)(2,1)S(1)}, bf16[16,896]{1,0:T(8,128)(2,1)S(1)}, u32[]{:S(2)}, u32[]{:S(2)}) collective-permute-start(bf16[16,896]{1,0:T(8,128)(2,1)S(1)} %get-tuple-element.49), channel_id=1, source_target_pairs={{0,12},{4,8},{8,4},{12,0},{1,13},{5,9},{9,5},{13,1},{2,14},{6,10},... | collective-permute-start | bytes 86024 | tf_op jit(solution)/shard_map/ppermute | solution.py:36
  8.8 4.8 %collective-permute-start.1 = (bf16[16,896]{1,0:T(8,128)(2,1)S(1)}, bf16[16,896]{1,0:T(8,128)(2,1)S(1)}, u32[]{:S(2)}, u32[]{:S(2)}) collective-permute-start(bf16[16,896]{1,0:T(8,128)(2,1)S(1)} %get-tuple-element.50), channel_id=1, source_target_pairs={{0,8},{4,12},{8,0},{12,4},{1,9},{5,13},{9,1},{13,5},{2,10},{6,14},... | collective-permute-start | bytes 86024 | tf_op jit(solution)/shard_map/ppermute | solution.py:36
  8.8 4.8 %collective-permute-start.2 = (bf16[16,896]{1,0:T(8,128)(2,1)S(1)}, bf16[16,896]{1,0:T(8,128)(2,1)S(1)}, u32[]{:S(2)}, u32[]{:S(2)}) collective-permute-start(bf16[16,896]{1,0:T(8,128)(2,1)S(1)} %get-tuple-element.51), channel_id=1, source_target_pairs={{0,4},{4,0},{8,12},{12,8},{1,5},{5,1},{9,13},{13,9},{2,6},{6,2},{1... | collective-permute-start | bytes 86024 | tf_op jit(solution)/shard_map/ppermute | solution.py:36
  9.5 4.1 %copy-start.3 = (bf16[128,768]{1,0:T(8,128)(2,1)S(1)}, bf16[128,768]{1,0:T(8,128)(2,1)}, u32[]{:S(2)}) copy-start(bf16[128,768]{1,0:T(8,128)(2,1)} %g_ref.1) | copy-start | bytes 589828
  9.5 4.1 %copy-start.4 = (bf16[1,768,32]{1,2,0:T(8,128)(2,1)S(1)}, bf16[1,768,32]{1,2,0:T(8,128)(2,1)}, u32[]{:S(2)}) copy-start(bf16[1,768,32]{1,2,0:T(8,128)(2,1)} %param.10) | copy-start | bytes 147460
  13.6 3.9 %copy-start.2 = (bf16[1,128,768]{2,1,0:T(8,128)(2,1)S(1)}, bf16[1,128,768]{2,1,0:T(8,128)(2,1)}, u32[]{:S(2)}) copy-start(bf16[1,128,768]{2,1,0:T(8,128)(2,1)} %x_ref.3) | copy-start | bytes 589828
  14.5 3.7 %copy-start = (bf16[1,768,768]{2,1,0:T(8,128)(2,1)S(1)}, bf16[1,768,768]{2,1,0:T(8,128)(2,1)}, u32[]{:S(2)}) copy-start(bf16[1,768,768]{2,1,0:T(8,128)(2,1)} %w_ref.3) | copy-start | bytes 3538948
  14.5 1.4 %collective-permute-start.3 = (bf16[128,384]{1,0:T(8,128)(2,1)S(1)}, bf16[128,384]{1,0:T(8,128)(2,1)S(1)}, u32[]{:S(2)}, u32[]{:S(2)}) collective-permute-start(bf16[128,384]{1,0:T(8,128)(2,1)S(1)} %get-tuple-element.53), channel_id=1, source_target_pairs={{0,1},{1,0},{2,3},{3,2},{4,5},{5,4},{6,7},{7,6},{8,9},{9,8},{10,11... | collective-permute-start | bytes 294920 | tf_op jit(solution)/shard_map/ppermute | solution.py:31
  15.9 4.9 %collective-permute-start.4 = (bf16[128,384]{1,0:T(8,128)(2,1)S(1)}, bf16[128,384]{1,0:T(8,128)(2,1)S(1)}, u32[]{:S(2)}, u32[]{:S(2)}) collective-permute-start(bf16[128,384]{1,0:T(8,128)(2,1)S(1)} %add_convert_fusion.kept_ref), channel_id=1, source_target_pairs={{0,2},{2,0},{1,3},{3,1},{4,6},{6,4},{5,7},{7,5},{8,10},{10,8},{9,1... | collective-permute-start | bytes 294920 | tf_op jit(solution)/shard_map/ppermute | solution.py:31
  20.8 1.3 %collective-permute-start.5 = (bf16[128,384]{1,0:T(8,128)(2,1)S(1)}, bf16[128,384]{1,0:T(8,128)(2,1)S(1)}, u32[]{:S(2)}, u32[]{:S(2)}) collective-permute-start(bf16[128,384]{1,0:T(8,128)(2,1)S(1)} %collective-permute-done.4.mine_ref), channel_id=1, source_target_pairs={{0,1},{1,0},{2,3},{3,2},{4,5},{5,4},{6,7},{7,6},{8,9},{9,8},{10,11... | collective-permute-start | bytes 294920 | tf_op jit(solution)/shard_map/ppermute | solution.py:31
  22.5 5.9 %collective-permute-start.8 = (bf16[16,768]{1,0:T(8,128)(2,1)S(1)}, bf16[16,768]{1,0:T(8,128)(2,1)S(1)}, u32[]{:S(2)}, u32[]{:S(2)}) collective-permute-start(bf16[16,768]{1,0:T(8,128)(2,1)S(1)} %get-tuple-element.66), channel_id=1, source_target_pairs={{0,12},{4,8},{8,4},{12,0},{1,13},{5,9},{9,5},{13,1},{2,14},{6,10},... | collective-permute-start | bytes 73736 | tf_op jit(solution)/shard_map/ppermute | solution.py:36
  24.0 4.7 %collective-permute-start.7 = (bf16[16,768]{1,0:T(8,128)(2,1)S(1)}, bf16[16,768]{1,0:T(8,128)(2,1)S(1)}, u32[]{:S(2)}, u32[]{:S(2)}) collective-permute-start(bf16[16,768]{1,0:T(8,128)(2,1)S(1)} %get-tuple-element.66), channel_id=1, source_target_pairs={{0,8},{4,12},{8,0},{12,4},{1,9},{5,13},{9,1},{13,5},{2,10},{6,14},... | collective-permute-start | bytes 73736 | tf_op jit(solution)/shard_map/ppermute | solution.py:36
  24.7 4.3 %collective-permute-start.6 = (bf16[16,768]{1,0:T(8,128)(2,1)S(1)}, bf16[16,768]{1,0:T(8,128)(2,1)S(1)}, u32[]{:S(2)}, u32[]{:S(2)}) collective-permute-start(bf16[16,768]{1,0:T(8,128)(2,1)S(1)} %get-tuple-element.66), channel_id=1, source_target_pairs={{0,4},{4,0},{8,12},{12,8},{1,5},{5,1},{9,13},{13,9},{2,6},{6,2},{1... | collective-permute-start | bytes 73736 | tf_op jit(solution)/shard_map/ppermute | solution.py:36
  29.4 1.3 %collective-permute-start.9 = (bf16[32,384]{1,0:T(8,128)(2,1)S(1)}, bf16[32,384]{1,0:T(8,128)(2,1)S(1)}, u32[]{:S(2)}, u32[]{:S(2)}) collective-permute-start(bf16[32,384]{1,0:T(8,128)(2,1)S(1)} %get-tuple-element.71), channel_id=1, source_target_pairs={{0,1},{1,0},{2,3},{3,2},{4,5},{5,4},{6,7},{7,6},{8,9},{9,8},{10,11... | collective-permute-start | bytes 73736 | tf_op jit(solution)/shard_map/ppermute | solution.py:31
  30.7 4.6 %collective-permute-start.10 = (bf16[128,768]{1,0:T(8,128)(2,1)S(1)}, bf16[128,768]{1,0:T(8,128)(2,1)S(1)}, u32[]{:S(2)}, u32[]{:S(2)}) collective-permute-start(bf16[128,768]{1,0:T(8,128)(2,1)S(1)} %last_input.1.part_ref), channel_id=1, source_target_pairs={{0,1},{1,0},{2,3},{3,2},{4,5},{5,4},{6,7},{7,6},{8,9},{9,8},{10,11... | collective-permute-start | bytes 589832 | tf_op jit(solution)/shard_map/ppermute | solution.py:31
  30.9 6.1 %collective-permute-start.13 = (bf16[40,384]{1,0:T(8,128)(2,1)S(1)}, bf16[40,384]{1,0:T(8,128)(2,1)S(1)}, u32[]{:S(2)}, u32[]{:S(2)}) collective-permute-start(bf16[40,384]{1,0:T(8,128)(2,1)S(1)} %pair.1.refs_0_), channel_id=1, source_target_pairs={{0,12},{4,8},{8,4},{12,0},{1,13},{5,9},{9,5},{13,1},{2,14},{6,10},... | collective-permute-start | bytes 92168 | tf_op jit(solution)/shard_map/ppermute | solution.py:36
  33.3 4.8 %collective-permute-start.12 = (bf16[40,384]{1,0:T(8,128)(2,1)S(1)}, bf16[40,384]{1,0:T(8,128)(2,1)S(1)}, u32[]{:S(2)}, u32[]{:S(2)}) collective-permute-start(bf16[40,384]{1,0:T(8,128)(2,1)S(1)} %pair.1.refs_0_), channel_id=1, source_target_pairs={{0,8},{4,12},{8,0},{12,4},{1,9},{5,13},{9,1},{13,5},{2,10},{6,14},... | collective-permute-start | bytes 92168 | tf_op jit(solution)/shard_map/ppermute | solution.py:36
  34.2 4.2 %collective-permute-start.11 = (bf16[40,384]{1,0:T(8,128)(2,1)S(1)}, bf16[40,384]{1,0:T(8,128)(2,1)S(1)}, u32[]{:S(2)}, u32[]{:S(2)}) collective-permute-start(bf16[40,384]{1,0:T(8,128)(2,1)S(1)} %pair.1.refs_0_), channel_id=1, source_target_pairs={{0,4},{4,0},{8,12},{12,8},{1,5},{5,1},{9,13},{13,9},{2,6},{6,2},{1... | collective-permute-start | bytes 92168 | tf_op jit(solution)/shard_map/ppermute | solution.py:36
  38.4 1.3 %collective-permute-start.14 = (f32[32,384]{1,0:T(8,128)S(1)}, f32[32,384]{1,0:T(8,128)S(1)}, u32[]{:S(2)}, u32[]{:S(2)}) collective-permute-start(f32[32,384]{1,0:T(8,128)S(1)} %get-tuple-element.79.mine_ref), channel_id=1, source_target_pairs={{0,1},{1,0},{2,3},{3,2},{4,5},{5,4},{6,7},{7,6},{8,9},{9,8},{10,11... | collective-permute-start | bytes 147464 | tf_op jit(solution)/shard_map/ppermute | solution.py:31

commit v6 on v5

--- a/solution.py
+++ b/solution.py
@@ -18,7 +18,11 @@
 
 RATE, EMID, ATOT, INV, COUNT = 0, 1, 2, 3, 4
 TABLE_ROWS = 8
-ORDERS = (lambda n: range(n - 1, 0, -1), lambda n: range(1, n), lambda n: range(1, n))
+ORDERS = (
+    lambda n: range(n - 1, 0, -1),
+    lambda n: range(1, n),
+    lambda n: (2, 1, *range(3, n)),
+)
 OUT_CHUNKS, IN_CHUNKS = 1, 1
 
 

time: 40.5 us -> 40.2 us (level)
  no operation moved by 1% of the time
where the time goes in v6:
time: 40.2 us; the launch traced here: 40.1 us
  starting transfers between devices  16.6 us (41%)
  waiting for transfers between devices  11.7 us (29%)
  Pallas kernels  10.9 us (27%)
  between operations  0.8 us (2%)
    ppermute x9, starting transfers between devices, partner(): return lax.ppermute(value, axis, [(i, i ^ k) for i in range(n)])  14.6 us
    pallas_call x17, Pallas kernels, call(): pl.pallas_call(kernel, out_shape=[jax.ShapeDtypeStruct(s, d) for s, d in...  10.9 us
    ppermute x9, waiting for transfers between devices, partner(): return lax.ppermute(value, axis, [(i, i ^ k) for i in range(n)])  6.13 us
    ppermute x6, waiting for transfers between devices, rotate(): return lax.ppermute(value, axis, [(i, (i + by) % n) for i in range(n)])  5.55 us
    ppermute x6, starting transfers between devices, rotate(): return lax.ppermute(value, axis, [(i, (i + by) % n) for i in range(n)])  2 us
  transfers between devices with their start and end apart: 15, of which 12 were waited for; matrix products, arithmetic and copies ran while one was open for 0% of the time, Pallas kernels for 14%

profile of v6, /device:TPU:0, one launch (start us, length us, event | category | flops | bytes accessed | tf_op | source)
XLA Modules:
  0.0 40.1 jit_solution(3033438952390760750)
XLA Ops:
  0.6 3.1 %start.1 = (bf16[128,768]{1,0:T(8,128)(2,1)S(1)}, bf16[128,768]{1,0:T(8,128)(2,1)S(1)}, bf16[128,32]{1,0:T(8,128)(2,1)S(1)}, f32[128,768]{1,0:T(8,128)S(1)}, f32...) custom-call(bf16[1,128,768]{2,1,0:T(8,128)(2,1)} %x_ref.3, ...), custom_call_target="tpu_custom_call" | custom-call | flops 301989888 | bytes 2359296 | tf_op jit(solution)/shard_map/start/pallas_call | solution.py:64
  3.7 5.1 %collective-permute-start = (bf16[16,896]{1,0:T(8,128)(2,1)S(1)}, bf16[16,896]{1,0:T(8,128)(2,1)S(1)}, u32[]{:S(2)}, u32[]{:S(2)}) collective-permute-start(bf16[16,896]{1,0:T(8,128)(2,1)S(1)} %get-tuple-element.49), channel_id=1, source_target_pairs={{0,12},{4,8},{8,4},{12,0},{1,13},{5,9},{9,5},{13,1},{2,14},{6,10},... | collective-permute-start | bytes 86024 | tf_op jit(solution)/shard_map/ppermute | solution.py:40
  8.8 0.6 %collective-permute-start.2 = (bf16[16,896]{1,0:T(8,128)(2,1)S(1)}, bf16[16,896]{1,0:T(8,128)(2,1)S(1)}, u32[]{:S(2)}, u32[]{:S(2)}) collective-permute-start(bf16[16,896]{1,0:T(8,128)(2,1)S(1)} %get-tuple-element.51), channel_id=1, source_target_pairs={{0,4},{4,0},{8,12},{12,8},{1,5},{5,1},{9,13},{13,9},{2,6},{6,2},{1... | collective-permute-start | bytes 86024 | tf_op jit(solution)/shard_map/ppermute | solution.py:40
  9.8 0.8 %local.2 = (f32[128,768]{1,0:T(8,128)S(1)}, f32[128,32]{1,0:T(8,128)S(1)}, f32[1,768]{1,0:T(1,128)S(1)}) custom-call(bf16[128,768]{1,0:T(8,128)(2,1)S(1)} %get-tuple-element.42.up_ref, bf16[128,768]{1,0:T(8,128)(2,1)S(1)} %get-tuple-element.44.gmp_ref, bf16[128,32]{1,0:T(8,128)(2,1)S(1)} %get-tuple-element.45.coef_ref), custom_call_target="tpu_custom_call" | custom-call | flops 150994944 | bytes 393216 | tf_op jit(solution)/shard_map/local/pallas_call | solution.py:64
  10.7 2.9 %collective-permute-done.1.refs_1_ = bf16[16,896]{1,0:T(8,128)(2,1)S(1)} collective-permute-done((bf16[16,896]{1,0:T(8,128)(2,1)S(1)}, bf16[16,896]{1,0:T(8,128)(2,1)S(1)}, u32[]{:S(2)}, u32[]{:S(2)}) %collective-permute-start.1) | collective-permute-done | bytes 28704 | tf_op jit(solution)/shard_map/ppermute | solution.py:40
  13.6 0.9 %first.1 = (f32[128,384]{1,0:T(8,128)S(1)}, bf16[128,384]{1,0:T(8,128)(2,1)S(1)}, f32[16,768]{1,0:T(8,128)S(1)}, f32[16,768]{1,0:T(8,128)S(1)}, f32[3,768]{1,0:T(4,128)S(1)}) custom-call(bf16[128,768]{1,0:T(8,128)(2,1)S(1)} %get-tuple-element.42.up_ref, bf16[128,768]{1,0:T(8,128)(2,1)S(1)} %get-tuple-element.44.gmp_ref, ...), custom_call_target="tpu_custom_call" | custom-call | flops 150994944 | bytes 1179648 | tf_op jit(solution)/shard_map/first/pallas_call | solution.py:64
  14.6 1.3 %collective-permute-done.3 = bf16[128,384]{1,0:T(8,128)(2,1)S(1)} collective-permute-done((bf16[128,384]{1,0:T(8,128)(2,1)S(1)}, bf16[128,384]{1,0:T(8,128)(2,1)S(1)}, u32[]{:S(2)}, u32[]{:S(2)}) %collective-permute-start.3) | collective-permute-done | bytes 98336 | tf_op jit(solution)/shard_map/ppermute | solution.py:35
  15.9 1.6 %collective-permute-start.4 = (bf16[128,384]{1,0:T(8,128)(2,1)S(1)}, bf16[128,384]{1,0:T(8,128)(2,1)S(1)}, u32[]{:S(2)}, u32[]{:S(2)}) collective-permute-start(bf16[128,384]{1,0:T(8,128)(2,1)S(1)} %add_convert_fusion.kept_ref), channel_id=1, source_target_pairs={{0,2},{2,0},{1,3},{3,1},{4,6},{6,4},{5,7},{7,5},{8,10},{10,8},{9,1... | collective-permute-start | bytes 294920 | tf_op jit(solution)/shard_map/ppermute | solution.py:35
  17.5 0.7 %first_parameters.1 = (f32[32,768]{1,0:T(8,128)S(1)}, f32[1,768]{1,0:T(1,128)S(1)}) custom-call(bf16[128,768]{1,0:T(8,128)(2,1)S(1)} %get-tuple-element.42.up_ref, bf16[128,768]{1,0:T(8,128)(2,1)S(1)} %get-tuple-element.44.gmp_ref, bf16[128,32]{1,0:T(8,128)(2,1)S(1)} %get-tuple-element.45.coef_ref, f32[8,768]{1,0:T(8,128)S(1)} %get-tuple-element.43.after_ref.table_ref, ...), custom_call_target="tpu_custom_call" | custom-call | flops 37748736 | bytes 393216 | tf_op jit(solution)/shard_map/first_parameters/pallas_call | solution.py:64
  18.6 2.3 %collective-permute-done.4.mine_ref = bf16[128,384]{1,0:T(8,128)(2,1)S(1)} collective-permute-done((bf16[128,384]{1,0:T(8,128)(2,1)S(1)}, bf16[128,384]{1,0:T(8,128)(2,1)S(1)}, u32[]{:S(2)}, u32[]{:S(2)}) %collective-permute-start.4) | collective-permute-done | bytes 98336 | tf_op jit(solution)/shard_map/ppermute | solution.py:35
  21.1 1.0 %collective-permute-done.5.other_ref = bf16[128,384]{1,0:T(8,128)(2,1)S(1)} collective-permute-done((bf16[128,384]{1,0:T(8,128)(2,1)S(1)}, bf16[128,384]{1,0:T(8,128)(2,1)S(1)}, u32[]{:S(2)}, u32[]{:S(2)}) %collective-permute-start.5) | collective-permute-done | bytes 98336 | tf_op jit(solution)/shard_map/ppermute | solution.py:35
  22.5 1.5 %collective-permute-start.8 = (bf16[16,768]{1,0:T(8,128)(2,1)S(1)}, bf16[16,768]{1,0:T(8,128)(2,1)S(1)}, u32[]{:S(2)}, u32[]{:S(2)}) collective-permute-start(bf16[16,768]{1,0:T(8,128)(2,1)S(1)} %get-tuple-element.66), channel_id=1, source_target_pairs={{0,12},{4,8},{8,4},{12,0},{1,13},{5,9},{9,5},{13,1},{2,14},{6,10},... | collective-permute-start | bytes 73736 | tf_op jit(solution)/shard_map/ppermute | solution.py:40
  24.0 0.6 %collective-permute-start.7 = (bf16[16,768]{1,0:T(8,128)(2,1)S(1)}, bf16[16,768]{1,0:T(8,128)(2,1)S(1)}, u32[]{:S(2)}, u32[]{:S(2)}) collective-permute-start(bf16[16,768]{1,0:T(8,128)(2,1)S(1)} %get-tuple-element.66), channel_id=1, source_target_pairs={{0,8},{4,12},{8,0},{12,4},{1,9},{5,13},{9,1},{13,5},{2,10},{6,14},... | collective-permute-start | bytes 73736 | tf_op jit(solution)/shard_map/ppermute | solution.py:40
  24.7 2.3 %collective-permute-start.6 = (bf16[16,768]{1,0:T(8,128)(2,1)S(1)}, bf16[16,768]{1,0:T(8,128)(2,1)S(1)}, u32[]{:S(2)}, u32[]{:S(2)}) collective-permute-start(bf16[16,768]{1,0:T(8,128)(2,1)S(1)} %get-tuple-element.66), channel_id=1, source_target_pairs={{0,4},{4,0},{8,12},{12,8},{1,5},{5,1},{9,13},{13,9},{2,6},{6,2},{1... | collective-permute-start | bytes 73736 | tf_op jit(solution)/shard_map/ppermute | solution.py:40
  27.0 0.8 %local.3 = (f32[128,768]{1,0:T(8,128)S(1)}, f32[128,32]{1,0:T(8,128)S(1)}, f32[1,768]{1,0:T(1,128)S(1)}) custom-call(bf16[128,768]{1,0:T(8,128)(2,1)S(1)} %get-tuple-element.42.up_ref, bf16[128,768]{1,0:T(8,128)(2,1)S(1)} %get-tuple-element.62.gmp_ref, bf16[128,32]{1,0:T(8,128)(2,1)S(1)} %get-tuple-element.45.coef_ref, ...), custom_call_target="tpu_custom_call" | custom-call | flops 150994944 | bytes 393216 | tf_op jit(solution)/shard_map/local/pallas_call | solution.py:64
  27.8 0.6 %collective-permute-done.8.refs_2_ = bf16[16,768]{1,0:T(8,128)(2,1)S(1)} collective-permute-done((bf16[16,768]{1,0:T(8,128)(2,1)S(1)}, bf16[16,768]{1,0:T(8,128)(2,1)S(1)}, u32[]{:S(2)}, u32[]{:S(2)}) %collective-permute-start.8) | collective-permute-done | bytes 24608 | tf_op jit(solution)/shard_map/ppermute | solution.py:40
  30.9 2.4 %collective-permute-start.13 = (bf16[40,384]{1,0:T(8,128)(2,1)S(1)}, bf16[40,384]{1,0:T(8,128)(2,1)S(1)}, u32[]{:S(2)}, u32[]{:S(2)}) collective-permute-start(bf16[40,384]{1,0:T(8,128)(2,1)S(1)} %pair.1.refs_0_), channel_id=1, source_target_pairs={{0,12},{4,8},{8,4},{12,0},{1,13},{5,9},{9,5},{13,1},{2,14},{6,10},... | collective-permute-start | bytes 92168 | tf_op jit(solution)/shard_map/ppermute | solution.py:40
  33.3 2.0 %collective-permute-start.11 = (bf16[40,384]{1,0:T(8,128)(2,1)S(1)}, bf16[40,384]{1,0:T(8,128)(2,1)S(1)}, u32[]{:S(2)}, u32[]{:S(2)}) collective-permute-start(bf16[40,384]{1,0:T(8,128)(2,1)S(1)} %pair.1.refs_0_), channel_id=1, source_target_pairs={{0,8},{4,12},{8,0},{12,4},{1,9},{5,13},{9,1},{13,5},{2,10},{6,14},... | collective-permute-start | bytes 92168 | tf_op jit(solution)/shard_map/ppermute | solution.py:40
  35.3 0.8 %output.1 = bf16[1,128,768]{2,1,0:T(8,128)(2,1)} custom-call(bf16[128,768]{1,0:T(8,128)(2,1)S(1)} %last_input.1.part_ref, bf16[128,768]{1,0:T(8,128)(2,1)S(1)} %collective-permute-done.10.part2_ref, bf16[128,384]{1,0:T(8,128)(2,1)S(1)} %collective-permute-done.4.mine_ref, bf16[128,384]{1,0:T(8,128)(2,1)S(1)} %collective-permute-done.5.other_ref), custom_call_target="tpu_custom_call" | custom-call | tf_op jit(solution)/shard_map/output/pallas_call | solution.py:64
  36.1 0.8 %collective-permute-done.13.refs_3_ = bf16[40,384]{1,0:T(8,128)(2,1)S(1)} collective-permute-done((bf16[40,384]{1,0:T(8,128)(2,1)S(1)}, bf16[40,384]{1,0:T(8,128)(2,1)S(1)}, u32[]{:S(2)}, u32[]{:S(2)}) %collective-permute-start.13) | collective-permute-done | bytes 30752 | tf_op jit(solution)/shard_map/ppermute | solution.py:40
  36.9 0.6 %collective-permute-done.12.refs_2_ = bf16[40,384]{1,0:T(8,128)(2,1)S(1)} collective-permute-done((bf16[40,384]{1,0:T(8,128)(2,1)S(1)}, bf16[40,384]{1,0:T(8,128)(2,1)S(1)}, u32[]{:S(2)}, u32[]{:S(2)}) %collective-permute-start.12) | collective-permute-done | bytes 30752 | tf_op jit(solution)/shard_map/ppermute | solution.py:40
  38.2 0.6 %heads.1 = f32[1,12]{1,0:T(1,128)} custom-call(f32[8,384]{1,0:T(8,128)S(1)} %get-tuple-element.80.row_ref), custom_call_target="tpu_custom_call" | custom-call | tf_op jit(solution)/shard_map/heads/pallas_call | solution.py:64
  38.8 0.6 %collective-permute-done.14.other_ref = f32[32,384]{1,0:T(8,128)S(1)} collective-permute-done((f32[32,384]{1,0:T(8,128)S(1)}, f32[32,384]{1,0:T(8,128)S(1)}, u32[]{:S(2)}, u32[]{:S(2)}) %collective-permute-start.14) | collective-permute-done | bytes 49184 | tf_op jit(solution)/shard_map/ppermute | solution.py:35
  39.4 0.7 %join.1 = f32[1,32,768]{2,1,0:T(8,128)} custom-call(f32[32,384]{1,0:T(8,128)S(1)} %get-tuple-element.79.mine_ref, f32[32,384]{1,0:T(8,128)S(1)} %collective-permute-done.14.other_ref), custom_call_target="tpu_custom_call" | custom-call | tf_op jit(solution)/shard_map/join/pallas_call | solution.py:64
  (34 shorter events, 4.5 us)
Async XLA Ops:
  0.6 8.8 %copy-start.1 = (bf16[1,768,768]{2,1,0:T(8,128)(2,1)S(1)}, bf16[1,768,768]{2,1,0:T(8,128)(2,1)}, u32[]{:S(2)}) copy-start(bf16[1,768,768]{2,1,0:T(8,128)(2,1)} %w_ref.2) | copy-start | bytes 3538948
  3.7 7.0 %collective-permute-start = (bf16[16,896]{1,0:T(8,128)(2,1)S(1)}, bf16[16,896]{1,0:T(8,128)(2,1)S(1)}, u32[]{:S(2)}, u32[]{:S(2)}) collective-permute-start(bf16[16,896]{1,0:T(8,128)(2,1)S(1)} %get-tuple-element.49), channel_id=1, source_target_pairs={{0,12},{4,8},{8,4},{12,0},{1,13},{5,9},{9,5},{13,1},{2,14},{6,10},... | collective-permute-start | bytes 86024 | tf_op jit(solution)/shard_map/ppermute | solution.py:40
  8.8 4.8 %collective-permute-start.1 = (bf16[16,896]{1,0:T(8,128)(2,1)S(1)}, bf16[16,896]{1,0:T(8,128)(2,1)S(1)}, u32[]{:S(2)}, u32[]{:S(2)}) collective-permute-start(bf16[16,896]{1,0:T(8,128)(2,1)S(1)} %get-tuple-element.50), channel_id=1, source_target_pairs={{0,8},{4,12},{8,0},{12,4},{1,9},{5,13},{9,1},{13,5},{2,10},{6,14},... | collective-permute-start | bytes 86024 | tf_op jit(solution)/shard_map/ppermute | solution.py:40
  8.8 4.8 %collective-permute-start.2 = (bf16[16,896]{1,0:T(8,128)(2,1)S(1)}, bf16[16,896]{1,0:T(8,128)(2,1)S(1)}, u32[]{:S(2)}, u32[]{:S(2)}) collective-permute-start(bf16[16,896]{1,0:T(8,128)(2,1)S(1)} %get-tuple-element.51), channel_id=1, source_target_pairs={{0,4},{4,0},{8,12},{12,8},{1,5},{5,1},{9,13},{13,9},{2,6},{6,2},{1... | collective-permute-start | bytes 86024 | tf_op jit(solution)/shard_map/ppermute | solution.py:40
  9.5 4.1 %copy-start.3 = (bf16[128,768]{1,0:T(8,128)(2,1)S(1)}, bf16[128,768]{1,0:T(8,128)(2,1)}, u32[]{:S(2)}) copy-start(bf16[128,768]{1,0:T(8,128)(2,1)} %g_ref.1) | copy-start | bytes 589828
  9.5 4.1 %copy-start.4 = (bf16[1,768,32]{1,2,0:T(8,128)(2,1)S(1)}, bf16[1,768,32]{1,2,0:T(8,128)(2,1)}, u32[]{:S(2)}) copy-start(bf16[1,768,32]{1,2,0:T(8,128)(2,1)} %param.10) | copy-start | bytes 147460
  13.6 3.9 %copy-start.2 = (bf16[1,128,768]{2,1,0:T(8,128)(2,1)S(1)}, bf16[1,128,768]{2,1,0:T(8,128)(2,1)}, u32[]{:S(2)}) copy-start(bf16[1,128,768]{2,1,0:T(8,128)(2,1)} %x_ref.3) | copy-start | bytes 589828
  14.5 3.7 %copy-start = (bf16[1,768,768]{2,1,0:T(8,128)(2,1)S(1)}, bf16[1,768,768]{2,1,0:T(8,128)(2,1)}, u32[]{:S(2)}) copy-start(bf16[1,768,768]{2,1,0:T(8,128)(2,1)} %w_ref.3) | copy-start | bytes 3538948
  14.5 1.4 %collective-permute-start.3 = (bf16[128,384]{1,0:T(8,128)(2,1)S(1)}, bf16[128,384]{1,0:T(8,128)(2,1)S(1)}, u32[]{:S(2)}, u32[]{:S(2)}) collective-permute-start(bf16[128,384]{1,0:T(8,128)(2,1)S(1)} %get-tuple-element.53), channel_id=1, source_target_pairs={{0,1},{1,0},{2,3},{3,2},{4,5},{5,4},{6,7},{7,6},{8,9},{9,8},{10,11... | collective-permute-start | bytes 294920 | tf_op jit(solution)/shard_map/ppermute | solution.py:35
  15.9 4.9 %collective-permute-start.4 = (bf16[128,384]{1,0:T(8,128)(2,1)S(1)}, bf16[128,384]{1,0:T(8,128)(2,1)S(1)}, u32[]{:S(2)}, u32[]{:S(2)}) collective-permute-start(bf16[128,384]{1,0:T(8,128)(2,1)S(1)} %add_convert_fusion.kept_ref), channel_id=1, source_target_pairs={{0,2},{2,0},{1,3},{3,1},{4,6},{6,4},{5,7},{7,5},{8,10},{10,8},{9,1... | collective-permute-start | bytes 294920 | tf_op jit(solution)/shard_map/ppermute | solution.py:35
  20.8 1.3 %collective-permute-start.5 = (bf16[128,384]{1,0:T(8,128)(2,1)S(1)}, bf16[128,384]{1,0:T(8,128)(2,1)S(1)}, u32[]{:S(2)}, u32[]{:S(2)}) collective-permute-start(bf16[128,384]{1,0:T(8,128)(2,1)S(1)} %collective-permute-done.4.mine_ref), channel_id=1, source_target_pairs={{0,1},{1,0},{2,3},{3,2},{4,5},{5,4},{6,7},{7,6},{8,9},{9,8},{10,11... | collective-permute-start | bytes 294920 | tf_op jit(solution)/shard_map/ppermute | solution.py:35
  22.5 5.9 %collective-permute-start.8 = (bf16[16,768]{1,0:T(8,128)(2,1)S(1)}, bf16[16,768]{1,0:T(8,128)(2,1)S(1)}, u32[]{:S(2)}, u32[]{:S(2)}) collective-permute-start(bf16[16,768]{1,0:T(8,128)(2,1)S(1)} %get-tuple-element.66), channel_id=1, source_target_pairs={{0,12},{4,8},{8,4},{12,0},{1,13},{5,9},{9,5},{13,1},{2,14},{6,10},... | collective-permute-start | bytes 73736 | tf_op jit(solution)/shard_map/ppermute | solution.py:40
  24.0 4.7 %collective-permute-start.7 = (bf16[16,768]{1,0:T(8,128)(2,1)S(1)}, bf16[16,768]{1,0:T(8,128)(2,1)S(1)}, u32[]{:S(2)}, u32[]{:S(2)}) collective-permute-start(bf16[16,768]{1,0:T(8,128)(2,1)S(1)} %get-tuple-element.66), channel_id=1, source_target_pairs={{0,8},{4,12},{8,0},{12,4},{1,9},{5,13},{9,1},{13,5},{2,10},{6,14},... | collective-permute-start | bytes 73736 | tf_op jit(solution)/shard_map/ppermute | solution.py:40
  24.7 4.3 %collective-permute-start.6 = (bf16[16,768]{1,0:T(8,128)(2,1)S(1)}, bf16[16,768]{1,0:T(8,128)(2,1)S(1)}, u32[]{:S(2)}, u32[]{:S(2)}) collective-permute-start(bf16[16,768]{1,0:T(8,128)(2,1)S(1)} %get-tuple-element.66), channel_id=1, source_target_pairs={{0,4},{4,0},{8,12},{12,8},{1,5},{5,1},{9,13},{13,9},{2,6},{6,2},{1... | collective-permute-start | bytes 73736 | tf_op jit(solution)/shard_map/ppermute | solution.py:40
  29.4 1.3 %collective-permute-start.9 = (bf16[32,384]{1,0:T(8,128)(2,1)S(1)}, bf16[32,384]{1,0:T(8,128)(2,1)S(1)}, u32[]{:S(2)}, u32[]{:S(2)}) collective-permute-start(bf16[32,384]{1,0:T(8,128)(2,1)S(1)} %get-tuple-element.71), channel_id=1, source_target_pairs={{0,1},{1,0},{2,3},{3,2},{4,5},{5,4},{6,7},{7,6},{8,9},{9,8},{10,11... | collective-permute-start | bytes 73736 | tf_op jit(solution)/shard_map/ppermute | solution.py:35
  30.7 4.6 %collective-permute-start.10 = (bf16[128,768]{1,0:T(8,128)(2,1)S(1)}, bf16[128,768]{1,0:T(8,128)(2,1)S(1)}, u32[]{:S(2)}, u32[]{:S(2)}) collective-permute-start(bf16[128,768]{1,0:T(8,128)(2,1)S(1)} %last_input.1.part_ref), channel_id=1, source_target_pairs={{0,1},{1,0},{2,3},{3,2},{4,5},{5,4},{6,7},{7,6},{8,9},{9,8},{10,11... | collective-permute-start | bytes 589832 | tf_op jit(solution)/shard_map/ppermute | solution.py:35
  30.9 6.0 %collective-permute-start.13 = (bf16[40,384]{1,0:T(8,128)(2,1)S(1)}, bf16[40,384]{1,0:T(8,128)(2,1)S(1)}, u32[]{:S(2)}, u32[]{:S(2)}) collective-permute-start(bf16[40,384]{1,0:T(8,128)(2,1)S(1)} %pair.1.refs_0_), channel_id=1, source_target_pairs={{0,12},{4,8},{8,4},{12,0},{1,13},{5,9},{9,5},{13,1},{2,14},{6,10},... | collective-permute-start | bytes 92168 | tf_op jit(solution)/shard_map/ppermute | solution.py:40
  33.3 4.3 %collective-permute-start.12 = (bf16[40,384]{1,0:T(8,128)(2,1)S(1)}, bf16[40,384]{1,0:T(8,128)(2,1)S(1)}, u32[]{:S(2)}, u32[]{:S(2)}) collective-permute-start(bf16[40,384]{1,0:T(8,128)(2,1)S(1)} %pair.1.refs_0_), channel_id=1, source_target_pairs={{0,4},{4,0},{8,12},{12,8},{1,5},{5,1},{9,13},{13,9},{2,6},{6,2},{1... | collective-permute-start | bytes 92168 | tf_op jit(solution)/shard_map/ppermute | solution.py:40
  33.3 4.8 %collective-permute-start.11 = (bf16[40,384]{1,0:T(8,128)(2,1)S(1)}, bf16[40,384]{1,0:T(8,128)(2,1)S(1)}, u32[]{:S(2)}, u32[]{:S(2)}) collective-permute-start(bf16[40,384]{1,0:T(8,128)(2,1)S(1)} %pair.1.refs_0_), channel_id=1, source_target_pairs={{0,8},{4,12},{8,0},{12,4},{1,9},{5,13},{9,1},{13,5},{2,10},{6,14},... | collective-permute-start | bytes 92168 | tf_op jit(solution)/shard_map/ppermute | solution.py:40
  38.1 1.3 %collective-permute-start.14 = (f32[32,384]{1,0:T(8,128)S(1)}, f32[32,384]{1,0:T(8,128)S(1)}, u32[]{:S(2)}, u32[]{:S(2)}) collective-permute-start(f32[32,384]{1,0:T(8,128)S(1)} %get-tuple-element.79.mine_ref), channel_id=1, source_target_pairs={{0,1},{1,0},{2,3},{3,2},{4,5},{5,4},{6,7},{7,6},{8,9},{9,8},{10,11... | collective-permute-start | bytes 147464 | tf_op jit(solution)/shard_map/ppermute | solution.py:35
